TPU v7x, 512 devices: a whole 4x8x8 slice. The times are simulated.
512 devices in a mesh: row: 8 (over y), chan: 16 (over z, core), dp: 4 (over x).
Axes of the slice: x: 4, y: 8, z: 8, core: 2. Of those that a mesh axis runs over, the one named last changes fastest.
Arguments:
- features_in: bfloat16 [4, 144, 64, 2048], P('dp', 'row', None, 'chan'), may hold values from -6 to 6
- depth_weights: bfloat16 [3, 3, 3, 2048], P(None, None, None, 'chan'), may hold values from -2 to 2
- point_weights: bfloat16 [4, 2048, 256], P(None, 'chan'), may hold values from -0.125 to 0.125
- proj_weights: bfloat16 [4, 256, 256], replicated, may hold values from -0.1875 to 0.1875
- cotangent: bfloat16 [4, 144, 64, 256], P('dp', 'row', 'chan'), may hold values from -18 to 18
Outputs:
- output: bfloat16 [4, 144, 64, 256], P('dp', 'row', 'chan')
- grad_input: bfloat16 [4, 144, 64, 2048], P('dp', 'row', None, 'chan')
- grad_depth: float32 [3, 3, 3, 2048], P(None, None, None, 'chan')
- grad_point: float32 [4, 2048, 256], P(None, 'chan')
- grad_proj: float32 [4, 256, 256], replicated
All inputs are finite; a program needn't handle non-finite values.
Results may differ from a plain program's by a relative error of at most 0.0059.
Values may be sent and summed in bfloat16 or wider, within the bound.
A program may use at most 64 MiB of HBM per device.

v0:
```python
import math

import jax
import jax.numpy as jnp
from jax import lax
from jax.sharding import PartitionSpec as P

BASE_DILATION = 12


def shifted(value, axis, steps):
    count = lax.axis_size(axis)
    first, last = (max(0, -steps), min(count, count - steps))
    return lax.ppermute(value, axis, [(source, source + steps) for source in range(first, last)])


def window(source, top, left, band_rows, band_cols):
    upper = lax.slice_in_dim(source, top, top + band_rows, axis=1)
    return lax.slice_in_dim(upper, left, left + band_cols, axis=2)


def on_device(features_in, depth_weights, point_weights, proj_weights, cotangent):
    samples, band_rows, band_cols, channels = features_in.shape
    weight_scale = 1.0 / math.sqrt(
        samples * lax.axis_size("dp") * band_rows * lax.axis_size("row") * band_cols
    )
    largest_reach = 3 * BASE_DILATION
    offsets = (2, 1, -1, -2)
    arrivals = []
    for offset in offsets:
        arrivals.append(shifted(features_in, "row", offset))
    tall_rows = jnp.concatenate(
        [arrivals[0], arrivals[1], features_in, arrivals[2], arrivals[3]], axis=1
    )
    padded = jnp.pad(tall_rows, ((0, 0), (0, 0), (largest_reach, largest_reach), (0, 0)))
    branch_maps = [features_in]
    for branch_level in range(3):
        tap_spacing = (branch_level + 1) * BASE_DILATION
        summed = jnp.zeros(features_in.shape, jnp.float32)
        for row_tap in range(3):
            for col_tap in range(3):
                input_kernel_tap = window(
                    padded,
                    largest_reach + (row_tap - 1) * tap_spacing,
                    largest_reach + (col_tap - 1) * tap_spacing,
                    band_rows,
                    band_cols,
                )
                summed = summed + input_kernel_tap.astype(jnp.float32) * depth_weights[
                    branch_level, row_tap, col_tap
                ].astype(jnp.float32)
        branch_maps.append(summed.astype(jnp.bfloat16))
    spread = jnp.stack(branch_maps)
    full_point = lax.all_gather(point_weights, "chan", axis=1, tiled=True)
    preact = jnp.einsum(
        "bsrwc,bcf->bsrwf",
        lax.all_to_all(spread, "chan", split_axis=3, concat_axis=4, tiled=True),
        full_point,
        preferred_element_type=jnp.float32,
    )
    activation = jax.nn.silu(preact).astype(jnp.bfloat16)
    output = jnp.einsum(
        "bsrwf,bfg->srwg", activation, proj_weights, preferred_element_type=jnp.float32
    ).astype(jnp.bfloat16)
    silu_gradient = jnp.einsum(
        "srwg,bfg->bsrwf", cotangent, proj_weights, preferred_element_type=jnp.float32
    )
    logistic = jax.nn.sigmoid(preact)
    pre_grad = (silu_gradient * logistic * (1.0 + preact * (1.0 - logistic))).astype(jnp.bfloat16)
    proj_term = jnp.einsum(
        "bsrwf,srwg->bfg", activation, cotangent, preferred_element_type=jnp.float32
    )
    grad_proj = lax.psum(proj_term, ("row", "chan", "dp")) * weight_scale
    incoming = lax.all_gather(pre_grad, "chan", axis=3, tiled=True)
    local_grad = jnp.einsum(
        "bsrwf,bcf->bsrwc", incoming, point_weights, preferred_element_type=jnp.float32
    ).astype(jnp.bfloat16)
    spread_grad = local_grad
    point_sum = jnp.einsum("bsrwc,bsrwf->bcf", spread, incoming, preferred_element_type=jnp.float32)
    spread_grad, point_term = (spread_grad, point_sum)
    depth_rows = []
    for branch_level in range(3):
        tap_spacing = (branch_level + 1) * BASE_DILATION
        branch_grad = spread_grad[branch_level + 1].astype(jnp.float32)
        gathered = []
        for row_tap in range(3):
            for col_tap in range(3):
                input_kernel_tap = window(
                    padded,
                    largest_reach + (row_tap - 1) * tap_spacing,
                    largest_reach + (col_tap - 1) * tap_spacing,
                    band_rows,
                    band_cols,
                )
                gathered.append(
                    jnp.sum(input_kernel_tap.astype(jnp.float32) * branch_grad, axis=(0, 1, 2))
                )
        depth_rows.append(jnp.stack(gathered).reshape(3, 3, channels))
    depth_term = jnp.stack(depth_rows)
    point_summed, depth_summed = lax.psum((point_term, depth_term), ("row", "dp"))
    grad_point = point_summed * weight_scale
    grad_depth = depth_summed * weight_scale
    neighbour_sets = []
    for branch_level in range(3):
        neighbour_sets.append(
            [shifted(spread_grad[branch_level + 1], "row", offset) for offset in offsets]
        )
    grad_in = spread_grad[0].astype(jnp.float32)
    for branch_level in range(3):
        tap_spacing = (branch_level + 1) * BASE_DILATION
        received = neighbour_sets[branch_level]
        grad_tall = jnp.concatenate(
            [received[0], received[1], spread_grad[branch_level + 1], received[2], received[3]],
            axis=1,
        )
        grad_padded = jnp.pad(grad_tall, ((0, 0), (0, 0), (largest_reach, largest_reach), (0, 0)))
        for row_tap in range(3):
            for col_tap in range(3):
                grad_tap = window(
                    grad_padded,
                    largest_reach - (row_tap - 1) * tap_spacing,
                    largest_reach - (col_tap - 1) * tap_spacing,
                    band_rows,
                    band_cols,
                )
                grad_in = grad_in + grad_tap.astype(jnp.float32) * depth_weights[
                    branch_level, row_tap, col_tap
                ].astype(jnp.float32)
    return (output, grad_in.astype(jnp.bfloat16), grad_depth, grad_point, grad_proj)


def solution(mesh):
    in_specs = (
        P("dp", "row", None, "chan"),
        P(None, None, None, "chan"),
        P(None, "chan", None),
        P(),
        P("dp", "row", "chan", None),
    )
    out_specs = (
        P("dp", "row", "chan", None),
        P("dp", "row", None, "chan"),
        P(None, None, None, "chan"),
        P(None, "chan", None),
        P(),
    )
    return jax.shard_map(
        on_device, mesh=mesh, in_specs=in_specs, out_specs=out_specs, check_vma=False
    )
```

profile of v0, /device:TPU:8, one launch (start us, length us, event | category | flops | bytes accessed | tf_op | source)
XLA Modules:
  0.0 665.3 jit_solution(2446986506534483894)
XLA Ops:
  8.0 4.5 collective-permute-start
  12.5 4.7 collective-permute-start.1
  17.2 1.9 collective-permute-start.2
  22.2 3.2 collective-permute-done
  25.4 6.2 collective-permute-done.1
  31.7 3.8 collective-permute-done.2
  39.6 43.2 %all_to_all.15 = bf16[4,1,18,64,128]{4,0,2,1,3:T(4,128)(2,1)S(1)} all-to-all(bf16[4,1,18,64,128]{4,0,2,1,3:T(4,128)(2,1)S(1)} %copy.33), channel_id=1, replica_groups=mesh['row'=8,'chan'=16,'dp'=4] {'chan'}, dimensions={3} | all-to-all | bytes 2359296 | tf_op jit(solution)/shard_map/all_to_all | solution.py:57
  84.3 2.5 reshape.148
  86.9 3.4 fusion
  92.5 2.0 fusion.16
  95.5 269.8 %all-reduce.9.cloned.1.call-done = f32[4,256,256]{2,1,0:T(8,128)} async-done(((f32[4,256,256]{2,1,0:T(8,128)}), f32[4,256,256]{2,1,0:T(8,128)}) %all-reduce.9.cloned.1.call-update) | async-done | bytes 1048592 | tf_op jit(solution)/shard_map/psum | solution.py:73
  365.3 2.3 broadcast_multiply_fusion
  367.6 40.3 %all-gather.5.cloned.1.call-done = bf16[4,1,18,64,256]{4,2,3,0,1:T(8,128)(2,1)} async-done(((bf16[4,1,18,4,256]{4,2,3,0,1:T(8,128)(2,1)}), bf16[4,1,18,64,256]{4,2,3,0,1:T(8,128)(2,1)}) %all-gather.5.cloned.1.call-update) | async-done | bytes 2359312 | tf_op jit(solution)/shard_map/all_gather | solution.py:74
  407.9 3.5 fusion.10
  411.4 2.7 fusion.7
  414.1 1.6 fusion.77
  417.7 5.0 collective-permute-start.8
  422.7 3.9 collective-permute-start.9
  426.6 3.2 collective-permute-start.4
  429.8 2.1 collective-permute-start.5
  437.4 1.8 collective-permute-start.12
  439.2 154.8 %psum.21 = f32[3,3,3,128]{3,2,1,0:T(4,128)S(1)} all-reduce(f32[3,3,3,128]{3,2,1,0:T(4,128)S(1)} %pad_maximum_fusion.9), channel_id=1, replica_groups=mesh['row'=8,'chan'=16,'dp'=4] {'row','dp'}, use_global_device_ids=true, to_apply=%region_27.28 | all-reduce | flops 3456 | bytes 27648 | tf_op jit(solution)/shard_map/psum | solution.py:100
  594.7 7.7 %collective-permute-start.13 = (bf16[1,18,64,128]{3,2,1,0:T(8,128)(2,1)}, bf16[1,18,64,128]{3,2,1,0:T(8,128)(2,1)S(1)}, u32[]{:S(2)}, u32[]{:S(2)}) collective-permute-start(bf16[1,18,64,128]{3,2,1,0:T(8,128)(2,1)} %get-tuple-element.56), channel_id=1, source_target_pairs={{0,64},{64,128},{128,192},{192,256},{256,320},{320,384},{384,448},... | collective-permute-start | bytes 884744 | tf_op jit(solution)/shard_map/ppermute | solution.py:14
  603.4 2.1 collective-permute-start.14
  607.8 1.9 collective-permute-start.10
  613.0 1.9 collective-permute-start.6
  615.1 4.8 collective-permute-done.14
  621.4 12.1 %collective-permute-done.15 = bf16[1,18,64,128]{3,2,1,0:T(8,128)(2,1)S(1)} collective-permute-done((bf16[1,18,64,128]{3,2,1,0:T(8,128)(2,1)S(1)}, bf16[1,18,64,128]{3,2,1,0:T(8,128)(2,1)S(1)}, u32[]{:S(2)}, u32[]{:S(2)}) %collective-permute-start.15) | collective-permute-done | bytes 294944 | tf_op jit(solution)/shard_map/ppermute | solution.py:14
  633.6 9.3 %collective-permute-done.11 = bf16[1,18,64,128]{3,2,1,0:T(8,128)(2,1)S(1)} collective-permute-done((bf16[1,18,64,128]{3,2,1,0:T(8,128)(2,1)}, bf16[1,18,64,128]{3,2,1,0:T(8,128)(2,1)S(1)}, u32[]{:S(2)}, u32[]{:S(2)}) %collective-permute-start.11) | collective-permute-done | bytes 294944 | tf_op jit(solution)/shard_map/ppermute | solution.py:14
  643.0 9.4 %collective-permute-done.7 = bf16[1,18,64,128]{3,2,1,0:T(8,128)(2,1)S(1)} collective-permute-done((bf16[1,18,64,128]{3,2,1,0:T(8,128)(2,1)S(1)}, bf16[1,18,64,128]{3,2,1,0:T(8,128)(2,1)S(1)}, u32[]{:S(2)}, u32[]{:S(2)}) %collective-permute-start.7) | collective-permute-done | bytes 294944 | tf_op jit(solution)/shard_map/ppermute | solution.py:14
  652.5 4.4 fusion.96
  656.8 1.9 broadcast_multiply_fusion.1
  (133 shorter events, 28.9 us)
Async XLA Ops:
  7.2 85.3 %copy-start = (bf16[4,256,256]{2,1,0:T(8,128)(2,1)S(1)}, bf16[4,256,256]{2,1,0:T(8,128)(2,1)}, u32[]{:S(2)}) copy-start(bf16[4,256,256]{2,1,0:T(8,128)(2,1)} %param.8) | copy-start | bytes 1572868
  7.2 79.7 %all-gather.3.cloned.1.call-start = ((), (), s32[]{:S(2)}) async-start(), calls=%async_computation.1 | async-start | bytes 4456448 | tf_op jit(solution)/shard_map/all_gather | solution.py:54
  7.9 357.3 %all-reduce.9.cloned.1.call-start = ((), (), s32[]{:S(2)}) async-start(), calls=%async_computation.4 | async-start | bytes 2097152 | tf_op jit(solution)/shard_map/psum | solution.py:73
  8.0 17.4 %collective-permute-start = (bf16[1,18,64,128]{3,2,1,0:T(8,128)(2,1)}, bf16[1,18,64,128]{3,2,1,0:T(8,128)(2,1)S(1)}, u32[]{:S(2)}, u32[]{:S(2)}) collective-permute-start(bf16[1,18,64,128]{3,2,1,0:T(8,128)(2,1)} %param.5), channel_id=1, source_target_pairs={{0,128},{64,192},{128,256},{192,320},{256,384},{320,448},{1,129},{... | collective-permute-start | bytes 884744 | tf_op jit(solution)/shard_map/ppermute | solution.py:14
  12.5 19.1 %collective-permute-start.1 = (bf16[1,18,64,128]{3,2,1,0:T(8,128)(2,1)}, bf16[1,18,64,128]{3,2,1,0:T(8,128)(2,1)S(1)}, u32[]{:S(2)}, u32[]{:S(2)}) collective-permute-start(bf16[1,18,64,128]{3,2,1,0:T(8,128)(2,1)} %param.5), channel_id=1, source_target_pairs={{0,64},{64,128},{128,192},{192,256},{256,320},{320,384},{384,448},... | collective-permute-start | bytes 884744 | tf_op jit(solution)/shard_map/ppermute | solution.py:14
  17.2 18.3 %collective-permute-start.2 = (bf16[1,18,64,128]{3,2,1,0:T(8,128)(2,1)}, bf16[1,18,64,128]{3,2,1,0:T(8,128)(2,1)S(1)}, u32[]{:S(2)}, u32[]{:S(2)}) collective-permute-start(bf16[1,18,64,128]{3,2,1,0:T(8,128)(2,1)} %param.5), channel_id=1, source_target_pairs={{64,0},{128,64},{192,128},{256,192},{320,256},{384,320},{448,384},... | collective-permute-start | bytes 884744 | tf_op jit(solution)/shard_map/ppermute | solution.py:14
  19.1 16.4 %collective-permute-start.3 = (bf16[1,18,64,128]{3,2,1,0:T(8,128)(2,1)}, bf16[1,18,64,128]{3,2,1,0:T(8,128)(2,1)S(1)}, u32[]{:S(2)}, u32[]{:S(2)}) collective-permute-start(bf16[1,18,64,128]{3,2,1,0:T(8,128)(2,1)} %param.5), channel_id=1, source_target_pairs={{128,0},{192,64},{256,128},{320,192},{384,256},{448,320},{129,1},{... | collective-permute-start | bytes 884744 | tf_op jit(solution)/shard_map/ppermute | solution.py:14
  92.4 315.4 %all-gather.5.cloned.1.call-start = ((), (), s32[]{:S(2)}) async-start(), calls=%async_computation.2 | async-start | bytes 3342336 | tf_op jit(solution)/shard_map/all_gather | solution.py:74
  94.5 562.3 %all-reduce.7.cloned.1.call-start = ((), (), s32[]{:S(2)}) async-start(), calls=%async_computation.3 | async-start | bytes 1048576 | tf_op jit(solution)/shard_map/psum | solution.py:100
  94.9 313.0 %copy-start.11 = (bf16[1,1,18,64,128]{4,3,2,1,0:T(8,128)(2,1)S(1)}, bf16[1,1,18,64,128]{4,3,2,1,0:T(8,128)(2,1)}, u32[]{:S(2)}) copy-start(bf16[1,1,18,64,128]{4,3,2,1,0:T(8,128)(2,1)} %copy-done.10) | copy-start | bytes 884740
  94.9 313.0 %copy-start.13 = (bf16[1,1,18,64,128]{4,3,2,1,0:T(8,128)(2,1)S(1)}, bf16[1,1,18,64,128]{4,3,2,1,0:T(8,128)(2,1)}, u32[]{:S(2)}) copy-start(bf16[1,1,18,64,128]{4,3,2,1,0:T(8,128)(2,1)} %copy-done.12) | copy-start | bytes 884740
  94.9 313.0 %copy-start.15 = (bf16[1,1,18,64,128]{4,3,2,1,0:T(8,128)(2,1)S(1)}, bf16[1,1,18,64,128]{4,3,2,1,0:T(8,128)(2,1)}, u32[]{:S(2)}) copy-start(bf16[1,1,18,64,128]{4,3,2,1,0:T(8,128)(2,1)} %copy-done.14) | copy-start | bytes 884740
  417.7 177.0 %collective-permute-start.8 = (bf16[1,18,64,128]{3,2,1,0:T(8,128)(2,1)}, bf16[1,18,64,128]{3,2,1,0:T(8,128)(2,1)}, u32[]{:S(2)}, u32[]{:S(2)}) collective-permute-start(bf16[1,18,64,128]{3,2,1,0:T(8,128)(2,1)} %get-tuple-element.55), channel_id=1, source_target_pairs={{0,128},{64,192},{128,256},{192,320},{256,384},{320,448},{1,129},{... | collective-permute-start | bytes 884744 | tf_op jit(solution)/shard_map/ppermute | solution.py:14
  422.7 185.1 %collective-permute-start.9 = (bf16[1,18,64,128]{3,2,1,0:T(8,128)(2,1)}, bf16[1,18,64,128]{3,2,1,0:T(8,128)(2,1)}, u32[]{:S(2)}, u32[]{:S(2)}) collective-permute-start(bf16[1,18,64,128]{3,2,1,0:T(8,128)(2,1)} %get-tuple-element.55), channel_id=1, source_target_pairs={{0,64},{64,128},{128,192},{192,256},{256,320},{320,384},{384,448},... | collective-permute-start | bytes 884744 | tf_op jit(solution)/shard_map/ppermute | solution.py:14
  426.6 176.8 %collective-permute-start.4 = (bf16[1,18,64,128]{3,2,1,0:T(8,128)(2,1)S(1)}, bf16[1,18,64,128]{3,2,1,0:T(8,128)(2,1)}, u32[]{:S(2)}, u32[]{:S(2)}) collective-permute-start(bf16[1,18,64,128]{3,2,1,0:T(8,128)(2,1)S(1)} %get-tuple-element.57), channel_id=1, source_target_pairs={{0,128},{64,192},{128,256},{192,320},{256,384},{320,448},{1,129},{... | collective-permute-start | bytes 884744 | tf_op jit(solution)/shard_map/ppermute | solution.py:14
  429.8 180.9 %collective-permute-start.5 = (bf16[1,18,64,128]{3,2,1,0:T(8,128)(2,1)S(1)}, bf16[1,18,64,128]{3,2,1,0:T(8,128)(2,1)}, u32[]{:S(2)}, u32[]{:S(2)}) collective-permute-start(bf16[1,18,64,128]{3,2,1,0:T(8,128)(2,1)S(1)} %get-tuple-element.57), channel_id=1, source_target_pairs={{0,64},{64,128},{128,192},{192,256},{256,320},{320,384},{384,448},... | collective-permute-start | bytes 884744 | tf_op jit(solution)/shard_map/ppermute | solution.py:14
  433.2 173.2 %copy-start.18 = (bf16[1,18,64,128]{3,2,1,0:T(8,128)(2,1)S(1)}, bf16[1,18,64,128]{3,2,1,0:T(8,128)(2,1)}, u32[]{:S(2)}) copy-start(bf16[1,18,64,128]{3,2,1,0:T(8,128)(2,1)} %get-tuple-element.56) | copy-start | bytes 884740
  437.4 169.0 %collective-permute-start.12 = (bf16[1,18,64,128]{3,2,1,0:T(8,128)(2,1)}, bf16[1,18,64,128]{3,2,1,0:T(8,128)(2,1)S(1)}, u32[]{:S(2)}, u32[]{:S(2)}) collective-permute-start(bf16[1,18,64,128]{3,2,1,0:T(8,128)(2,1)} %get-tuple-element.56), channel_id=1, source_target_pairs={{0,128},{64,192},{128,256},{192,320},{256,384},{320,448},{1,129},{... | collective-permute-start | bytes 884744 | tf_op jit(solution)/shard_map/ppermute | solution.py:14
  594.7 18.4 %collective-permute-start.13 = (bf16[1,18,64,128]{3,2,1,0:T(8,128)(2,1)}, bf16[1,18,64,128]{3,2,1,0:T(8,128)(2,1)S(1)}, u32[]{:S(2)}, u32[]{:S(2)}) collective-permute-start(bf16[1,18,64,128]{3,2,1,0:T(8,128)(2,1)} %get-tuple-element.56), channel_id=1, source_target_pairs={{0,64},{64,128},{128,192},{192,256},{256,320},{320,384},{384,448},... | collective-permute-start | bytes 884744 | tf_op jit(solution)/shard_map/ppermute | solution.py:14
  603.4 16.6 %collective-permute-start.14 = (bf16[1,18,64,128]{3,2,1,0:T(8,128)(2,1)}, bf16[1,18,64,128]{3,2,1,0:T(8,128)(2,1)S(1)}, u32[]{:S(2)}, u32[]{:S(2)}) collective-permute-start(bf16[1,18,64,128]{3,2,1,0:T(8,128)(2,1)} %get-tuple-element.56), channel_id=1, source_target_pairs={{64,0},{128,64},{192,128},{256,192},{320,256},{384,320},{448,384},... | collective-permute-start | bytes 884744 | tf_op jit(solution)/shard_map/ppermute | solution.py:14
  606.4 27.0 %collective-permute-start.15 = (bf16[1,18,64,128]{3,2,1,0:T(8,128)(2,1)S(1)}, bf16[1,18,64,128]{3,2,1,0:T(8,128)(2,1)S(1)}, u32[]{:S(2)}, u32[]{:S(2)}) collective-permute-start(bf16[1,18,64,128]{3,2,1,0:T(8,128)(2,1)S(1)} %copy-done.18), channel_id=1, source_target_pairs={{128,0},{192,64},{256,128},{320,192},{384,256},{448,320},{129,1},{... | collective-permute-start | bytes 884744 | tf_op jit(solution)/shard_map/ppermute | solution.py:14
  607.8 25.7 %collective-permute-start.10 = (bf16[1,18,64,128]{3,2,1,0:T(8,128)(2,1)}, bf16[1,18,64,128]{3,2,1,0:T(8,128)(2,1)S(1)}, u32[]{:S(2)}, u32[]{:S(2)}) collective-permute-start(bf16[1,18,64,128]{3,2,1,0:T(8,128)(2,1)} %get-tuple-element.55), channel_id=1, source_target_pairs={{64,0},{128,64},{192,128},{256,192},{320,256},{384,320},{448,384},... | collective-permute-start | bytes 884744 | tf_op jit(solution)/shard_map/ppermute | solution.py:14
  610.7 32.2 %collective-permute-start.11 = (bf16[1,18,64,128]{3,2,1,0:T(8,128)(2,1)}, bf16[1,18,64,128]{3,2,1,0:T(8,128)(2,1)S(1)}, u32[]{:S(2)}, u32[]{:S(2)}) collective-permute-start(bf16[1,18,64,128]{3,2,1,0:T(8,128)(2,1)} %get-tuple-element.55), channel_id=1, source_target_pairs={{128,0},{192,64},{256,128},{320,192},{384,256},{448,320},{129,1},{... | collective-permute-start | bytes 884744 | tf_op jit(solution)/shard_map/ppermute | solution.py:14
  613.0 29.9 %collective-permute-start.6 = (bf16[1,18,64,128]{3,2,1,0:T(8,128)(2,1)S(1)}, bf16[1,18,64,128]{3,2,1,0:T(8,128)(2,1)S(1)}, u32[]{:S(2)}, u32[]{:S(2)}) collective-permute-start(bf16[1,18,64,128]{3,2,1,0:T(8,128)(2,1)S(1)} %get-tuple-element.57), channel_id=1, source_target_pairs={{64,0},{128,64},{192,128},{256,192},{320,256},{384,320},{448,384},... | collective-permute-start | bytes 884744 | tf_op jit(solution)/shard_map/ppermute | solution.py:14
  620.0 32.4 %collective-permute-start.7 = (bf16[1,18,64,128]{3,2,1,0:T(8,128)(2,1)S(1)}, bf16[1,18,64,128]{3,2,1,0:T(8,128)(2,1)S(1)}, u32[]{:S(2)}, u32[]{:S(2)}) collective-permute-start(bf16[1,18,64,128]{3,2,1,0:T(8,128)(2,1)S(1)} %get-tuple-element.57), channel_id=1, source_target_pairs={{128,0},{192,64},{256,128},{320,192},{384,256},{448,320},{129,1},{... | collective-permute-start | bytes 884744 | tf_op jit(solution)/shard_map/ppermute | solution.py:14
  621.3 31.1 %copy-start.20 = (f32[128]{0:T(128)S(1)}, f32[128]{0:T(128)}, u32[]{:S(2)}) copy-start(f32[128]{0:T(128)} %copy-done.19) | copy-start | bytes 1540
  621.3 31.1 %copy-start.22 = (f32[128]{0:T(128)S(1)}, f32[128]{0:T(128)}, u32[]{:S(2)}) copy-start(f32[128]{0:T(128)} %copy-done.21) | copy-start | bytes 1540
  621.3 31.1 %copy-start.24 = (f32[128]{0:T(128)S(1)}, f32[128]{0:T(128)}, u32[]{:S(2)}) copy-start(f32[128]{0:T(128)} %copy-done.23) | copy-start | bytes 1540
  621.4 31.1 %copy-start.26 = (f32[128]{0:T(128)S(1)}, f32[128]{0:T(128)}, u32[]{:S(2)}) copy-start(f32[128]{0:T(128)} %copy-done.25) | copy-start | bytes 1540
  621.4 31.1 %copy-start.28 = (f32[128]{0:T(128)S(1)}, f32[128]{0:T(128)}, u32[]{:S(2)}) copy-start(f32[128]{0:T(128)} %copy-done.27) | copy-start | bytes 1540
  621.4 31.1 %copy-start.30 = (f32[128]{0:T(128)S(1)}, f32[128]{0:T(128)}, u32[]{:S(2)}) copy-start(f32[128]{0:T(128)} %copy-done.29) | copy-start | bytes 1540
  621.4 31.1 %copy-start.32 = (f32[128]{0:T(128)S(1)}, f32[128]{0:T(128)}, u32[]{:S(2)}) copy-start(f32[128]{0:T(128)} %copy-done.31) | copy-start | bytes 1540
  (23 other events, 215.7 us)
Sparse Core Ops, SparseCore 0:
  10.1 57.5 all-gather.2
  92.5 272.7 all-reduce.8
  367.4 40.3 all-gather.4
  432.1 164.8 all-reduce.6
where the time goes:
time: 666 us; the launch traced here: 665 us
  waiting for transfers between devices  360 us (54%)
  blocking collectives  198 us (30%)
  starting transfers between devices  46.1 us (7%)
  other arithmetic  17 us (3%)
  local copies, waits for them, and re-layouts  16.8 us (3%)
  between operations  14.6 us (2%)
  matrix products  13.2 us (2%)
    psum x1, waiting for transfers between devices, on_device(): grad_proj = lax.psum(proj_term, ('row', 'chan', 'dp')) * weight_scale  270 us
    psum x1, blocking collectives, on_device(): lax.psum((point_term, depth_term), ('row', 'dp'))  155 us
    ppermute x16, waiting for transfers between devices, shifted(): lax.ppermute(value, axis, [(source, source + steps) for source in range(f...  48.8 us
    ppermute x16, starting transfers between devices, shifted(): lax.ppermute(value, axis, [(source, source + steps) for source in range(f...  45.9 us
    all_to_all x1, blocking collectives, on_device(): lax.all_to_all(spread, 'chan', split_axis=3, concat_axis=4, tiled=True)  43.2 us
    all_gather x1, waiting for transfers between devices, on_device(): incoming = lax.all_gather(pre_grad, 'chan', axis=3, tiled=True)  40.3 us
  transfers between devices with their start and end apart: 20, of which 9 were waited for; matrix products, arithmetic and copies ran while one was open for 4% of the time, Pallas kernels for 0%

commit v1 on v0

v1 whole, which is shorter than its diff:
```python
import functools
import math

import jax
import jax.numpy as jnp
from jax import lax
from jax.experimental import pallas as pl
from jax.experimental.pallas import tpu as pltpu
from jax.sharding import PartitionSpec as P

BASE_DILATION = 12
ROW_CLASSES = 2
COL_CLASSES = 4
MESH = pl.DeviceIdType.MESH


def reduce_kernel(rows, dps, x_ref, out_ref, landed, total, gathered, send1, recv1, send2, recv2):
    count = rows * dps
    me = lax.axis_index("row") * dps + lax.axis_index("dp")

    def device(step):
        peer = lax.rem(me + step, count)
        return peer, {"row": lax.div(peer, dps), "dp": lax.rem(peer, dps)}

    barrier = pltpu.get_barrier_semaphore()
    for step in range(1, count):
        pl.semaphore_signal(barrier, inc=1, device_id=device(step)[1], device_id_type=MESH)
    pl.semaphore_wait(barrier, count - 1)

    def scatter(step):
        peer, where = device(step)
        return pltpu.make_async_remote_copy(
            src_ref=x_ref.at[peer],
            dst_ref=landed.at[step],
            send_sem=send1.at[step],
            recv_sem=recv1.at[step],
            device_id=where,
            device_id_type=MESH,
        )

    def gather(step):
        _, where = device(step)
        return pltpu.make_async_remote_copy(
            src_ref=total,
            dst_ref=gathered.at[me],
            send_sem=send2.at[step],
            recv_sem=recv2.at[step],
            device_id=where,
            device_id_type=MESH,
        )

    for step in range(1, count):
        scatter(step).start()
    summed = x_ref[me]
    for step in range(1, count):
        scatter(step).wait_recv()
        summed = summed + landed[step]
    total[...] = summed
    for step in range(1, count):
        gather(step).start()
    for step in range(1, count):
        scatter(step).wait_send()
    for step in range(1, count):
        gather(step).wait()
    out_ref[...] = gathered[...]
    out_ref[me] = total[...]


def group_sum(value, collective_id):
    rows, dps = lax.axis_size("row"), lax.axis_size("dp")
    count, height, width = value.shape
    return pl.pallas_call(
        functools.partial(reduce_kernel, rows, dps),
        out_shape=jax.ShapeDtypeStruct(value.shape, jnp.float32),
        in_specs=[pl.BlockSpec(memory_space=pltpu.VMEM)],
        out_specs=pl.BlockSpec(memory_space=pltpu.VMEM),
        scratch_shapes=[
            pltpu.VMEM((count, height, width), jnp.float32),
            pltpu.VMEM((height, width), jnp.float32),
            pltpu.VMEM((count, height, width), jnp.float32),
            pltpu.SemaphoreType.DMA((count,)),
            pltpu.SemaphoreType.DMA((count,)),
            pltpu.SemaphoreType.DMA((count,)),
            pltpu.SemaphoreType.DMA((count,)),
        ],
        compiler_params=pltpu.CompilerParams(collective_id=collective_id, has_side_effects=True),
    )(value)


def exchange(value, axis):
    return lax.all_to_all(value, axis, split_axis=0, concat_axis=0, tiled=True)


def window(source, left, top, cols, rows):
    return source[left : left + cols, top : top + rows]


def on_device(features_in, depth_weights, point_weights, proj_weights, cotangent):
    samples, band_rows, band_cols, channels = features_in.shape
    bands, shares, dps = lax.axis_size("row"), lax.axis_size("chan"), lax.axis_size("dp")
    branches, _, width = point_weights.shape
    weight_scale = 1.0 / math.sqrt(samples * dps * band_rows * bands * band_cols)
    half = band_rows // ROW_CLASSES
    cols = band_cols // COL_CLASSES
    rows = half * bands
    row_step, col_step = BASE_DILATION // ROW_CLASSES, BASE_DILATION // COL_CLASSES

    classes = features_in.reshape(half, ROW_CLASSES, cols, COL_CLASSES, channels)
    classes = classes.transpose(1, 3, 0, 2, 4).reshape(bands, half, cols, channels)
    grid = exchange(classes, "row").reshape(rows, cols, channels).transpose(1, 0, 2)
    cells = cotangent.reshape(half, ROW_CLASSES, COL_CLASSES, width).transpose(1, 2, 0, 3)
    cot = exchange(cells.reshape(bands, half, width), "row").reshape(rows, width)
    full_point = lax.all_gather(point_weights, "chan", axis=0)
    full_cot = lax.all_gather(cot, "chan", axis=0)

    pads = ((3 * col_step, 3 * col_step), (3 * row_step, 3 * row_step), (0, 0))
    padded = jnp.pad(grid, pads)
    weights = depth_weights.astype(jnp.float32)
    maps = [grid]
    for level in range(1, branches):
        summed = jnp.zeros(grid.shape, jnp.float32)
        for i in range(3):
            for j in range(3):
                tap = window(
                    padded,
                    3 * col_step + (j - 1) * level * col_step,
                    3 * row_step + (i - 1) * level * row_step,
                    cols,
                    rows,
                )
                summed = summed + tap.astype(jnp.float32) * weights[level - 1, i, j]
        maps.append(summed.astype(jnp.bfloat16))
    spread = jnp.stack(maps, axis=1)
    preact = jnp.einsum(
        "gbnk,gbkf->bnf",
        exchange(spread, "chan"),
        full_point,
        preferred_element_type=jnp.float32,
    )
    logistic = jax.nn.sigmoid(preact)
    activation = (preact * logistic).astype(jnp.bfloat16)
    act_grad = jnp.einsum("ng,bfg->bnf", cot, proj_weights, preferred_element_type=jnp.float32)
    pre_grad = (act_grad * logistic * (1.0 + preact * (1.0 - logistic))).astype(jnp.bfloat16)
    incoming = lax.all_gather(pre_grad, "chan", axis=0)

    out_cells = jnp.einsum(
        "bnf,bfg->ng", activation, proj_weights, preferred_element_type=jnp.float32
    ).astype(jnp.bfloat16)
    output = exchange(out_cells.reshape(bands, half, width), "row")
    output = output.reshape(ROW_CLASSES, COL_CLASSES, half, width).transpose(2, 0, 1, 3)
    output = output.reshape(1, band_rows, COL_CLASSES, width)

    slices = shares // branches
    part = width // slices
    packed = activation.reshape(branches, 2, rows // 2, slices, part)
    packed = packed.transpose(0, 3, 2, 1, 4).reshape(shares, rows // 2, 2 * part)
    packed = exchange(packed, "chan")
    proj_part = jnp.zeros((part, width), jnp.float32)
    for side in range(2):
        proj_part = proj_part + jnp.einsum(
            "xnf,xng->fg",
            packed[:, :, side * part : (side + 1) * part],
            full_cot[:, side * (rows // 2) : (side + 1) * (rows // 2)],
            preferred_element_type=jnp.float32,
        )
    group = bands * dps
    proj_part = group_sum(proj_part.reshape(group, part // group, width), 0)
    proj_part = proj_part.reshape(part, width) * weight_scale
    grad_proj = lax.all_gather(proj_part, "chan", axis=0).reshape(branches, width, width)

    point_sum = jnp.einsum("xbnk,xbnf->bkf", spread, incoming, preferred_element_type=jnp.float32)
    spread_grad = jnp.einsum(
        "xbnf,bkf->bxnk", incoming, point_weights, preferred_element_type=jnp.float32
    ).astype(jnp.bfloat16)
    grad_in = spread_grad[0].astype(jnp.float32)
    depth_sums = []
    for level in range(1, branches):
        branch_grad = spread_grad[level].astype(jnp.float32)
        grad_padded = jnp.pad(spread_grad[level], pads)
        for i in range(3):
            for j in range(3):
                left, top = (j - 1) * level * col_step, (i - 1) * level * row_step
                tap = window(padded, 3 * col_step + left, 3 * row_step + top, cols, rows)
                depth_sums.append(jnp.sum(tap.astype(jnp.float32) * branch_grad, axis=(0, 1)))
                grad_tap = window(
                    grad_padded, 3 * col_step - left, 3 * row_step - top, cols, rows
                )
                grad_in = grad_in + grad_tap.astype(jnp.float32) * weights[level - 1, i, j]
    returned = grad_in.astype(jnp.bfloat16).transpose(1, 0, 2)
    returned = exchange(returned.reshape(bands, half, cols, channels), "row")
    returned = returned.reshape(ROW_CLASSES, COL_CLASSES, half, cols, channels)
    grad_input = returned.transpose(2, 0, 3, 1, 4).reshape(features_in.shape)

    taps = len(depth_sums)
    depth_part = jnp.pad(jnp.stack(depth_sums), ((0, group - taps), (0, width - channels)))
    summed = group_sum(
        jnp.concatenate(
            [
                point_sum.reshape(group, branches * channels // group, width),
                depth_part[:, None],
            ],
            axis=1,
        ),
        1,
    )
    grad_point = summed[:, :-1].reshape(point_weights.shape) * weight_scale
    grad_depth = summed[:taps, -1, :channels].reshape(depth_weights.shape) * weight_scale
    return (output, grad_input, grad_depth, grad_point, grad_proj)


def solution(mesh):
    in_specs = (
        P("dp", "row", None, "chan"),
        P(None, None, None, "chan"),
        P(None, "chan", None),
        P(),
        P("dp", "row", "chan", None),
    )
    out_specs = (
        P("dp", "row", "chan", None),
        P("dp", "row", None, "chan"),
        P(None, None, None, "chan"),
        P(None, "chan", None),
        P(),
    )
    return jax.shard_map(
        on_device, mesh=mesh, in_specs=in_specs, out_specs=out_specs, check_vma=False
    )
```

time: 666 us -> 302 us (0.45)
  the two profiles are of different devices: /device:TPU:8 before, /device:TPU:1 now
where the time goes in v1:
time: 302 us; the launch traced here: 299 us
  waiting for transfers between devices  115 us (38%)
  Pallas kernels  68 us (23%)
  starting transfers between devices  38.1 us (13%)
  blocking collectives  29.9 us (10%)
  other arithmetic  14.7 us (5%)
  between operations  14 us (5%)
  local copies, waits for them, and re-layouts  10.3 us (3%)
  matrix products  9.59 us (3%)
    pallas_call x2, Pallas kernels, group_sum(): pl.pallas_call(functools.partial(reduce_kernel, rows, dps), out_shape=jax...  68 us
    all_gather x1, waiting for transfers between devices, on_device(): incoming = lax.all_gather(pre_grad, 'chan', axis=0)  44 us
    all_to_all x5, waiting for transfers between devices, exchange(): return lax.all_to_all(value, axis, split_axis=0, concat_axis=0, tiled=True)  43.3 us
    all_to_all x5, starting transfers between devices, exchange(): return lax.all_to_all(value, axis, split_axis=0, concat_axis=0, tiled=True)  38 us
    all_gather x1, waiting for transfers between devices, on_device(): lax.all_gather(proj_part, 'chan', axis=0).reshape(branches, width, width)  26.6 us
    all_gather x1, blocking collectives, on_device(): full_cot = lax.all_gather(cot, 'chan', axis=0)  19.7 us
    all_to_all x1, blocking collectives, exchange(): return lax.all_to_all(value, axis, split_axis=0, concat_axis=0, tiled=True)  10.2 us
    transpose x1, other arithmetic, on_device(): returned = grad_in.astype(jnp.bfloat16).transpose(1, 0, 2)  6.26 us
  transfers between devices with their start and end apart: 8, of which 5 were waited for; matrix products, arithmetic and copies ran while one was open for 4% of the time, Pallas kernels for 16%

profile of v1, /device:TPU:1, one launch (start us, length us, event | category | flops | bytes accessed | tf_op | source)
XLA Modules:
  0.0 299.2 jit_solution(2597817781822283957)
XLA Ops:
  7.2 0.7 all-gather.8.cloned.1.call-update
  7.9 1.7 copy.39
  9.7 7.6 %all-to-all-start = ((bf16[8,9,16,128]{3,2,1,0:T(8,128)(2,1)}), bf16[8,9,16,128]{3,2,1,0:T(8,128)(2,1)S(1)}, u32[]{:S(2)}, u32[]{:S(2)}) async-start(bf16[8,9,16,128]{3,2,1,0:T(8,128)(2,1)} %bitcast.2), calls=%async_computation | async-start | bytes 589824 | tf_op jit(solution)/shard_map/all_to_all | solution.py:91
  18.0 9.3 %all-to-all-done = bf16[8,9,16,128]{3,2,1,0:T(8,128)(2,1)S(1)} async-done(((bf16[8,9,16,128]{3,2,1,0:T(8,128)(2,1)}), bf16[8,9,16,128]{3,2,1,0:T(8,128)(2,1)S(1)}, u32[]{:S(2)}, u32[]{:S(2)}) %all-to-all-start) | async-done | bytes 294944 | tf_op jit(solution)/shard_map/all_to_all | solution.py:91
  27.3 3.4 %all-to-all-start.3 = ((bf16[8,9,256]{2,1,0:T(8,128)(2,1)}), bf16[8,9,256]{2,1,0:T(8,128)(2,1)S(1)}, u32[]{:S(2)}, u32[]{:S(2)}) async-start(bf16[8,9,256]{2,1,0:T(8,128)(2,1)} %bitcast.44), calls=%async_computation.3 | async-start | bytes 131072 | tf_op jit(solution)/shard_map/all_to_all | solution.py:91
  32.5 1.1 copy.41
  33.6 4.2 %all-to-all-done.3 = bf16[8,9,256]{2,1,0:T(8,128)(2,1)S(1)} async-done(((bf16[8,9,256]{2,1,0:T(8,128)(2,1)}), bf16[8,9,256]{2,1,0:T(8,128)(2,1)S(1)}, u32[]{:S(2)}, u32[]{:S(2)}) %all-to-all-start.3) | async-done | bytes 36896 | tf_op jit(solution)/shard_map/all_to_all | solution.py:91
  37.8 15.0 %all-to-all-start.1 = ((bf16[16,4,72,128]{3,2,1,0:T(8,128)(2,1)}), bf16[16,4,72,128]{3,2,1,0:T(8,128)(2,1)S(1)}, u32[]{:S(2)}, u32[]{:S(2)}) async-start(bf16[16,4,72,128]{3,2,1,0:T(8,128)(2,1)} %copy.41), calls=%async_computation.1 | async-start | bytes 2359296 | tf_op jit(solution)/shard_map/all_to_all | solution.py:91
  52.8 29.8 %all-to-all-done.1 = bf16[16,4,72,128]{3,2,1,0:T(8,128)(2,1)S(1)} async-done(((bf16[16,4,72,128]{3,2,1,0:T(8,128)(2,1)}), bf16[16,4,72,128]{3,2,1,0:T(8,128)(2,1)S(1)}, u32[]{:S(2)}, u32[]{:S(2)}) %all-to-all-start.1) | async-done | bytes 1179680 | tf_op jit(solution)/shard_map/all_to_all | solution.py:91
  82.6 3.8 %multiply_convert_fusion = (bf16[4,72,256]{2,1,0:T(8,128)(2,1)S(1)}, f32[4,72,256]{2,1,0:T(8,128)}) fusion(bf16[16,4,72,128]{3,2,1,0:T(8,128)(2,1)S(1)} %all-to-all-done.1, bf16[16,4,128,256]{3,2,1,0:T(8,128)(2,1)} %bitcast.238), kind=kOutput, calls=%fused_computation.212 | convolution fusion | flops 302358528 | bytes 5816320 | tf_op jit(solution)/shard_map/gbnk,gbkf->bnf/dot_general | solution.py:134
  87.0 0.7 copy.49
  87.7 5.5 %all-to-all-start.5 = ((bf16[16,36,128]{2,1,0:T(8,128)(2,1)}), bf16[16,36,128]{2,1,0:T(8,128)(2,1)S(1)}, u32[]{:S(2)}, u32[]{:S(2)}) async-start(bf16[16,36,128]{2,1,0:T(8,128)(2,1)} %copy.49), calls=%async_computation.5 | async-start | bytes 327680 | tf_op jit(solution)/shard_map/all_to_all | solution.py:91
  93.2 19.7 %all_gather.23 = bf16[16,72,256]{2,1,0:T(8,128)(2,1)S(1)} all-gather(bf16[1,72,256]{2,1,0:T(8,128)(2,1)S(1)} %all_gather_reshape.3), channel_id=1, replica_groups=mesh['row'=8,'chan'=16,'dp'=4] {'chan'}, dimensions={0}, use_global_device_ids=true | all-gather | bytes 626688 | tf_op jit(solution)/shard_map/all_gather | solution.py:114
  114.1 19.6 %shard_map.93 = f32[32,2,256]{2,1,0:T(2,128)} custom-call(f32[32,2,256]{2,1,0:T(2,128)} %reshape.123.x_ref), custom_call_target="tpu_custom_call" | custom-call | tf_op jit(solution)/shard_map/pallas_call | solution.py:72
  133.8 0.9 broadcast_multiply_fusion
  134.6 0.7 mul.706
  135.4 1.0 fusion.9
  136.7 10.2 %all_to_all.30 = bf16[8,9,256]{2,1,0:T(8,128)(2,1)S(1)} all-to-all(bf16[8,9,256]{2,1,0:T(8,128)(2,1)S(1)} %reshape.111), channel_id=1, replica_groups=mesh['row'=8,'chan'=16,'dp'=4] {'row'}, dimensions={0} | all-to-all | bytes 73728 | tf_op jit(solution)/shard_map/all_to_all | solution.py:91
  147.6 26.6 %all-gather.6.cloned.1.call-done = f32[16,64,256]{2,1,0:T(8,128)} async-done(((f32[1,64,256]{2,1,0:T(8,128)}), f32[16,64,256]{2,1,0:T(8,128)}) %all-gather.6.cloned.1.call-update) | async-done | bytes 1048592 | tf_op jit(solution)/shard_map/all_gather | solution.py:169
  174.1 44.0 %all-gather.10.cloned.1.call-done = bf16[64,72,256]{2,1,0:T(8,128)(2,1)} async-done(((bf16[4,72,256]{2,1,0:T(8,128)(2,1)}), bf16[64,72,256]{2,1,0:T(8,128)(2,1)}) %all-gather.10.cloned.1.call-update) | async-done | bytes 2359312 | tf_op jit(solution)/shard_map/all_gather | solution.py:144
  218.2 3.3 %fusion = f32[4,128,256,1]{2,1,3,0:T(8,128)} fusion(bf16[16,4,72,256]{3,2,1,0:T(8,128)(2,1)} %bitcast.278, bf16[16,1,72,128]{3,2,0,1:T(8,128)(2,1)S(1)} %fusion.95, bf16[16,1,72,128]{3,2,0,1:T(8,128)(2,1)S(1)} %fusion.96, bf16[16,1,72,128]{3,2,0,1:T(8,128)(2,1)S(1)} %fusion.97, bf16[16,1,72,128]{3,2,0,1:T(8,128)(2,1)S(1)} %bitcast.234), kind=kOutput, calls=%fused_computation.48 | convolution fusion | flops 303759360 | bytes 4063232 | tf_op jit(solution)/shard_map/xbnk,xbnf->bkf/dot_general | solution.py:171
  221.5 0.8 fusion.4
  222.3 0.7 fusion.88
  223.7 6.3 %fusion.98 = bf16[72,16,128]{2,0,1:T(8,128)(2,1)S(1)} fusion(f32[128]{0:T(128)S(1)} %get-tuple-element.41, bf16[16,72,128]{2,1,0:T(8,128)(2,1)S(1)} %get-tuple-element.36, f32[128]{0:T(128)S(1)} %get-tuple-element.42, f32[128]{0:T(128)S(1)} %get-tuple-element.43, f32[128]{0:T(128)S(1)} %get-tuple-element.44, f32[128]{0:T(128)S(1)} %get-tuple-element.45, ...), kind=kLoop, calls=%fused_computation.217 | loop fusion | flops 12238848 | bytes 1488384 | tf_op jit(solution)/shard_map/transpose | solution.py:189
  230.0 0.8 copy.45
  230.7 6.6 %all-to-all-start.4 = ((bf16[8,9,16,128]{3,2,1,0:T(8,128)(2,1)}), bf16[8,9,16,128]{3,2,1,0:T(8,128)(2,1)S(1)}, u32[]{:S(2)}, u32[]{:S(2)}) async-start(bf16[8,9,16,128]{3,2,1,0:T(8,128)(2,1)} %bitcast.54), calls=%async_computation.4 | async-start | bytes 589824 | tf_op jit(solution)/shard_map/all_to_all | solution.py:91
  238.0 1.0 pad_maximum_fusion.1.x_ref
  238.9 48.4 %shard_map.92 = f32[32,17,256]{2,1,0:T(8,128)} custom-call(f32[32,17,256]{2,1,0:T(8,128)} %pad_maximum_fusion.1.x_ref), custom_call_target="tpu_custom_call" | custom-call | tf_op jit(solution)/shard_map/pallas_call | solution.py:72
  287.3 1.0 multiply_reduce_fusion
  289.0 1.9 slice_multiply_fusion
  290.9 0.9 copy.46
  291.7 1.0 copy.71
  (51 shorter events, 7.4 us)
Async XLA Ops:
  7.2 128.3 %copy-start = (bf16[4,256,256]{2,1,0:T(8,128)(2,1)S(1)}, bf16[4,256,256]{2,1,0:T(8,128)(2,1)}, u32[]{:S(2)}) copy-start(bf16[4,256,256]{2,1,0:T(8,128)(2,1)} %param.8) | copy-start | bytes 1572868
  7.2 10.1 %copy-start.6 = (bf16[3,3,3,128]{3,2,1,0:T(4,128)(2,1)S(1)}, bf16[3,3,3,128]{3,2,1,0:T(4,128)(2,1)}, u32[]{:S(2)}) copy-start(bf16[3,3,3,128]{3,2,1,0:T(4,128)(2,1)} %param.6) | copy-start | bytes 20740
  7.2 10.1 %copy-start.5 = (bf16[1,18,4,256]{3,2,1,0:T(4,128)(2,1)S(1)}, bf16[1,18,4,256]{3,2,1,0:T(4,128)(2,1)}, u32[]{:S(2)}) copy-start(bf16[1,18,4,256]{3,2,1,0:T(4,128)(2,1)} %param.9) | copy-start | bytes 110596
  7.2 75.4 %all-gather.8.cloned.1.call-start = ((), (), s32[]{:S(2)}) async-start(), calls=%async_computation.7 | async-start | bytes 4456448 | tf_op jit(solution)/shard_map/all_gather | solution.py:113
  9.7 17.6 %all-to-all-start = ((bf16[8,9,16,128]{3,2,1,0:T(8,128)(2,1)}), bf16[8,9,16,128]{3,2,1,0:T(8,128)(2,1)S(1)}, u32[]{:S(2)}, u32[]{:S(2)}) async-start(bf16[8,9,16,128]{3,2,1,0:T(8,128)(2,1)} %bitcast.2), calls=%async_computation | async-start | bytes 589824 | tf_op jit(solution)/shard_map/all_to_all | solution.py:91
  27.3 10.5 %all-to-all-start.3 = ((bf16[8,9,256]{2,1,0:T(8,128)(2,1)}), bf16[8,9,256]{2,1,0:T(8,128)(2,1)S(1)}, u32[]{:S(2)}, u32[]{:S(2)}) async-start(bf16[8,9,256]{2,1,0:T(8,128)(2,1)} %bitcast.44), calls=%async_computation.3 | async-start | bytes 131072 | tf_op jit(solution)/shard_map/all_to_all | solution.py:91
  37.8 44.8 %all-to-all-start.1 = ((bf16[16,4,72,128]{3,2,1,0:T(8,128)(2,1)}), bf16[16,4,72,128]{3,2,1,0:T(8,128)(2,1)S(1)}, u32[]{:S(2)}, u32[]{:S(2)}) async-start(bf16[16,4,72,128]{3,2,1,0:T(8,128)(2,1)} %copy.41), calls=%async_computation.1 | async-start | bytes 2359296 | tf_op jit(solution)/shard_map/all_to_all | solution.py:91
  87.7 25.2 %all-to-all-start.5 = ((bf16[16,36,128]{2,1,0:T(8,128)(2,1)}), bf16[16,36,128]{2,1,0:T(8,128)(2,1)S(1)}, u32[]{:S(2)}, u32[]{:S(2)}) async-start(bf16[16,36,128]{2,1,0:T(8,128)(2,1)} %copy.49), calls=%async_computation.5 | async-start | bytes 327680 | tf_op jit(solution)/shard_map/all_to_all | solution.py:91
  93.2 80.9 %all-gather.6.cloned.1.call-start = ((), (), s32[]{:S(2)}) async-start(), calls=%async_computation.6 | async-start | bytes 1114112 | tf_op jit(solution)/shard_map/all_gather | solution.py:169
  112.9 22.5 %copy-start.3 = (f32[4,72,256]{2,1,0:T(8,128)S(1)}, f32[4,72,256]{2,1,0:T(8,128)}, u32[]{:S(2)}) copy-start(f32[4,72,256]{2,1,0:T(8,128)} %get-tuple-element.68) | copy-start | bytes 884740
  135.3 82.8 %all-gather.10.cloned.1.call-start = ((), (), s32[]{:S(2)}) async-start(), calls=%async_computation.8 | async-start | bytes 2506752 | tf_op jit(solution)/shard_map/all_gather | solution.py:144
  218.2 3.3 %copy-start.4 = (bf16[4,128,256]{2,1,0:T(8,128)(2,1)S(1)}, bf16[4,128,256]{2,1,0:T(8,128)(2,1)}, u32[]{:S(2)}) copy-start(bf16[4,128,256]{2,1,0:T(8,128)(2,1)} %param.7) | copy-start | bytes 786436
  218.2 3.3 %copy-start.7 = (bf16[64,72,256]{2,1,0:T(8,128)(2,1)S(1)}, bf16[64,72,256]{2,1,0:T(8,128)(2,1)}, u32[]{:S(2)}) copy-start(bf16[64,72,256]{2,1,0:T(8,128)(2,1)} %all-gather.10.cloned.1.call-done) | copy-start | bytes 7077892
  230.7 7.3 %copy-start.2 = (f32[4,128,256,1]{2,1,3,0:T(8,128)S(1)}, f32[4,128,256,1]{2,1,3,0:T(8,128)}, u32[]{:S(2)}) copy-start(f32[4,128,256,1]{2,1,3,0:T(8,128)} %fusion) | copy-start | bytes 1572868
  230.7 60.2 %all-to-all-start.4 = ((bf16[8,9,16,128]{3,2,1,0:T(8,128)(2,1)}), bf16[8,9,16,128]{3,2,1,0:T(8,128)(2,1)S(1)}, u32[]{:S(2)}, u32[]{:S(2)}) async-start(bf16[8,9,16,128]{3,2,1,0:T(8,128)(2,1)} %bitcast.54), calls=%async_computation.4 | async-start | bytes 589824 | tf_op jit(solution)/shard_map/all_to_all | solution.py:91
  287.3 4.4 %copy-start.1 = (f32[16,64,256]{2,1,0:T(8,128)S(1)}, f32[16,64,256]{2,1,0:T(8,128)}, u32[]{:S(2)}) copy-start(f32[16,64,256]{2,1,0:T(8,128)} %all-gather.6.cloned.1.call-done) | copy-start | bytes 3145732
Sparse Core Ops, SparseCore 0:
  10.1 57.5 all-gather.7
  135.5 38.6 all-gather.5
  176.8 41.2 all-gather.9

commit v2 on v1

--- a/solution.py
+++ b/solution.py
@@ -51,11 +51,11 @@
 
     for step in range(1, count):
         scatter(step).start()
-    summed = x_ref[me]
+    summed = x_ref[me].astype(jnp.float32)
     for step in range(1, count):
         scatter(step).wait_recv()
-        summed = summed + landed[step]
-    total[...] = summed
+        summed = summed + landed[step].astype(jnp.float32)
+    total[...] = summed.astype(total.dtype)
     for step in range(1, count):
         gather(step).start()
     for step in range(1, count):
@@ -71,19 +71,105 @@
     count, height, width = value.shape
     return pl.pallas_call(
         functools.partial(reduce_kernel, rows, dps),
-        out_shape=jax.ShapeDtypeStruct(value.shape, jnp.float32),
+        out_shape=jax.ShapeDtypeStruct(value.shape, value.dtype),
         in_specs=[pl.BlockSpec(memory_space=pltpu.VMEM)],
         out_specs=pl.BlockSpec(memory_space=pltpu.VMEM),
         scratch_shapes=[
-            pltpu.VMEM((count, height, width), jnp.float32),
-            pltpu.VMEM((height, width), jnp.float32),
-            pltpu.VMEM((count, height, width), jnp.float32),
+            pltpu.VMEM((count, height, width), value.dtype),
+            pltpu.VMEM((height, width), value.dtype),
+            pltpu.VMEM((count, height, width), value.dtype),
             pltpu.SemaphoreType.DMA((count,)),
             pltpu.SemaphoreType.DMA((count,)),
             pltpu.SemaphoreType.DMA((count,)),
             pltpu.SemaphoreType.DMA((count,)),
         ],
         compiler_params=pltpu.CompilerParams(collective_id=collective_id, has_side_effects=True),
+        cost_estimate=pl.CostEstimate(flops=0, bytes_accessed=80_000_000, transcendentals=0),
+    )(value)
+
+
+def ring_kernel(chips, cut, x_ref, out_ref, held, ring_send, ring_recv, pair_send, pair_recv):
+    me = lax.axis_index("chan")
+    chip, core = lax.div(me, 2), lax.rem(me, 2)
+    hops = chips // 2
+    size = x_ref.shape[0]
+    spans = (pl.ds(0, cut), pl.ds(cut, size - cut))
+
+    def block(away):
+        return lax.rem(chip + away + chips, chips) * 2 + core
+
+    ahead = {"chan": block(1)}
+    behind = {"chan": block(-1)}
+    twin = {"chan": chip * 2 + 1 - core}
+    targets = (ahead, behind)
+
+    barrier = pltpu.get_barrier_semaphore()
+    for where in (ahead, behind, twin):
+        pl.semaphore_signal(barrier, inc=1, device_id=where, device_id_type=MESH)
+    pl.semaphore_wait(barrier, 3)
+
+    def ring(way, hop):
+        away = 1 - hop if way == 0 else hop - 1
+        source, landing = (x_ref if hop == 1 else held.at[block(away)]), held.at[block(away)]
+        if hop == hops:
+            source, landing = source.at[spans[way]], landing.at[spans[way]]
+        return pltpu.make_async_remote_copy(
+            src_ref=source,
+            dst_ref=landing,
+            send_sem=ring_send.at[way, hop],
+            recv_sem=ring_recv.at[way, hop],
+            device_id=targets[way],
+            device_id_type=MESH,
+        )
+
+    def pair(way, hop):
+        away = -hop if way == 0 else hop
+        source, landing = (x_ref if hop == 0 else held.at[block(away)]), held.at[block(away)]
+        if hop == hops:
+            source, landing = source.at[spans[way]], landing.at[spans[way]]
+        return pltpu.make_async_remote_copy(
+            src_ref=source,
+            dst_ref=landing,
+            send_sem=pair_send.at[way, hop],
+            recv_sem=pair_recv.at[way, hop],
+            device_id=twin,
+            device_id_type=MESH,
+        )
+
+    pairs = [(0, 0)]
+    for way in range(2):
+        ring(way, 1).start()
+    pair(0, 0).start()
+    for hop in range(1, hops + 1):
+        for way in range(2):
+            ring(way, hop).wait_recv()
+            if hop < hops:
+                ring(way, hop + 1).start()
+            pair(way, hop).start()
+            pairs.append((way, hop))
+    for hop in range(1, hops + 1):
+        for way in range(2):
+            ring(way, hop).wait_send()
+    for way, hop in pairs:
+        pair(way, hop).wait()
+    out_ref[...] = held[...]
+    out_ref[me] = x_ref[...]
+
+
+def ring_gather(value, cut, collective_id):
+    shares = lax.axis_size("chan")
+    chips = shares // 2
+    sems = pltpu.SemaphoreType.DMA((2, chips // 2 + 1))
+    return pl.pallas_call(
+        functools.partial(ring_kernel, chips, cut),
+        out_shape=jax.ShapeDtypeStruct((shares,) + value.shape, value.dtype),
+        in_specs=[pl.BlockSpec(memory_space=pltpu.VMEM)],
+        out_specs=pl.BlockSpec(memory_space=pltpu.VMEM),
+        scratch_shapes=[
+            pltpu.VMEM((shares,) + value.shape, value.dtype), sems, sems, sems, sems
+        ],
+        compiler_params=pltpu.CompilerParams(collective_id=collective_id, has_side_effects=True),
+        cost_estimate=pl.CostEstimate(flops=0, bytes_accessed=80_000_000, transcendentals=0),
     )(value)
 
 
@@ -106,12 +192,17 @@
     row_step, col_step = BASE_DILATION // ROW_CLASSES, BASE_DILATION // COL_CLASSES
 
     classes = features_in.reshape(half, ROW_CLASSES, cols, COL_CLASSES, channels)
-    classes = classes.transpose(1, 3, 0, 2, 4).reshape(bands, half, cols, channels)
-    grid = exchange(classes, "row").reshape(rows, cols, channels).transpose(1, 0, 2)
+    classes = classes.transpose(1, 3, 0, 2, 4).reshape(bands, half * cols, channels)
     cells = cotangent.reshape(half, ROW_CLASSES, COL_CLASSES, width).transpose(1, 2, 0, 3)
-    cot = exchange(cells.reshape(bands, half, width), "row").reshape(rows, width)
+    cells = cells.reshape(bands, half, width)
+    landed = exchange(
+        jnp.concatenate([classes, cells[:, :, :channels], cells[:, :, channels:]], axis=1), "row"
+    )
+    area = half * cols
+    grid = landed[:, :area].reshape(rows, cols, channels).transpose(1, 0, 2)
+    cot = jnp.concatenate([landed[:, area : area + half], landed[:, area + half :]], axis=2)
+    cot = cot.reshape(rows, width)
     full_point = lax.all_gather(point_weights, "chan", axis=0)
-    full_cot = lax.all_gather(cot, "chan", axis=0)
 
     pads = ((3 * col_step, 3 * col_step), (3 * row_step, 3 * row_step), (0, 0))
     padded = jnp.pad(grid, pads)
@@ -141,20 +232,19 @@
     activation = (preact * logistic).astype(jnp.bfloat16)
     act_grad = jnp.einsum("ng,bfg->bnf", cot, proj_weights, preferred_element_type=jnp.float32)
     pre_grad = (act_grad * logistic * (1.0 + preact * (1.0 - logistic))).astype(jnp.bfloat16)
-    incoming = lax.all_gather(pre_grad, "chan", axis=0)
-
     out_cells = jnp.einsum(
         "bnf,bfg->ng", activation, proj_weights, preferred_element_type=jnp.float32
     ).astype(jnp.bfloat16)
-    output = exchange(out_cells.reshape(bands, half, width), "row")
-    output = output.reshape(ROW_CLASSES, COL_CLASSES, half, width).transpose(2, 0, 1, 3)
-    output = output.reshape(1, band_rows, COL_CLASSES, width)
 
     slices = shares // branches
     part = width // slices
     packed = activation.reshape(branches, 2, rows // 2, slices, part)
     packed = packed.transpose(0, 3, 2, 1, 4).reshape(shares, rows // 2, 2 * part)
     packed = exchange(packed, "chan")
+    sent = jnp.concatenate([pre_grad.reshape(branches * rows, width), cot], axis=0)
+    held = ring_gather(sent, sent.shape[0] // 32 * 16, 0)
+    incoming = held[:, : branches * rows].reshape(shares, branches, rows, width)
+    full_cot = held[:, branches * rows :]
     proj_part = jnp.zeros((part, width), jnp.float32)
     for side in range(2):
         proj_part = proj_part + jnp.einsum(
@@ -164,10 +254,6 @@
             preferred_element_type=jnp.float32,
         )
     group = bands * dps
-    proj_part = group_sum(proj_part.reshape(group, part // group, width), 0)
-    proj_part = proj_part.reshape(part, width) * weight_scale
-    grad_proj = lax.all_gather(proj_part, "chan", axis=0).reshape(branches, width, width)
-
     point_sum = jnp.einsum("xbnk,xbnf->bkf", spread, incoming, preferred_element_type=jnp.float32)
     spread_grad = jnp.einsum(
         "xbnf,bkf->bxnk", incoming, point_weights, preferred_element_type=jnp.float32
@@ -186,25 +272,39 @@
                     grad_padded, 3 * col_step - left, 3 * row_step - top, cols, rows
                 )
                 grad_in = grad_in + grad_tap.astype(jnp.float32) * weights[level - 1, i, j]
-    returned = grad_in.astype(jnp.bfloat16).transpose(1, 0, 2)
-    returned = exchange(returned.reshape(bands, half, cols, channels), "row")
-    returned = returned.reshape(ROW_CLASSES, COL_CLASSES, half, cols, channels)
-    grad_input = returned.transpose(2, 0, 3, 1, 4).reshape(features_in.shape)
+    returned = grad_in.astype(jnp.bfloat16).transpose(1, 0, 2).reshape(bands, area, channels)
+    out_cells = out_cells.reshape(bands, half, width)
+    returned = exchange(
+        jnp.concatenate([returned, out_cells[:, :, :channels], out_cells[:, :, channels:]], axis=1),
+        "row",
+    )
+    output = jnp.concatenate(
+        [returned[:, area : area + half], returned[:, area + half :]], axis=2
+    )
+    output = output.reshape(ROW_CLASSES, COL_CLASSES, half, width).transpose(2, 0, 1, 3)
+    output = output.reshape(1, band_rows, COL_CLASSES, width)
+    grad_input = returned[:, :area].reshape(ROW_CLASSES, COL_CLASSES, half, cols, channels)
+    grad_input = grad_input.transpose(2, 0, 3, 1, 4).reshape(features_in.shape)
 
     taps = len(depth_sums)
     depth_part = jnp.pad(jnp.stack(depth_sums), ((0, group - taps), (0, width - channels)))
+    height = branches * channels // group
     summed = group_sum(
         jnp.concatenate(
             [
-                point_sum.reshape(group, branches * channels // group, width),
+                point_sum.reshape(group, height, width),
                 depth_part[:, None],
+                proj_part.reshape(group, part // group, width),
             ],
             axis=1,
-        ),
+        ).astype(jnp.bfloat16),
         1,
     )
-    grad_point = summed[:, :-1].reshape(point_weights.shape) * weight_scale
-    grad_depth = summed[:taps, -1, :channels].reshape(depth_weights.shape) * weight_scale
+    grad_point = summed[:, :height].reshape(point_weights.shape).astype(jnp.float32) * weight_scale
+    grad_depth = summed[:taps, height, :channels].reshape(depth_weights.shape)
+    grad_depth = grad_depth.astype(jnp.float32) * weight_scale
+    grad_proj = ring_gather(summed[:, height + 1 :].reshape(part, width), part // 2, 2)
+    grad_proj = grad_proj.reshape(branches, width, width).astype(jnp.float32) * weight_scale
     return (output, grad_input, grad_depth, grad_point, grad_proj)
 
 

time: 302 us -> 221 us (0.73)
  waiting for transfers between devices: 115 us -> 46.8 us
  blocking collectives: 29.9 us -> 0 us
  Pallas kernels: 68 us -> 79.2 us
  local copies, waits for them, and re-layouts: 10.3 us -> 20.3 us
  starting transfers between devices: 38.1 us -> 33.3 us
    all_gather x2 -> x0, waiting for transfers between devices: 70.6 us -> none  [the longest x1 44 us: on_device(): incoming = lax.all_gather(pre_grad, 'chan', axis=0)]
    pallas_call x0 -> x2, Pallas kernels: none -> 46.9 us  [ring_gather(): pl.pallas_call(functools.partial(ring_kernel, chips, cut), out_shape=jax....]
    pallas_call x2 -> x1, Pallas kernels: 68 us -> 32.3 us  [group_sum(): pl.pallas_call(functools.partial(reduce_kernel, rows, dps), out_shape=jax...]
    all_gather x1 -> x0, blocking collectives: 19.7 us -> none  [on_device(): full_cot = lax.all_gather(cot, 'chan', axis=0)]
    all_to_all x1 -> x0, blocking collectives: 10.2 us -> none  [exchange(): return lax.all_to_all(value, axis, split_axis=0, concat_axis=0, tiled=True)]
    all_to_all x5 -> x4, starting transfers between devices: 38 us -> 33.3 us  [exchange(): return lax.all_to_all(value, axis, split_axis=0, concat_axis=0, tiled=True)]
    all_to_all x5 -> x4, waiting for transfers between devices: 43.3 us -> 46.1 us  [exchange(): return lax.all_to_all(value, axis, split_axis=0, concat_axis=0, tiled=True)]
  transfers between devices with their start and end apart: 8 -> 5, of which waited for: 5 -> 3; matrix products, arithmetic and copies ran while one was open for 4% -> 11% of each run, Pallas kernels for 16% -> 23%
where the time goes in v2:
time: 221 us; the launch traced here: 220 us
  Pallas kernels  79.2 us (36%)
  waiting for transfers between devices  46.8 us (21%)
  starting transfers between devices  33.3 us (15%)
  local copies, waits for them, and re-layouts  20.3 us (9%)
  other arithmetic  16.5 us (7%)
  between operations  14.8 us (7%)
  matrix products  9.38 us (4%)
    pallas_call x2, Pallas kernels, ring_gather(): pl.pallas_call(functools.partial(ring_kernel, chips, cut), out_shape=jax....  46.9 us
    all_to_all x4, waiting for transfers between devices, exchange(): return lax.all_to_all(value, axis, split_axis=0, concat_axis=0, tiled=True)  46.1 us
    all_to_all x4, starting transfers between devices, exchange(): return lax.all_to_all(value, axis, split_axis=0, concat_axis=0, tiled=True)  33.3 us
    pallas_call x1, Pallas kernels, group_sum(): pl.pallas_call(functools.partial(reduce_kernel, rows, dps), out_shape=jax...  32.3 us
  transfers between devices with their start and end apart: 5, of which 3 were waited for; matrix products, arithmetic and copies ran while one was open for 11% of the time, Pallas kernels for 23%

profile of v2, /device:TPU:1, one launch (start us, length us, event | category | flops | bytes accessed | tf_op | source)
XLA Modules:
  0.0 220.2 jit_solution(11205111466177326951)
XLA Ops:
  8.7 1.0 copy.40
  10.5 7.6 %all-to-all-start = ((bf16[8,162,128]{2,1,0:T(8,128)(2,1)}), bf16[8,162,128]{2,1,0:T(8,128)(2,1)S(1)}, u32[]{:S(2)}, u32[]{:S(2)}) async-start(bf16[8,162,128]{2,1,0:T(8,128)(2,1)} %pad_maximum_fusion.2), calls=%async_computation | async-start | bytes 688128 | tf_op jit(solution)/shard_map/all_to_all | solution.py:177
  18.5 9.8 %all-to-all-done = bf16[8,162,128]{2,1,0:T(8,128)(2,1)S(1)} async-done(((bf16[8,162,128]{2,1,0:T(8,128)(2,1)}), bf16[8,162,128]{2,1,0:T(8,128)(2,1)S(1)}, u32[]{:S(2)}, u32[]{:S(2)}) %all-to-all-start) | async-done | bytes 331808 | tf_op jit(solution)/shard_map/all_to_all | solution.py:177
  30.5 1.2 copy.43
  31.6 14.8 %all-to-all-start.1 = ((bf16[16,4,72,128]{3,2,1,0:T(8,128)(2,1)}), bf16[16,4,72,128]{3,2,1,0:T(8,128)(2,1)S(1)}, u32[]{:S(2)}, u32[]{:S(2)}) async-start(bf16[16,4,72,128]{3,2,1,0:T(8,128)(2,1)} %copy.43), calls=%async_computation.1 | async-start | bytes 2359296 | tf_op jit(solution)/shard_map/all_to_all | solution.py:177
  47.1 34.2 %all-to-all-done.1 = bf16[16,4,72,128]{3,2,1,0:T(8,128)(2,1)S(1)} async-done(((bf16[16,4,72,128]{3,2,1,0:T(8,128)(2,1)}), bf16[16,4,72,128]{3,2,1,0:T(8,128)(2,1)S(1)}, u32[]{:S(2)}, u32[]{:S(2)}) %all-to-all-start.1) | async-done | bytes 1179680 | tf_op jit(solution)/shard_map/all_to_all | solution.py:177
  81.3 3.1 %multiply_convert_fusion = (bf16[4,72,256]{2,1,0:T(8,128)(2,1)S(1)}, f32[4,72,256]{2,1,0:T(8,128)S(1)}) fusion(bf16[16,4,72,128]{3,2,1,0:T(8,128)(2,1)S(1)} %all-to-all-done.1, bf16[16,4,128,256]{3,2,1,0:T(8,128)(2,1)} %bitcast.299), kind=kOutput, calls=%fused_computation.218 | convolution fusion | flops 302358528 | bytes 5816320 | tf_op jit(solution)/shard_map/gbnk,gbkf->bnf/dot_general | solution.py:225
  85.4 28.0 %shard_map.92 = bf16[16,360,256]{2,1,0:T(8,128)(2,1)} custom-call(bf16[360,256]{1,0:T(8,128)(2,1)} %pad_maximum_fusion.4.x_ref), custom_call_target="tpu_custom_call" | custom-call | bytes 80000000 | tf_op jit(solution)/shard_map/pallas_call | solution.py:163
  113.4 1.9 slice.413
  116.7 1.1 fusion.93
  117.8 1.3 fusion.95
  119.0 1.2 fusion.94
  120.3 0.9 slice_bitcast_fusion.2
  121.1 0.9 reshape.124
  122.3 2.8 %stack.159 = bf16[27,128]{1,0:T(8,128)(2,1)S(1)} concatenate(bf16[1,128]{1,0:T(2,128)(2,1)S(1)} %bitcast.323, bf16[1,128]{1,0:T(2,128)(2,1)} %bitcast.328, bf16[1,128]{1,0:T(2,128)(2,1)} %bitcast.329, bf16[1,128]{1,0:T(2,128)(2,1)} %bitcast.330, bf16[1,128]{1,0:T(2,128)(2,1)S(1)} %bitcast.324, bf16[1,128]{1,0:T(2,128)(2,1)} %bitcast.331, bf16[1,128]{1,0:T(2,128)(2,1)} %bitcast.332, ...), dimensions={0} | concatenate | bytes 13824 | tf_op jit(solution)/shard_map/stack | solution.py:290
  125.1 1.9 copy.78
  127.1 1.8 reshape.125
  128.9 1.6 copy.52
  130.5 4.4 %all-to-all-start.3 = ((bf16[16,36,128]{2,1,0:T(8,128)(2,1)}), bf16[16,36,128]{2,1,0:T(8,128)(2,1)}, u32[]{:S(2)}, u32[]{:S(2)}) async-start(bf16[16,36,128]{2,1,0:T(8,128)(2,1)} %copy.52), calls=%async_computation.3 | async-start | bytes 327680 | tf_op jit(solution)/shard_map/all_to_all | solution.py:177
  134.9 4.3 %fusion.105 = bf16[72,16,128]{2,0,1:T(8,128)(2,1)S(1)} fusion(f32[128]{0:T(128)} %copy-done.17, bf16[16,72,128]{2,1,0:T(8,128)(2,1)S(1)} %copy-done.3, f32[128]{0:T(128)} %copy-done.18, f32[128]{0:T(128)} %copy-done.19, f32[128]{0:T(128)} %copy-done.20, f32[128]{0:T(128)} %copy-done.21, f32[128]{0:T(128)} %copy-done.22, f32[128]{0:T(128)} %copy-done.23, ...), kind=kLoop, calls=%fused_computation.223 | loop fusion | flops 12238848 | bytes 1488384 | tf_op jit(solution)/shard_map/transpose | solution.py:275
  140.1 2.4 %fusion.10 = bf16[4,128,256]{2,1,0:T(8,128)(2,1)S(1)} fusion(bf16[16,4,72,256]{3,2,1,0:T(8,128)(2,1)} %bitcast.303, bf16[16,1,72,128]{3,2,0,1:T(8,128)(2,1)S(1)} %fusion.102, bf16[16,1,72,128]{3,2,0,1:T(8,128)(2,1)S(1)} %fusion.103, bf16[16,1,72,128]{3,2,0,1:T(8,128)(2,1)S(1)} %fusion.104, bf16[16,1,72,128]{3,2,0,1:T(8,128)(2,1)S(1)} %bitcast.298), kind=kOutput, calls=%fused_computation.87 | convolution fusion | flops 303890432 | bytes 3801088 | tf_op jit(solution)/shard_map/xbnk,xbnf->bkf/dot_general | solution.py:257
  142.5 2.1 all-to-all-done.3
  144.5 6.5 %all-to-all-start.2 = ((bf16[8,162,128]{2,1,0:T(8,128)(2,1)}), bf16[8,162,128]{2,1,0:T(8,128)(2,1)S(1)}, u32[]{:S(2)}, u32[]{:S(2)}) async-start(bf16[8,162,128]{2,1,0:T(8,128)(2,1)} %pad_maximum_fusion.3), calls=%async_computation.2 | async-start | bytes 688128 | tf_op jit(solution)/shard_map/all_to_all | solution.py:177
  151.0 1.3 convolution_bitcast_fusion.4
  152.3 1.4 fusion.18
  154.6 32.3 %shard_map.93 = bf16[32,19,256]{2,1,0:T(8,128)(2,1)} custom-call(bf16[32,19,256]{2,1,0:T(8,128)(2,1)} %pad_maximum_fusion.1.x_ref), custom_call_target="tpu_custom_call" | custom-call | bytes 80000000 | tf_op jit(solution)/shard_map/pallas_call | solution.py:72
  186.8 0.9 slice.453
  188.4 18.9 %shard_map.94 = bf16[16,64,256]{2,1,0:T(8,128)(2,1)} custom-call(bf16[64,256]{1,0:T(8,128)(2,1)} %reshape.127.x_ref), custom_call_target="tpu_custom_call" | custom-call | bytes 80000000 | tf_op jit(solution)/shard_map/pallas_call | solution.py:163
  207.3 0.9 multiply_reduce_fusion
  208.9 1.8 convert_multiply_fusion.58
  210.7 1.1 convert_multiply_fusion.33
  211.8 0.9 copy.49
  (108 shorter events, 11.3 us)
Async XLA Ops:
  7.2 77.2 %copy-start = (bf16[4,256,256]{2,1,0:T(8,128)(2,1)S(1)}, bf16[4,256,256]{2,1,0:T(8,128)(2,1)}, u32[]{:S(2)}) copy-start(bf16[4,256,256]{2,1,0:T(8,128)(2,1)} %param.8) | copy-start | bytes 1572868
  7.2 74.1 %all-gather.3.cloned.1.call-start = ((), (), s32[]{:S(2)}) async-start(), calls=%async_computation.4 | async-start | bytes 4456448 | tf_op jit(solution)/shard_map/all_gather | solution.py:205
  10.5 17.8 %all-to-all-start = ((bf16[8,162,128]{2,1,0:T(8,128)(2,1)}), bf16[8,162,128]{2,1,0:T(8,128)(2,1)S(1)}, u32[]{:S(2)}, u32[]{:S(2)}) async-start(bf16[8,162,128]{2,1,0:T(8,128)(2,1)} %pad_maximum_fusion.2), calls=%async_computation | async-start | bytes 688128 | tf_op jit(solution)/shard_map/all_to_all | solution.py:177
  18.2 11.5 %copy-start.7 = (f32[128]{0:T(128)}, f32[128]{0:T(128)S(1)}, u32[]{:S(2)}) copy-start(f32[128]{0:T(128)S(1)} %get-tuple-element.67) | copy-start | bytes 1540
  18.2 11.5 %copy-start.9 = (f32[128]{0:T(128)}, f32[128]{0:T(128)S(1)}, u32[]{:S(2)}) copy-start(f32[128]{0:T(128)S(1)} %get-tuple-element.68) | copy-start | bytes 1540
  18.2 11.5 %copy-start.10 = (f32[128]{0:T(128)}, f32[128]{0:T(128)S(1)}, u32[]{:S(2)}) copy-start(f32[128]{0:T(128)S(1)} %get-tuple-element.69) | copy-start | bytes 1540
  18.2 11.5 %copy-start.11 = (f32[128]{0:T(128)}, f32[128]{0:T(128)S(1)}, u32[]{:S(2)}) copy-start(f32[128]{0:T(128)S(1)} %get-tuple-element.70) | copy-start | bytes 1540
  18.2 11.5 %copy-start.12 = (f32[128]{0:T(128)}, f32[128]{0:T(128)S(1)}, u32[]{:S(2)}) copy-start(f32[128]{0:T(128)S(1)} %get-tuple-element.71) | copy-start | bytes 1540
  18.2 11.5 %copy-start.13 = (f32[128]{0:T(128)}, f32[128]{0:T(128)S(1)}, u32[]{:S(2)}) copy-start(f32[128]{0:T(128)S(1)} %get-tuple-element.72) | copy-start | bytes 1540
  18.2 11.5 %copy-start.14 = (f32[128]{0:T(128)}, f32[128]{0:T(128)S(1)}, u32[]{:S(2)}) copy-start(f32[128]{0:T(128)S(1)} %get-tuple-element.73) | copy-start | bytes 1540
  18.2 11.5 %copy-start.15 = (f32[128]{0:T(128)}, f32[128]{0:T(128)S(1)}, u32[]{:S(2)}) copy-start(f32[128]{0:T(128)S(1)} %get-tuple-element.74) | copy-start | bytes 1540
  18.3 11.2 %copy-start.17 = (f32[128]{0:T(128)}, f32[128]{0:T(128)S(1)}, u32[]{:S(2)}) copy-start(f32[128]{0:T(128)S(1)} %get-tuple-element.49) | copy-start | bytes 1540
  18.3 11.2 %copy-start.18 = (f32[128]{0:T(128)}, f32[128]{0:T(128)S(1)}, u32[]{:S(2)}) copy-start(f32[128]{0:T(128)S(1)} %get-tuple-element.50) | copy-start | bytes 1540
  18.3 11.2 %copy-start.19 = (f32[128]{0:T(128)}, f32[128]{0:T(128)S(1)}, u32[]{:S(2)}) copy-start(f32[128]{0:T(128)S(1)} %get-tuple-element.51) | copy-start | bytes 1540
  18.3 11.2 %copy-start.20 = (f32[128]{0:T(128)}, f32[128]{0:T(128)S(1)}, u32[]{:S(2)}) copy-start(f32[128]{0:T(128)S(1)} %get-tuple-element.52) | copy-start | bytes 1540
  18.3 11.2 %copy-start.21 = (f32[128]{0:T(128)}, f32[128]{0:T(128)S(1)}, u32[]{:S(2)}) copy-start(f32[128]{0:T(128)S(1)} %get-tuple-element.53) | copy-start | bytes 1540
  18.3 11.2 %copy-start.22 = (f32[128]{0:T(128)}, f32[128]{0:T(128)S(1)}, u32[]{:S(2)}) copy-start(f32[128]{0:T(128)S(1)} %get-tuple-element.54) | copy-start | bytes 1540
  18.3 11.2 %copy-start.23 = (f32[128]{0:T(128)}, f32[128]{0:T(128)S(1)}, u32[]{:S(2)}) copy-start(f32[128]{0:T(128)S(1)} %get-tuple-element.55) | copy-start | bytes 1540
  18.4 11.2 %copy-start.24 = (f32[128]{0:T(128)}, f32[128]{0:T(128)S(1)}, u32[]{:S(2)}) copy-start(f32[128]{0:T(128)S(1)} %get-tuple-element.56) | copy-start | bytes 1540
  18.4 11.2 %copy-start.25 = (f32[128]{0:T(128)}, f32[128]{0:T(128)S(1)}, u32[]{:S(2)}) copy-start(f32[128]{0:T(128)S(1)} %get-tuple-element.57) | copy-start | bytes 1540
  18.4 11.2 %copy-start.26 = (f32[128]{0:T(128)}, f32[128]{0:T(128)S(1)}, u32[]{:S(2)}) copy-start(f32[128]{0:T(128)S(1)} %get-tuple-element.58) | copy-start | bytes 1540
  18.4 11.2 %copy-start.27 = (f32[128]{0:T(128)}, f32[128]{0:T(128)S(1)}, u32[]{:S(2)}) copy-start(f32[128]{0:T(128)S(1)} %get-tuple-element.59) | copy-start | bytes 1540
  18.4 11.2 %copy-start.28 = (f32[128]{0:T(128)}, f32[128]{0:T(128)S(1)}, u32[]{:S(2)}) copy-start(f32[128]{0:T(128)S(1)} %get-tuple-element.60) | copy-start | bytes 1540
  18.4 11.2 %copy-start.29 = (f32[128]{0:T(128)}, f32[128]{0:T(128)S(1)}, u32[]{:S(2)}) copy-start(f32[128]{0:T(128)S(1)} %get-tuple-element.61) | copy-start | bytes 1540
  18.4 11.2 %copy-start.30 = (f32[128]{0:T(128)}, f32[128]{0:T(128)S(1)}, u32[]{:S(2)}) copy-start(f32[128]{0:T(128)S(1)} %get-tuple-element.62) | copy-start | bytes 1540
  18.4 11.2 %copy-start.31 = (f32[128]{0:T(128)}, f32[128]{0:T(128)S(1)}, u32[]{:S(2)}) copy-start(f32[128]{0:T(128)S(1)} %get-tuple-element.63) | copy-start | bytes 1540
  18.5 11.3 %copy-start.16 = (f32[128]{0:T(128)}, f32[128]{0:T(128)S(1)}, u32[]{:S(2)}) copy-start(f32[128]{0:T(128)S(1)} %get-tuple-element.48) | copy-start | bytes 1540
  31.6 49.6 %all-to-all-start.1 = ((bf16[16,4,72,128]{3,2,1,0:T(8,128)(2,1)}), bf16[16,4,72,128]{3,2,1,0:T(8,128)(2,1)S(1)}, u32[]{:S(2)}, u32[]{:S(2)}) async-start(bf16[16,4,72,128]{3,2,1,0:T(8,128)(2,1)} %copy.43), calls=%async_computation.1 | async-start | bytes 2359296 | tf_op jit(solution)/shard_map/all_to_all | solution.py:177
  122.0 12.9 %copy-start.8 = (f32[128]{0:T(128)S(1)}, f32[128]{0:T(128)}, u32[]{:S(2)}) copy-start(f32[128]{0:T(128)} %copy-done.7) | copy-start | bytes 1540
  122.2 12.7 %copy-start.3 = (bf16[16,72,128]{2,1,0:T(8,128)(2,1)S(1)}, bf16[16,72,128]{2,1,0:T(8,128)(2,1)}, u32[]{:S(2)}) copy-start(bf16[16,72,128]{2,1,0:T(8,128)(2,1)} %get-tuple-element.36) | copy-start | bytes 884740
  130.5 14.0 %all-to-all-start.3 = ((bf16[16,36,128]{2,1,0:T(8,128)(2,1)}), bf16[16,36,128]{2,1,0:T(8,128)(2,1)}, u32[]{:S(2)}, u32[]{:S(2)}) async-start(bf16[16,36,128]{2,1,0:T(8,128)(2,1)} %copy.52), calls=%async_computation.3 | async-start | bytes 327680 | tf_op jit(solution)/shard_map/all_to_all | solution.py:177
  144.5 67.3 %all-to-all-start.2 = ((bf16[8,162,128]{2,1,0:T(8,128)(2,1)}), bf16[8,162,128]{2,1,0:T(8,128)(2,1)S(1)}, u32[]{:S(2)}, u32[]{:S(2)}) async-start(bf16[8,162,128]{2,1,0:T(8,128)(2,1)} %pad_maximum_fusion.3), calls=%async_computation.2 | async-start | bytes 688128 | tf_op jit(solution)/shard_map/all_to_all | solution.py:177
  (8 other events, 54.5 us)
Sparse Core Ops, SparseCore 0:
  10.1 66.6 all-gather.2

commit v3 on v2

--- a/solution.py
+++ b/solution.py
@@ -14,81 +14,102 @@
 MESH = pl.DeviceIdType.MESH
 
 
-def reduce_kernel(rows, dps, x_ref, out_ref, landed, total, gathered, send1, recv1, send2, recv2):
-    count = rows * dps
-    me = lax.axis_index("row") * dps + lax.axis_index("dp")
-
-    def device(step):
-        peer = lax.rem(me + step, count)
-        return peer, {"row": lax.div(peer, dps), "dp": lax.rem(peer, dps)}
+def reduce_kernel(rows, dps, x_ref, out_ref, land1, part, land2, total, held, send, recv):
+    row, dp = lax.axis_index("row"), lax.axis_index("dp")
+
+    def dp_peer(step):
+        return lax.rem(dp + step, dps)
+
+    def row_peer(step):
+        return lax.rem(row + step, rows)
 
     barrier = pltpu.get_barrier_semaphore()
-    for step in range(1, count):
-        pl.semaphore_signal(barrier, inc=1, device_id=device(step)[1], device_id_type=MESH)
-    pl.semaphore_wait(barrier, count - 1)
-
-    def scatter(step):
-        peer, where = device(step)
+    for step in range(1, dps):
+        where = {"dp": dp_peer(step)}
+        pl.semaphore_signal(barrier, inc=1, device_id=where, device_id_type=MESH)
+    for step in range(1, rows):
+        where = {"row": row_peer(step)}
+        pl.semaphore_signal(barrier, inc=1, device_id=where, device_id_type=MESH)
+    pl.semaphore_wait(barrier, rows + dps - 2)
+
+    def copy(level, step):
+        if level == 0:
+            where, source, landing = {"dp": dp_peer(step)}, x_ref.at[dp_peer(step)], land1.at[step]
+        elif level == 1:
+            where, source, landing = {"row": row_peer(step)}, part.at[row_peer(step)], land2.at[step]
+        elif level == 2:
+            where, source, landing = {"row": row_peer(step)}, total, held.at[dp, row]
+        else:
+            where, source, landing = {"dp": dp_peer(step)}, held.at[dp], held.at[dp]
         return pltpu.make_async_remote_copy(
-            src_ref=x_ref.at[peer],
-            dst_ref=landed.at[step],
-            send_sem=send1.at[step],
-            recv_sem=recv1.at[step],
+            src_ref=source,
+            dst_ref=landing,
+            send_sem=send.at[level, step],
+            recv_sem=recv.at[level, step],
             device_id=where,
             device_id_type=MESH,
         )
 
-    def gather(step):
-        _, where = device(step)
-        return pltpu.make_async_remote_copy(
-            src_ref=total,
-            dst_ref=gathered.at[me],
-            send_sem=send2.at[step],
-            recv_sem=recv2.at[step],
-            device_id=where,
-            device_id_type=MESH,
-        )
-
-    for step in range(1, count):
-        scatter(step).start()
-    summed = x_ref[me].astype(jnp.float32)
-    for step in range(1, count):
-        scatter(step).wait_recv()
-        summed = summed + landed[step].astype(jnp.float32)
+    for step in range(1, dps):
+        copy(0, step).start()
+    summed = x_ref[dp].astype(jnp.float32)
+    for step in range(1, dps):
+        copy(0, step).wait_recv()
+        summed = summed + land1[step].astype(jnp.float32)
+    part[...] = summed.astype(part.dtype)
+    for step in range(1, rows):
+        copy(1, step).start()
+    summed = part[row].astype(jnp.float32)
+    for step in range(1, rows):
+        copy(1, step).wait_recv()
+        summed = summed + land2[step].astype(jnp.float32)
     total[...] = summed.astype(total.dtype)
-    for step in range(1, count):
-        gather(step).start()
-    for step in range(1, count):
-        scatter(step).wait_send()
-    for step in range(1, count):
-        gather(step).wait()
-    out_ref[...] = gathered[...]
-    out_ref[me] = total[...]
+    held[dp, row] = total[...]
+    for step in range(1, rows):
+        copy(2, step).start()
+    for step in range(1, rows):
+        copy(2, step).wait_recv()
+    for step in range(1, dps):
+        copy(3, step).start()
+    for step in range(1, dps):
+        copy(0, step).wait_send()
+    for level in (1, 2):
+        for step in range(1, rows):
+            copy(level, step).wait_send()
+    for step in range(1, dps):
+        copy(3, step).wait()
+    out_ref[...] = held[...]
 
 
 def group_sum(value, collective_id):
-    rows, dps = lax.axis_size("row"), lax.axis_size("dp")
-    count, height, width = value.shape
+    dps, rows, height, width = value.shape
+    sems = pltpu.SemaphoreType.DMA((4, max(rows, dps)))
     return pl.pallas_call(
         functools.partial(reduce_kernel, rows, dps),
         out_shape=jax.ShapeDtypeStruct(value.shape, value.dtype),
         in_specs=[pl.BlockSpec(memory_space=pltpu.VMEM)],
         out_specs=pl.BlockSpec(memory_space=pltpu.VMEM),
         scratch_shapes=[
-            pltpu.VMEM((count, height, width), value.dtype),
+            pltpu.VMEM(value.shape, value.dtype),
+            pltpu.VMEM((rows, height, width), value.dtype),
+            pltpu.VMEM((rows, height, width), value.dtype),
             pltpu.VMEM((height, width), value.dtype),
-            pltpu.VMEM((count, height, width), value.dtype),
-            pltpu.SemaphoreType.DMA((count,)),
-            pltpu.SemaphoreType.DMA((count,)),
-            pltpu.SemaphoreType.DMA((count,)),
-            pltpu.SemaphoreType.DMA((count,)),
+            pltpu.VMEM(value.shape, value.dtype),
+            sems,
+            sems,
         ],
         compiler_params=pltpu.CompilerParams(collective_id=collective_id, has_side_effects=True),
         cost_estimate=pl.CostEstimate(flops=0, bytes_accessed=80_000_000, transcendentals=0),
     )(value)
 
 
-def ring_kernel(chips, cut, x_ref, out_ref, held, ring_send, ring_recv, pair_send, pair_recv):
+def ring_kernel(chips, cut, deal, *refs):
+    if deal:
+        x_ref, y_ref, out_ref, dealt_ref, held, dealt = refs[:6]
+        deal_send, deal_recv, twin_send, twin_recv = refs[6:10]
+    else:
+        x_ref, out_ref, held = refs[:3]
+    ring_send, ring_recv, pair_send, pair_recv = refs[-4:]
     me = lax.axis_index("chan")
     chip, core = lax.div(me, 2), lax.rem(me, 2)
     hops = chips // 2
@@ -104,9 +125,35 @@
     targets = (ahead, behind)
 
     barrier = pltpu.get_barrier_semaphore()
-    for where in (ahead, behind, twin):
+    greeted = [twin]
+    if deal:
+        greeted += [{"chan": block(step)} for step in range(1, chips)]
+    else:
+        greeted += [ahead, behind]
+    for where in greeted:
         pl.semaphore_signal(barrier, inc=1, device_id=where, device_id_type=MESH)
-    pl.semaphore_wait(barrier, 3)
+    pl.semaphore_wait(barrier, len(greeted))
+
+    def direct(step):
+        return pltpu.make_async_remote_copy(
+            src_ref=y_ref.at[lax.rem(chip + step, chips)],
+            dst_ref=dealt.at[me],
+            send_sem=deal_send.at[step],
+            recv_sem=deal_recv.at[step],
+            device_id={"chan": block(step)},
+            device_id_type=MESH,
+        )
+
+    def onward(step):
+        slot = block(-step)
+        return pltpu.make_async_remote_copy(
+            src_ref=y_ref.at[chip] if step == 0 else dealt.at[slot],
+            dst_ref=dealt.at[slot],
+            send_sem=twin_send.at[step],
+            recv_sem=twin_recv.at[step],
+            device_id=twin,
+            device_id_type=MESH,
+        )
 
     def ring(way, hop):
         away = 1 - hop if way == 0 else hop - 1
@@ -140,7 +187,15 @@
     for way in range(2):
         ring(way, 1).start()
     pair(0, 0).start()
+    if deal:
+        for step in range(1, chips):
+            direct(step).start()
+        onward(0).start()
     for hop in range(1, hops + 1):
+        if deal and hop == hops:
+            for step in range(1, chips):
+                direct(step).wait_recv()
+                onward(step).start()
         for way in range(2):
             ring(way, hop).wait_recv()
             if hop < hops:
@@ -154,23 +209,37 @@
         pair(way, hop).wait()
     out_ref[...] = held[...]
     out_ref[me] = x_ref[...]
-
-
-def ring_gather(value, cut, collective_id):
+    if deal:
+        for step in range(1, chips):
+            direct(step).wait_send()
+        for step in range(chips):
+            onward(step).wait()
+        dealt_ref[...] = dealt[...]
+        dealt_ref[me] = y_ref[chip]
+
+
+def ring_gather(value, cut, collective_id, dealt=None):
     shares = lax.axis_size("chan")
     chips = shares // 2
-    sems = pltpu.SemaphoreType.DMA((2, chips // 2 + 1))
-    return pl.pallas_call(
-        functools.partial(ring_kernel, chips, cut),
-        out_shape=jax.ShapeDtypeStruct((shares,) + value.shape, value.dtype),
-        in_specs=[pl.BlockSpec(memory_space=pltpu.VMEM)],
-        out_specs=pl.BlockSpec(memory_space=pltpu.VMEM),
-        scratch_shapes=[
-            pltpu.VMEM((shares,) + value.shape, value.dtype), sems, sems, sems, sems
-        ],
+    operands = [value] if dealt is None else [value, dealt]
+    gathered = [(shares,) + value.shape]
+    if dealt is not None:
+        gathered.append((shares,) + dealt.shape[1:])
+    scratch = [pltpu.VMEM(shape, value.dtype) for shape in gathered]
+    if dealt is not None:
+        scratch += [pltpu.SemaphoreType.DMA((chips,))] * 4
+    scratch += [pltpu.SemaphoreType.DMA((2, chips // 2 + 1))] * 4
+    vmem = pl.BlockSpec(memory_space=pltpu.VMEM)
+    result = pl.pallas_call(
+        functools.partial(ring_kernel, chips, cut, dealt is not None),
+        out_shape=[jax.ShapeDtypeStruct(shape, value.dtype) for shape in gathered],
+        in_specs=[vmem] * len(operands),
+        out_specs=[vmem] * len(gathered),
+        scratch_shapes=scratch,
         compiler_params=pltpu.CompilerParams(collective_id=collective_id, has_side_effects=True),
         cost_estimate=pl.CostEstimate(flops=0, bytes_accessed=80_000_000, transcendentals=0),
-    )(value)
+    )(*operands)
+    return result[0] if dealt is None else result
 
 
 def exchange(value, axis):
@@ -202,7 +271,9 @@
     grid = landed[:, :area].reshape(rows, cols, channels).transpose(1, 0, 2)
     cot = jnp.concatenate([landed[:, area : area + half], landed[:, area + half :]], axis=2)
     cot = cot.reshape(rows, width)
-    full_point = lax.all_gather(point_weights, "chan", axis=0)
+    full_point = ring_gather(
+        point_weights.reshape(branches * channels, width), branches * channels // 2, 3
+    ).reshape((shares,) + point_weights.shape)
 
     pads = ((3 * col_step, 3 * col_step), (3 * row_step, 3 * row_step), (0, 0))
     padded = jnp.pad(grid, pads)
@@ -236,23 +307,21 @@
         "bnf,bfg->ng", activation, proj_weights, preferred_element_type=jnp.float32
     ).astype(jnp.bfloat16)
 
-    slices = shares // branches
-    part = width // slices
-    packed = activation.reshape(branches, 2, rows // 2, slices, part)
-    packed = packed.transpose(0, 3, 2, 1, 4).reshape(shares, rows // 2, 2 * part)
-    packed = exchange(packed, "chan")
+    chips = shares // 2
+    per = chips // branches
+    part, side = width // per, width // 2
+    pieces = activation.reshape(branches, rows, per, part).transpose(0, 2, 1, 3)
     sent = jnp.concatenate([pre_grad.reshape(branches * rows, width), cot], axis=0)
-    held = ring_gather(sent, sent.shape[0] // 32 * 16, 0)
+    held, slices = ring_gather(
+        sent, sent.shape[0] // 32 * 16, 0, pieces.reshape(chips, rows, part)
+    )
     incoming = held[:, : branches * rows].reshape(shares, branches, rows, width)
-    full_cot = held[:, branches * rows :]
-    proj_part = jnp.zeros((part, width), jnp.float32)
-    for side in range(2):
-        proj_part = proj_part + jnp.einsum(
-            "xnf,xng->fg",
-            packed[:, :, side * part : (side + 1) * part],
-            full_cot[:, side * (rows // 2) : (side + 1) * (rows // 2)],
-            preferred_element_type=jnp.float32,
-        )
+    core = lax.rem(lax.axis_index("chan"), 2)
+    cot_side = lax.dynamic_slice_in_dim(held[:, branches * rows :], core * side, side, axis=2)
+    proj_part = jnp.einsum(
+        "xnf,xng->fg", slices, cot_side, preferred_element_type=jnp.float32
+    )
+    proj_part = jnp.concatenate([proj_part[: part // 2], proj_part[part // 2 :]], axis=1)
     group = bands * dps
     point_sum = jnp.einsum("xbnk,xbnf->bkf", spread, incoming, preferred_element_type=jnp.float32)
     spread_grad = jnp.einsum(
@@ -294,16 +363,19 @@
             [
                 point_sum.reshape(group, height, width),
                 depth_part[:, None],
-                proj_part.reshape(group, part // group, width),
+                proj_part.reshape(group, part // 2 // group, width),
             ],
             axis=1,
-        ).astype(jnp.bfloat16),
+        )
+        .astype(jnp.bfloat16)
+        .reshape(dps, bands, -1, width),
         1,
-    )
+    ).reshape(group, -1, width)
     grad_point = summed[:, :height].reshape(point_weights.shape).astype(jnp.float32) * weight_scale
     grad_depth = summed[:taps, height, :channels].reshape(depth_weights.shape)
     grad_depth = grad_depth.astype(jnp.float32) * weight_scale
-    grad_proj = ring_gather(summed[:, height + 1 :].reshape(part, width), part // 2, 2)
+    grad_proj = ring_gather(summed[:, height + 1 :].reshape(part // 2, width), part // 4, 2)
+    grad_proj = grad_proj.reshape(branches, per, 2, part // 2, 2, side).transpose(0, 1, 4, 3, 2, 5)
     grad_proj = grad_proj.reshape(branches, width, width).astype(jnp.float32) * weight_scale
     return (output, grad_input, grad_depth, grad_point, grad_proj)
 

time: 221 us -> 219 us (level)
  Pallas kernels: 79.2 us -> 136 us
  waiting for transfers between devices: 46.8 us -> 9.88 us
  between operations: 14.8 us -> 1.73 us
  starting transfers between devices: 33.3 us -> 27 us
  matrix products: 9.38 us -> 6.71 us
    pallas_call x2 -> x3, Pallas kernels: 46.9 us -> 110 us  [ring_gather(): pl.pallas_call(functools.partial(ring_kernel, chips, cut, dealt is not No...]
    all_to_all x4 -> x3, waiting for transfers between devices: 46.1 us -> 9.88 us  [exchange(): return lax.all_to_all(value, axis, split_axis=0, concat_axis=0, tiled=True)]
    all_to_all x4 -> x3, starting transfers between devices: 33.3 us -> 27 us  [exchange(): return lax.all_to_all(value, axis, split_axis=0, concat_axis=0, tiled=True)]
    reshape x6 -> x1, local copies, waits for them, and re-layouts: 6.92 us -> 0.63 us  [on_device(): summed[:, height + 1:].reshape(part // 2, width)]
    pallas_call x1, Pallas kernels: 32.3 us -> 26.1 us  [group_sum(): pl.pallas_call(functools.partial(reduce_kernel, rows, dps), out_shape=jax...]
    mul x0 -> x3, local copies, waits for them, and re-layouts: none -> 3.29 us  [on_device(): grad_proj.reshape(branches, width, width).astype(jnp.float32) * weight_scale]
    dot_general x2 -> x1, matrix products: 2.65 us -> 0.28 us  [on_device(): jnp.einsum('xnf,xng->fg', slices, cot_side, preferred_element_type=jnp.fl...]
  transfers between devices with their start and end apart: 5 -> 3, of which waited for: 3 -> 1; matrix products, arithmetic and copies ran while one was open for 11% -> 3% of each run, Pallas kernels for 23% -> 36%
where the time goes in v3:
time: 219 us; the launch traced here: 218 us
  Pallas kernels  136 us (62%)
  starting transfers between devices  27 us (12%)
  local copies, waits for them, and re-layouts  18.5 us (8%)
  other arithmetic  18.4 us (8%)
  waiting for transfers between devices  9.88 us (5%)
  matrix products  6.71 us (3%)
    pallas_call x3, Pallas kernels, ring_gather(): pl.pallas_call(functools.partial(ring_kernel, chips, cut, dealt is not No...  110 us
    all_to_all x3, starting transfers between devices, exchange(): return lax.all_to_all(value, axis, split_axis=0, concat_axis=0, tiled=True)  27 us
    pallas_call x1, Pallas kernels, group_sum(): pl.pallas_call(functools.partial(reduce_kernel, rows, dps), out_shape=jax...  26.1 us
    all_to_all x3, waiting for transfers between devices, exchange(): return lax.all_to_all(value, axis, split_axis=0, concat_axis=0, tiled=True)  9.88 us
    transpose x1, other arithmetic, on_device(): grad_in.astype(jnp.bfloat16).transpose(1, 0, 2)  6.24 us
  transfers between devices with their start and end apart: 3, of which 1 were waited for; matrix products, arithmetic and copies ran while one was open for 3% of the time, Pallas kernels for 36%

profile of v3, /device:TPU:1, one launch (start us, length us, event | category | flops | bytes accessed | tf_op | source)
XLA Modules:
  0.0 218.2 jit_solution(14389227447562582244)
XLA Ops:
  0.7 0.8 copy.40
  1.5 1.0 copy.39
  2.5 0.8 pad_maximum_fusion.2
  3.3 7.6 %all-to-all-start = ((bf16[8,162,128]{2,1,0:T(8,128)(2,1)}), bf16[8,162,128]{2,1,0:T(8,128)(2,1)S(1)}, u32[]{:S(2)}, u32[]{:S(2)}) async-start(bf16[8,162,128]{2,1,0:T(8,128)(2,1)} %pad_maximum_fusion.2), calls=%async_computation | async-start | bytes 688128 | tf_op jit(solution)/shard_map/all_to_all | solution.py:246
  11.2 9.9 %all-to-all-done = bf16[8,162,128]{2,1,0:T(8,128)(2,1)S(1)} async-done(((bf16[8,162,128]{2,1,0:T(8,128)(2,1)}), bf16[8,162,128]{2,1,0:T(8,128)(2,1)S(1)}, u32[]{:S(2)}, u32[]{:S(2)}) %all-to-all-start) | async-done | bytes 331808 | tf_op jit(solution)/shard_map/all_to_all | solution.py:246
  23.8 1.1 copy.42
  24.9 14.8 %all-to-all-start.1 = ((bf16[16,4,72,128]{3,2,1,0:T(8,128)(2,1)}), bf16[16,4,72,128]{3,2,1,0:T(8,128)(2,1)S(1)}, u32[]{:S(2)}, u32[]{:S(2)}) async-start(bf16[16,4,72,128]{3,2,1,0:T(8,128)(2,1)} %copy.42), calls=%async_computation.1 | async-start | bytes 2359296 | tf_op jit(solution)/shard_map/all_to_all | solution.py:246
  39.6 58.4 %shard_map.92 = bf16[16,512,256]{2,1,0:T(8,128)(2,1)} custom-call(bf16[512,256]{1,0:T(8,128)(2,1)} %bitcast.310), custom_call_target="tpu_custom_call" | custom-call | bytes 80000000 | tf_op jit(solution)/shard_map/pallas_call | solution.py:233
  98.2 3.1 %multiply_convert_fusion = (bf16[4,72,256]{2,1,0:T(8,128)(2,1)S(1)}, f32[4,72,256]{2,1,0:T(8,128)S(1)}) fusion(bf16[16,4,72,128]{3,2,1,0:T(8,128)(2,1)S(1)} %all-to-all-done.1, bf16[16,4,128,256]{3,2,1,0:T(8,128)(2,1)} %bitcast.294), kind=kOutput, calls=%fused_computation.214 | convolution fusion | flops 302358528 | bytes 5816320 | tf_op jit(solution)/shard_map/gbnk,gbkf->bnf/dot_general | solution.py:296
  101.3 0.8 fusion.16
  103.8 31.2 %shard_map.93 = (bf16[16,360,256]{2,1,0:T(8,128)(2,1)}, bf16[16,72,128]{2,1,0:T(8,128)(2,1)}) custom-call(bf16[360,256]{1,0:T(8,128)(2,1)} %pad_maximum_fusion.4.refs_0_, bf16[8,72,128]{2,1,0:T(8,128)(2,1)} %bitcast.306), custom_call_target="tpu_custom_call" | custom-call | bytes 80000000 | tf_op jit(solution)/shard_map/pallas_call | solution.py:233
  135.0 1.1 slice.451
  136.1 1.9 slice.417
  138.0 1.4 fusion.10
  139.4 0.8 fusion.4
  140.2 1.1 fusion.92
  141.4 1.2 fusion.93
  142.6 1.3 fusion.94
  143.9 0.8 reshape.136
  146.0 2.9 %stack.159 = bf16[27,128]{1,0:T(8,128)(2,1)S(1)} concatenate(bf16[1,128]{1,0:T(2,128)(2,1)} %bitcast.322, bf16[1,128]{1,0:T(2,128)(2,1)} %bitcast.336, bf16[1,128]{1,0:T(2,128)(2,1)} %bitcast.337, bf16[1,128]{1,0:T(2,128)(2,1)} %bitcast.338, bf16[1,128]{1,0:T(2,128)(2,1)} %bitcast.323, bf16[1,128]{1,0:T(2,128)(2,1)} %bitcast.339, bf16[1,128]{1,0:T(2,128)(2,1)} %bitcast.340, ...), dimensions={0} | concatenate | bytes 13824 | tf_op jit(solution)/shard_map/stack | solution.py:359
  148.9 1.8 pad_maximum_fusion.1.x_ref
  150.7 26.1 %shard_map.94 = bf16[4,8,19,256]{3,2,1,0:T(8,128)(2,1)} custom-call(bf16[4,8,19,256]{3,2,1,0:T(8,128)(2,1)} %pad_maximum_fusion.1.x_ref), custom_call_target="tpu_custom_call" | custom-call | bytes 80000000 | tf_op jit(solution)/shard_map/pallas_call | solution.py:87
  176.8 1.0 slice.504
  178.0 6.2 %fusion.103 = bf16[72,16,128]{2,0,1:T(8,128)(2,1)S(1)} fusion(f32[128]{0:T(128)S(1)} %copy-done.20, bf16[16,72,128]{2,1,0:T(8,128)(2,1)S(1)} %get-tuple-element.40, f32[128]{0:T(128)S(1)} %copy-done.22, f32[128]{0:T(128)S(1)} %copy-done.24, f32[128]{0:T(128)S(1)} %copy-done.26, f32[128]{0:T(128)S(1)} %copy-done.28, f32[128]{0:T(128)S(1)} %copy-done.30, ...), kind=kLoop, calls=%fused_computation.219 | loop fusion | flops 12238848 | bytes 1488384 | tf_op jit(solution)/shard_map/transpose | solution.py:344
  184.3 0.8 pad_maximum_fusion.3
  185.1 4.6 %all-to-all-start.2 = ((bf16[8,162,128]{2,1,0:T(8,128)(2,1)}), bf16[8,162,128]{2,1,0:T(8,128)(2,1)S(1)}, u32[]{:S(2)}, u32[]{:S(2)}) async-start(bf16[8,162,128]{2,1,0:T(8,128)(2,1)} %pad_maximum_fusion.3), calls=%async_computation.2 | async-start | bytes 688128 | tf_op jit(solution)/shard_map/all_to_all | solution.py:246
  191.0 20.4 %shard_map.95 = bf16[16,64,256]{2,1,0:T(8,128)(2,1)} custom-call(bf16[64,256]{1,0:T(8,128)(2,1)} %reshape.142.refs_0_), custom_call_target="tpu_custom_call" | custom-call | bytes 80000000 | tf_op jit(solution)/shard_map/pallas_call | solution.py:233
  211.3 1.2 convert_multiply_fusion.33
  213.0 0.9 copy.51
  214.0 1.8 mul.711
  215.8 0.9 convert_multiply_fusion.58
  216.7 0.9 copy.48
  (147 shorter events, 8.1 us)
Async XLA Ops:
  0.6 100.7 %copy-start = (bf16[4,256,256]{2,1,0:T(8,128)(2,1)S(1)}, bf16[4,256,256]{2,1,0:T(8,128)(2,1)}, u32[]{:S(2)}) copy-start(bf16[4,256,256]{2,1,0:T(8,128)(2,1)} %param.8) | copy-start | bytes 1572868
  3.3 17.8 %all-to-all-start = ((bf16[8,162,128]{2,1,0:T(8,128)(2,1)}), bf16[8,162,128]{2,1,0:T(8,128)(2,1)S(1)}, u32[]{:S(2)}, u32[]{:S(2)}) async-start(bf16[8,162,128]{2,1,0:T(8,128)(2,1)} %pad_maximum_fusion.2), calls=%async_computation | async-start | bytes 688128 | tf_op jit(solution)/shard_map/all_to_all | solution.py:246
  11.0 11.4 %copy-start.9 = (f32[128]{0:T(128)}, f32[128]{0:T(128)S(1)}, u32[]{:S(2)}) copy-start(f32[128]{0:T(128)S(1)} %get-tuple-element.79) | copy-start | bytes 1540
  11.0 11.4 %copy-start.11 = (f32[128]{0:T(128)}, f32[128]{0:T(128)S(1)}, u32[]{:S(2)}) copy-start(f32[128]{0:T(128)S(1)} %get-tuple-element.80) | copy-start | bytes 1540
  11.0 11.4 %copy-start.13 = (f32[128]{0:T(128)}, f32[128]{0:T(128)S(1)}, u32[]{:S(2)}) copy-start(f32[128]{0:T(128)S(1)} %get-tuple-element.81) | copy-start | bytes 1540
  11.0 11.4 %copy-start.15 = (f32[128]{0:T(128)}, f32[128]{0:T(128)S(1)}, u32[]{:S(2)}) copy-start(f32[128]{0:T(128)S(1)} %get-tuple-element.82) | copy-start | bytes 1540
  11.1 11.3 %copy-start.17 = (f32[128]{0:T(128)}, f32[128]{0:T(128)S(1)}, u32[]{:S(2)}) copy-start(f32[128]{0:T(128)S(1)} %get-tuple-element.56) | copy-start | bytes 1540
  24.9 73.3 %all-to-all-start.1 = ((bf16[16,4,72,128]{3,2,1,0:T(8,128)(2,1)}), bf16[16,4,72,128]{3,2,1,0:T(8,128)(2,1)S(1)}, u32[]{:S(2)}, u32[]{:S(2)}) async-start(bf16[16,4,72,128]{3,2,1,0:T(8,128)(2,1)} %copy.42), calls=%async_computation.1 | async-start | bytes 2359296 | tf_op jit(solution)/shard_map/all_to_all | solution.py:246
  145.4 32.3 %copy-start.10 = (f32[128]{0:T(128)S(1)}, f32[128]{0:T(128)}, u32[]{:S(2)}) copy-start(f32[128]{0:T(128)} %copy-done.9) | copy-start | bytes 1540
  145.4 32.4 %copy-start.12 = (f32[128]{0:T(128)S(1)}, f32[128]{0:T(128)}, u32[]{:S(2)}) copy-start(f32[128]{0:T(128)} %copy-done.11) | copy-start | bytes 1540
  145.4 32.4 %copy-start.14 = (f32[128]{0:T(128)S(1)}, f32[128]{0:T(128)}, u32[]{:S(2)}) copy-start(f32[128]{0:T(128)} %copy-done.13) | copy-start | bytes 1540
  145.4 32.4 %copy-start.16 = (f32[128]{0:T(128)S(1)}, f32[128]{0:T(128)}, u32[]{:S(2)}) copy-start(f32[128]{0:T(128)} %copy-done.15) | copy-start | bytes 1540
  145.4 32.4 %copy-start.18 = (f32[128]{0:T(128)S(1)}, f32[128]{0:T(128)}, u32[]{:S(2)}) copy-start(f32[128]{0:T(128)} %copy-done.17) | copy-start | bytes 1540
  145.4 32.4 %copy-start.20 = (f32[128]{0:T(128)S(1)}, f32[128]{0:T(128)}, u32[]{:S(2)}) copy-start(f32[128]{0:T(128)} %copy-done.19) | copy-start | bytes 1540
  145.5 32.4 %copy-start.22 = (f32[128]{0:T(128)S(1)}, f32[128]{0:T(128)}, u32[]{:S(2)}) copy-start(f32[128]{0:T(128)} %copy-done.21) | copy-start | bytes 1540
  145.5 32.4 %copy-start.24 = (f32[128]{0:T(128)S(1)}, f32[128]{0:T(128)}, u32[]{:S(2)}) copy-start(f32[128]{0:T(128)} %copy-done.23) | copy-start | bytes 1540
  145.5 32.4 %copy-start.26 = (f32[128]{0:T(128)S(1)}, f32[128]{0:T(128)}, u32[]{:S(2)}) copy-start(f32[128]{0:T(128)} %copy-done.25) | copy-start | bytes 1540
  145.5 32.4 %copy-start.28 = (f32[128]{0:T(128)S(1)}, f32[128]{0:T(128)}, u32[]{:S(2)}) copy-start(f32[128]{0:T(128)} %copy-done.27) | copy-start | bytes 1540
  145.5 32.4 %copy-start.30 = (f32[128]{0:T(128)S(1)}, f32[128]{0:T(128)}, u32[]{:S(2)}) copy-start(f32[128]{0:T(128)} %copy-done.29) | copy-start | bytes 1540
  145.5 32.4 %copy-start.32 = (f32[128]{0:T(128)S(1)}, f32[128]{0:T(128)}, u32[]{:S(2)}) copy-start(f32[128]{0:T(128)} %copy-done.31) | copy-start | bytes 1540
  145.5 32.4 %copy-start.34 = (f32[128]{0:T(128)S(1)}, f32[128]{0:T(128)}, u32[]{:S(2)}) copy-start(f32[128]{0:T(128)} %copy-done.33) | copy-start | bytes 1540
  145.5 32.4 %copy-start.36 = (f32[128]{0:T(128)S(1)}, f32[128]{0:T(128)}, u32[]{:S(2)}) copy-start(f32[128]{0:T(128)} %copy-done.35) | copy-start | bytes 1540
  145.5 32.4 %copy-start.38 = (f32[128]{0:T(128)S(1)}, f32[128]{0:T(128)}, u32[]{:S(2)}) copy-start(f32[128]{0:T(128)} %copy-done.37) | copy-start | bytes 1540
  145.5 32.4 %copy-start.40 = (f32[128]{0:T(128)S(1)}, f32[128]{0:T(128)}, u32[]{:S(2)}) copy-start(f32[128]{0:T(128)} %copy-done.39) | copy-start | bytes 1540
  145.8 32.1 %copy-start.42 = (f32[128]{0:T(128)S(1)}, f32[128]{0:T(128)}, u32[]{:S(2)}) copy-start(f32[128]{0:T(128)} %copy-done.41) | copy-start | bytes 1540
  145.9 32.1 %copy-start.44 = (f32[128]{0:T(128)S(1)}, f32[128]{0:T(128)}, u32[]{:S(2)}) copy-start(f32[128]{0:T(128)} %copy-done.43) | copy-start | bytes 1540
  145.9 32.1 %copy-start.46 = (f32[128]{0:T(128)S(1)}, f32[128]{0:T(128)}, u32[]{:S(2)}) copy-start(f32[128]{0:T(128)} %copy-done.45) | copy-start | bytes 1540
  145.9 32.1 %copy-start.48 = (f32[128]{0:T(128)S(1)}, f32[128]{0:T(128)}, u32[]{:S(2)}) copy-start(f32[128]{0:T(128)} %copy-done.47) | copy-start | bytes 1540
  145.9 32.1 %copy-start.50 = (f32[128]{0:T(128)S(1)}, f32[128]{0:T(128)}, u32[]{:S(2)}) copy-start(f32[128]{0:T(128)} %copy-done.49) | copy-start | bytes 1540
  145.9 32.1 %copy-start.52 = (f32[128]{0:T(128)S(1)}, f32[128]{0:T(128)}, u32[]{:S(2)}) copy-start(f32[128]{0:T(128)} %copy-done.51) | copy-start | bytes 1540
  145.9 32.1 %copy-start.54 = (f32[128]{0:T(128)S(1)}, f32[128]{0:T(128)}, u32[]{:S(2)}) copy-start(f32[128]{0:T(128)} %copy-done.53) | copy-start | bytes 1540
  185.1 31.6 %all-to-all-start.2 = ((bf16[8,162,128]{2,1,0:T(8,128)(2,1)}), bf16[8,162,128]{2,1,0:T(8,128)(2,1)S(1)}, u32[]{:S(2)}, u32[]{:S(2)}) async-start(bf16[8,162,128]{2,1,0:T(8,128)(2,1)} %pad_maximum_fusion.3), calls=%async_computation.2 | async-start | bytes 688128 | tf_op jit(solution)/shard_map/all_to_all | solution.py:246
  (26 other events, 234.1 us)

commit v4 on v1

v4 whole, which is shorter than its diff:
```python
import functools
import math

import jax
import jax.numpy as jnp
from jax import lax
from jax.experimental import pallas as pl
from jax.experimental.pallas import tpu as pltpu
from jax.sharding import PartitionSpec as P

BASE_DILATION = 12
ROW_CLASSES = 2
COL_CLASSES = 4
MESH = pl.DeviceIdType.MESH


def remote(source, landing, send_sem, recv_sem, where):
    return pltpu.make_async_remote_copy(
        src_ref=source,
        dst_ref=landing,
        send_sem=send_sem,
        recv_sem=recv_sem,
        device_id=where,
        device_id_type=MESH,
    )


def greet(places):
    barrier = pltpu.get_barrier_semaphore()
    for where in places:
        pl.semaphore_signal(barrier, inc=1, device_id=where, device_id_type=MESH)
    pl.semaphore_wait(barrier, len(places))


class Levels:
    def __init__(self, rows, dps, x_ref, land1, part, land2, total, held, send, recv):
        self.rows, self.dps, self.x_ref = rows, dps, x_ref
        self.land1, self.part, self.land2, self.total, self.held = land1, part, land2, total, held
        self.send, self.recv = send, recv
        self.row, self.dp = lax.axis_index("row"), lax.axis_index("dp")

    def dp_peer(self, step):
        return lax.rem(self.dp + step, self.dps)

    def row_peer(self, step):
        return lax.rem(self.row + step, self.rows)

    def places(self):
        found = [{"dp": self.dp_peer(step)} for step in range(1, self.dps)]
        return found + [{"row": self.row_peer(step)} for step in range(1, self.rows)]

    def steps(self, level):
        return range(1, self.dps if level in (0, 3) else self.rows)

    def copy(self, level, step):
        if level in (0, 3):
            peer, where = self.dp_peer(step), {"dp": self.dp_peer(step)}
        else:
            peer, where = self.row_peer(step), {"row": self.row_peer(step)}
        source, landing = (
            lambda: (self.x_ref.at[peer], self.land1.at[step]),
            lambda: (self.part.at[peer], self.land2.at[step]),
            lambda: (self.total, self.held.at[self.dp, self.row]),
            lambda: (self.held.at[self.dp], self.held.at[self.dp]),
        )[level]()
        return remote(source, landing, self.send.at[level, step], self.recv.at[level, step], where)

    def start(self, level):
        for step in self.steps(level):
            self.copy(level, step).start()

    def arrive(self, level):
        if level == 0:
            summed = self.x_ref[self.dp].astype(jnp.float32)
        elif level == 1:
            summed = self.part[self.row].astype(jnp.float32)
        for step in self.steps(level):
            self.copy(level, step).wait_recv()
            if level == 0:
                summed = summed + self.land1[step].astype(jnp.float32)
            elif level == 1:
                summed = summed + self.land2[step].astype(jnp.float32)
        if level == 0:
            self.part[...] = summed.astype(self.part.dtype)
        elif level == 1:
            self.total[...] = summed.astype(self.total.dtype)
            self.held[self.dp, self.row] = self.total[...]
        if level < 3:
            self.start(level + 1)

    def finish(self):
        for level in range(4):
            for step in self.steps(level):
                self.copy(level, step).wait_send()


class Ring:
    def __init__(self, chips, cut, x_ref, held, ring_send, ring_recv, pair_send, pair_recv):
        self.chips, self.hops, self.x_ref, self.held = chips, chips // 2, x_ref, held
        self.sems = ring_send, ring_recv, pair_send, pair_recv
        self.me = lax.axis_index("chan")
        self.chip, self.core = lax.div(self.me, 2), lax.rem(self.me, 2)
        self.spans = (pl.ds(0, cut), pl.ds(cut, x_ref.shape[0] - cut))
        self.ways = ({"chan": self.block(1)}, {"chan": self.block(-1)})
        self.twin = {"chan": self.chip * 2 + 1 - self.core}
        self.pairs = []

    def block(self, away):
        return lax.rem(self.chip + away + self.chips, self.chips) * 2 + self.core

    def refs(self, own, away, way, hop):
        source, landing = (self.x_ref if own else self.held.at[away]), self.held.at[away]
        if hop == self.hops:
            source, landing = source.at[self.spans[way]], landing.at[self.spans[way]]
        return source, landing

    def ring(self, way, hop):
        away = self.block(1 - hop if way == 0 else hop - 1)
        source, landing = self.refs(hop == 1, away, way, hop)
        send, recv, _, _ = self.sems
        return remote(source, landing, send.at[way, hop], recv.at[way, hop], self.ways[way])

    def pair(self, way, hop):
        away = self.block(-hop if way == 0 else hop)
        source, landing = self.refs(hop == 0, away, way, hop)
        _, _, send, recv = self.sems
        return remote(source, landing, send.at[way, hop], recv.at[way, hop], self.twin)

    def start(self):
        for way in range(2):
            self.ring(way, 1).start()
        self.pair(0, 0).start()
        self.pairs.append((0, 0))

    def advance(self, hop):
        for way in range(2):
            self.ring(way, hop).wait_recv()
            if hop < self.hops:
                self.ring(way, hop + 1).start()
            self.pair(way, hop).start()
            self.pairs.append((way, hop))

    def finish(self):
        for hop in range(1, self.hops + 1):
            for way in range(2):
                self.ring(way, hop).wait_send()
        for way, hop in self.pairs:
            self.pair(way, hop).wait()


def sum_kernel(rows, dps, chips, x_ref, y_ref, out_ref, all_ref, *scratch):
    main = Levels(rows, dps, x_ref, *scratch[:5], *scratch[10:12])
    side = Levels(rows, dps, y_ref, *scratch[5:10], *scratch[12:14])
    gathered = scratch[14]
    ring = Ring(chips, dps // 2, side.held, gathered, *scratch[15:])
    greet(main.places() + [*ring.ways, ring.twin])
    side.start(0)
    main.start(0)
    for level in range(3):
        side.arrive(level)
        main.arrive(level)
    side.arrive(3)
    ring.start()
    for hop in range(1, ring.hops + 1):
        ring.advance(hop)
    main.arrive(3)
    out_ref[...] = main.held[...]
    main.finish()
    side.finish()
    ring.finish()
    all_ref[...] = gathered[...]
    all_ref[ring.me] = side.held[...]


def group_sum(value, slices, collective_id):
    dps, rows = value.shape[:2]
    shares = lax.axis_size("chan")
    chips = shares // 2
    dtype = value.dtype
    buffers = []
    for shape in (value.shape, slices.shape):
        kinds = (shape, shape[1:], shape[1:], shape[2:], shape)
        buffers += [pltpu.VMEM(kind, dtype) for kind in kinds]
    gathered = (shares,) + slices.shape
    vmem = pl.BlockSpec(memory_space=pltpu.VMEM)
    return pl.pallas_call(
        functools.partial(sum_kernel, rows, dps, chips),
        out_shape=[
            jax.ShapeDtypeStruct(value.shape, dtype), jax.ShapeDtypeStruct(gathered, dtype)
        ],
        in_specs=[vmem] * 2,
        out_specs=[vmem] * 2,
        scratch_shapes=buffers
        + [pltpu.SemaphoreType.DMA((4, max(rows, dps)))] * 4
        + [pltpu.VMEM(gathered, dtype)]
        + [pltpu.SemaphoreType.DMA((2, chips // 2 + 1))] * 4,
        compiler_params=pltpu.CompilerParams(collective_id=collective_id, has_side_effects=True),
        cost_estimate=pl.CostEstimate(flops=0, bytes_accessed=100_000_000, transcendentals=0),
    )(value, slices)


def ring_kernel(chips, cut, deal, *refs):
    if not deal:
        x_ref, out_ref, held = refs[:3]
        ring = Ring(chips, cut, x_ref, held, *refs[3:])
        greet([*ring.ways, ring.twin])
        ring.start()
        for hop in range(1, ring.hops + 1):
            ring.advance(hop)
        ring.finish()
        out_ref[...] = held[...]
        out_ref[ring.me] = x_ref[...]
        return
    x_ref, y_ref, first_ref, last_ref, dealt_ref, held, dealt = refs[:7]
    deal_send, deal_recv, twin_send, twin_recv = refs[7:11]
    ring = Ring(chips, cut, x_ref, held, *refs[11:])
    greet([ring.twin] + [{"chan": ring.block(step)} for step in range(1, chips)])

    def direct(step):
        return remote(
            y_ref.at[lax.rem(ring.chip + step, chips)],
            dealt.at[ring.me],
            deal_send.at[step],
            deal_recv.at[step],
            {"chan": ring.block(step)},
        )

    def onward(step):
        slot = ring.block(-step)
        source = y_ref.at[ring.chip] if step == 0 else dealt.at[slot]
        return remote(source, dealt.at[slot], twin_send.at[step], twin_recv.at[step], ring.twin)

    ring.start()
    for step in range(1, chips):
        direct(step).start()
    onward(0).start()
    for hop in range(1, ring.hops):
        ring.advance(hop)
    for step in range(1, chips):
        direct(step).wait_recv()
        onward(step).start()
    ring.advance(ring.hops)
    ring.finish()
    for step in range(1, chips):
        direct(step).wait_send()
    for step in range(chips):
        onward(step).wait()
    first_ref[...] = held[:, :deal]
    last_ref[...] = held[:, deal:]
    first_ref[ring.me] = x_ref[:deal]
    last_ref[ring.me] = x_ref[deal:]
    dealt_ref[...] = dealt[...]
    dealt_ref[ring.me] = y_ref[ring.chip]


def ring_gather(value, cut, collective_id, dealt=None, split=0):
    shares = lax.axis_size("chan")
    chips = shares // 2
    held = (shares,) + value.shape
    if dealt is None:
        operands, outs, buffers, sems = [value], [held], [held], []
    else:
        slices = (shares,) + dealt.shape[1:]
        operands, buffers = [value, dealt], [held, slices]
        outs = [(shares, split, held[2]), (shares, held[1] - split, held[2]), slices]
        sems = [pltpu.SemaphoreType.DMA((chips,))] * 4
    vmem = pl.BlockSpec(memory_space=pltpu.VMEM)
    return pl.pallas_call(
        functools.partial(ring_kernel, chips, cut, split),
        out_shape=[jax.ShapeDtypeStruct(shape, value.dtype) for shape in outs],
        in_specs=[vmem] * len(operands),
        out_specs=[vmem] * len(outs),
        scratch_shapes=[pltpu.VMEM(shape, value.dtype) for shape in buffers]
        + sems
        + [pltpu.SemaphoreType.DMA((2, chips // 2 + 1))] * 4,
        compiler_params=pltpu.CompilerParams(collective_id=collective_id, has_side_effects=True),
        cost_estimate=pl.CostEstimate(flops=0, bytes_accessed=80_000_000, transcendentals=0),
    )(*operands)


def exchange(value, axis):
    return lax.all_to_all(value, axis, split_axis=0, concat_axis=0, tiled=True)


def window(source, left, top, cols, rows):
    return source[left : left + cols, top : top + rows]


def on_device(features_in, depth_weights, point_weights, proj_weights, cotangent):
    samples, band_rows, band_cols, channels = features_in.shape
    bands, shares, dps = lax.axis_size("row"), lax.axis_size("chan"), lax.axis_size("dp")
    branches, _, width = point_weights.shape
    weight_scale = 1.0 / math.sqrt(samples * dps * band_rows * bands * band_cols)
    half = band_rows // ROW_CLASSES
    cols = band_cols // COL_CLASSES
    rows = half * bands
    row_step, col_step = BASE_DILATION // ROW_CLASSES, BASE_DILATION // COL_CLASSES

    classes = features_in.reshape(half, ROW_CLASSES, cols, COL_CLASSES, channels)
    classes = classes.transpose(1, 3, 0, 2, 4).reshape(bands, half * cols, channels)
    cells = cotangent.reshape(half, ROW_CLASSES, COL_CLASSES, width).transpose(1, 2, 0, 3)
    cells = cells.reshape(bands, half, width)
    landed = exchange(
        jnp.concatenate([classes, cells[:, :, :channels], cells[:, :, channels:]], axis=1), "row"
    )
    area = half * cols
    grid = landed[:, :area].reshape(rows, cols, channels).transpose(1, 0, 2)
    cot = jnp.concatenate([landed[:, area : area + half], landed[:, area + half :]], axis=2)
    cot = cot.reshape(rows, width)
    full_point = ring_gather(
        point_weights.reshape(branches * channels, width), branches * channels // 2, 2
    )[0].reshape((shares,) + point_weights.shape)

    pads = ((3 * col_step, 3 * col_step), (3 * row_step, 3 * row_step), (0, 0))
    padded = jnp.pad(grid, pads)
    weights = depth_weights.astype(jnp.float32)
    maps = [grid]
    for level in range(1, branches):
        summed = jnp.zeros(grid.shape, jnp.float32)
        for i in range(3):
            for j in range(3):
                tap = window(
                    padded,
                    3 * col_step + (j - 1) * level * col_step,
                    3 * row_step + (i - 1) * level * row_step,
                    cols,
                    rows,
                )
                summed = summed + tap.astype(jnp.float32) * weights[level - 1, i, j]
        maps.append(summed.astype(jnp.bfloat16))
    spread, full_point = lax.optimization_barrier((jnp.stack(maps, axis=1), full_point))
    preact = jnp.einsum(
        "gbnk,gbkf->bnf",
        exchange(spread, "chan"),
        full_point,
        preferred_element_type=jnp.float32,
    )
    logistic = jax.nn.sigmoid(preact)
    activation = (preact * logistic).astype(jnp.bfloat16)
    act_grad = jnp.einsum("ng,bfg->bnf", cot, proj_weights, preferred_element_type=jnp.float32)
    pre_grad = (act_grad * logistic * (1.0 + preact * (1.0 - logistic))).astype(jnp.bfloat16)
    out_cells = jnp.einsum(
        "bnf,bfg->ng", activation, proj_weights, preferred_element_type=jnp.float32
    ).astype(jnp.bfloat16)

    chips = shares // 2
    per = chips // branches
    part, side = width // per, width // 2
    pieces = activation.reshape(branches, rows, per, part).transpose(0, 2, 1, 3)
    sent = jnp.concatenate([pre_grad.reshape(branches * rows, width), cot], axis=0)
    incoming, full_cot, slices = ring_gather(
        sent, sent.shape[0] // 32 * 16, 0, pieces.reshape(chips, rows, part), branches * rows
    )
    incoming = incoming.reshape(shares, branches, rows, width)
    core = lax.rem(lax.axis_index("chan"), 2)
    cot_side = lax.dynamic_slice_in_dim(full_cot, core * side, side, axis=2)
    proj_part = jnp.einsum(
        "xnf,xng->fg", slices, cot_side, preferred_element_type=jnp.float32
    )
    proj_part = jnp.concatenate([proj_part[: part // 2], proj_part[part // 2 :]], axis=1)
    group = bands * dps
    point_sum = jnp.einsum("xbnk,xbnf->bkf", spread, incoming, preferred_element_type=jnp.float32)
    spread_grad = jnp.einsum(
        "xbnf,bkf->bxnk", incoming, point_weights, preferred_element_type=jnp.float32
    ).astype(jnp.bfloat16)
    grad_in = spread_grad[0].astype(jnp.float32)
    depth_sums = []
    for level in range(1, branches):
        branch_grad = spread_grad[level].astype(jnp.float32)
        grad_padded = jnp.pad(spread_grad[level], pads)
        for i in range(3):
            for j in range(3):
                left, top = (j - 1) * level * col_step, (i - 1) * level * row_step
                tap = window(padded, 3 * col_step + left, 3 * row_step + top, cols, rows)
                depth_sums.append(jnp.sum(tap.astype(jnp.float32) * branch_grad, axis=(0, 1)))
                grad_tap = window(
                    grad_padded, 3 * col_step - left, 3 * row_step - top, cols, rows
                )
                grad_in = grad_in + grad_tap.astype(jnp.float32) * weights[level - 1, i, j]
    returned = grad_in.astype(jnp.bfloat16).transpose(1, 0, 2).reshape(bands, area, channels)
    out_cells = out_cells.reshape(bands, half, width)
    leaving = jnp.concatenate(
        [returned, out_cells[:, :, :channels], out_cells[:, :, channels:]], axis=1
    )
    taps = len(depth_sums)
    depth_part = jnp.pad(jnp.stack(depth_sums), ((0, group - taps), (0, width - channels)))
    height = branches * channels // group
    terms = jnp.concatenate(
        [point_sum.reshape(group, height, width), depth_part[:, None]], axis=1
    ).astype(jnp.bfloat16)
    leaving, terms = lax.optimization_barrier((leaving, terms))
    returned = exchange(leaving, "row")
    output = jnp.concatenate(
        [returned[:, area : area + half], returned[:, area + half :]], axis=2
    )
    output = output.reshape(ROW_CLASSES, COL_CLASSES, half, width).transpose(2, 0, 1, 3)
    output = output.reshape(1, band_rows, COL_CLASSES, width)
    grad_input = returned[:, :area].reshape(ROW_CLASSES, COL_CLASSES, half, cols, channels)
    grad_input = grad_input.transpose(2, 0, 3, 1, 4).reshape(features_in.shape)

    summed, grad_proj = group_sum(
        terms.reshape(dps, bands, height + 1, width),
        proj_part.astype(jnp.bfloat16).reshape(dps, bands, -1, width),
        1,
    )
    summed = summed.reshape(group, height + 1, width)
    grad_point = summed[:, :height].reshape(point_weights.shape).astype(jnp.float32) * weight_scale
    grad_depth = summed[:taps, height, :channels].reshape(depth_weights.shape)
    grad_depth = grad_depth.astype(jnp.float32) * weight_scale
    grad_proj = grad_proj.reshape(branches, per, 2, part // 2, 2, side).transpose(0, 1, 4, 3, 2, 5)
    grad_proj = grad_proj.reshape(branches, width, width).astype(jnp.float32) * weight_scale
    return (output, grad_input, grad_depth, grad_point, grad_proj)


def solution(mesh):
    in_specs = (
        P("dp", "row", None, "chan"),
        P(None, None, None, "chan"),
        P(None, "chan", None),
        P(),
        P("dp", "row", "chan", None),
    )
    out_specs = (
        P("dp", "row", "chan", None),
        P("dp", "row", None, "chan"),
        P(None, None, None, "chan"),
        P(None, "chan", None),
        P(),
    )
    return jax.shard_map(
        on_device, mesh=mesh, in_specs=in_specs, out_specs=out_specs, check_vma=False
    )
```

time: 302 us -> 202 us (0.67)
  waiting for transfers between devices: 115 us -> 28.5 us
  Pallas kernels: 68 us -> 113 us
  blocking collectives: 29.9 us -> 0 us
  starting transfers between devices: 38.1 us -> 20.1 us
  between operations: 14 us -> 1.73 us
    all_gather x3 -> x0, waiting for transfers between devices: 70.6 us -> none  [the longest x1 44 us: on_device(): incoming = lax.all_gather(pre_grad, 'chan', axis=0)]
    pallas_call x2 -> x3, Pallas kernels: 68 us -> 113 us  [the longest x2 71.3 us: ring_gather(): pl.pallas_call(functools.partial(ring_kernel, chips, cut, split), out_sha...]
    all_gather x1 -> x0, blocking collectives: 19.7 us -> none  [on_device(): full_cot = lax.all_gather(cot, 'chan', axis=0)]
    all_to_all x5 -> x3, starting transfers between devices: 38 us -> 20.1 us  [exchange(): return lax.all_to_all(value, axis, split_axis=0, concat_axis=0, tiled=True)]
    all_to_all x5 -> x3, waiting for transfers between devices: 43.3 us -> 28.5 us  [exchange(): return lax.all_to_all(value, axis, split_axis=0, concat_axis=0, tiled=True)]
    all_to_all x1 -> x0, blocking collectives: 10.2 us -> none  [exchange(): return lax.all_to_all(value, axis, split_axis=0, concat_axis=0, tiled=True)]
    concatenate x1 -> x8, other arithmetic: 0.95 us -> 4.36 us  [the longest x1 0.79 us: on_device(): jnp.concatenate([point_sum.reshape(group, height, width), depth_part[:, N...]
    mul x2 -> x4, local copies, waits for them, and re-layouts: 1.29 us -> 4.56 us  [the longest x3 3.95 us: on_device(): grad_proj.reshape(branches, width, width).astype(jnp.float32) * weight_scale]
  transfers between devices with their start and end apart: 8 -> 3, of which waited for: 5 -> 1; matrix products, arithmetic and copies ran while one was open for 4% -> 5% of each run, Pallas kernels for 16% -> 40%
where the time goes in v4:
time: 202 us
  Pallas kernels  113 us (56%)
  waiting for transfers between devices  28.5 us (14%)
  starting transfers between devices  20.1 us (10%)
  other arithmetic  17.6 us (9%)
  local copies, waits for them, and re-layouts  12.5 us (6%)
  matrix products  8.06 us (4%)
    pallas_call x2, Pallas kernels, ring_gather(): pl.pallas_call(functools.partial(ring_kernel, chips, cut, split), out_sha...  71.3 us
    pallas_call x1, Pallas kernels, group_sum(): pl.pallas_call(functools.partial(sum_kernel, rows, dps, chips), out_shape...  41.8 us
    all_to_all x3, waiting for transfers between devices, exchange(): return lax.all_to_all(value, axis, split_axis=0, concat_axis=0, tiled=True)  28.5 us
    all_to_all x3, starting transfers between devices, exchange(): return lax.all_to_all(value, axis, split_axis=0, concat_axis=0, tiled=True)  20.1 us
    transpose x1, other arithmetic, on_device(): grad_in.astype(jnp.bfloat16).transpose(1, 0, 2)  6.24 us
  transfers between devices with their start and end apart: 3, of which 1 were waited for; matrix products, arithmetic and copies ran while one was open for 5% of the time, Pallas kernels for 40%

profile of v4, /device:TPU:1, one launch (start us, length us, event | category | flops | bytes accessed | tf_op | source)
XLA Modules:
  0.0 201.6 jit_solution(6377939868760524376)
XLA Ops:
  0.7 0.8 copy.41
  1.5 1.0 copy.40
  2.5 0.8 pad_maximum_fusion.2
  3.3 7.6 %all-to-all-start = ((bf16[8,162,128]{2,1,0:T(8,128)(2,1)}), bf16[8,162,128]{2,1,0:T(8,128)(2,1)S(1)}, u32[]{:S(2)}, u32[]{:S(2)}) async-start(bf16[8,162,128]{2,1,0:T(8,128)(2,1)} %pad_maximum_fusion.2), calls=%async_computation | async-start | bytes 688128 | tf_op jit(solution)/shard_map/all_to_all | solution.py:282
  11.0 39.9 %shard_map.92 = bf16[16,512,256]{2,1,0:T(8,128)(2,1)} custom-call(bf16[512,256]{1,0:T(8,128)(2,1)} %bitcast.309), custom_call_target="tpu_custom_call" | custom-call | bytes 80000000 | tf_op jit(solution)/shard_map/pallas_call | solution.py:268
  53.2 1.1 copy.43
  54.3 4.6 %all-to-all-start.1 = ((bf16[16,4,72,128]{3,2,1,0:T(8,128)(2,1)}), bf16[16,4,72,128]{3,2,1,0:T(8,128)(2,1)S(1)}, u32[]{:S(2)}, u32[]{:S(2)}) async-start(bf16[16,4,72,128]{3,2,1,0:T(8,128)(2,1)} %copy.43), calls=%async_computation.1 | async-start | bytes 2359296 | tf_op jit(solution)/shard_map/all_to_all | solution.py:282
  59.0 0.8 fusion.109
  59.8 0.6 reshape.142
  60.5 0.6 reshape.125
  61.1 28.5 %all-to-all-done.1 = bf16[16,4,72,128]{3,2,1,0:T(8,128)(2,1)S(1)} async-done(((bf16[16,4,72,128]{3,2,1,0:T(8,128)(2,1)}), bf16[16,4,72,128]{3,2,1,0:T(8,128)(2,1)S(1)}, u32[]{:S(2)}, u32[]{:S(2)}) %all-to-all-start.1) | async-done | bytes 1179680 | tf_op jit(solution)/shard_map/all_to_all | solution.py:282
  89.6 3.1 %multiply_convert_fusion = (bf16[4,72,256]{2,1,0:T(8,128)(2,1)S(1)}, f32[4,72,256]{2,1,0:T(8,128)S(1)}) fusion(bf16[16,4,72,128]{3,2,1,0:T(8,128)(2,1)S(1)} %all-to-all-done.1, bf16[16,4,128,256]{3,2,1,0:T(8,128)(2,1)} %bitcast.297), kind=kOutput, calls=%fused_computation.214 | convolution fusion | flops 302358528 | bytes 5816320 | tf_op jit(solution)/shard_map/gbnk,gbkf->bnf/dot_general | solution.py:332
  93.5 0.7 pad_maximum_fusion.4.refs_0_
  94.2 0.7 pad_maximum_fusion.5
  94.9 31.4 %shard_map.93 = (bf16[16,288,256]{2,1,0:T(8,128)(2,1)}, bf16[16,72,256]{2,1,0:T(8,128)(2,1)}, bf16[16,72,128]{2,1,0:T(8,128)(2,1)}) custom-call(bf16[360,256]{1,0:T(8,128)(2,1)} %pad_maximum_fusion.4.refs_0_, bf16[8,72,128]{2,1,0:T(8,128)(2,1)} %bitcast.305), custom_call_target="tpu_custom_call" | custom-call | bytes 80000000 | tf_op jit(solution)/shard_map/pallas_call | solution.py:268
  126.3 2.4 %fusion.10 = bf16[4,128,256]{2,1,0:T(8,128)(2,1)S(1)} fusion(bf16[16,4,72,128]{3,2,0,1:T(8,128)(2,1)S(1)} %pad_maximum_fusion, bf16[16,4,72,256]{3,2,1,0:T(8,128)(2,1)} %bitcast.347), kind=kOutput, calls=%fused_computation.87 | convolution fusion | flops 302120960 | bytes 3801088 | tf_op jit(solution)/shard_map/xbnk,xbnf->bkf/dot_general | solution.py:362
  128.8 0.8 fusion.4
  130.8 0.7 fusion.94
  132.4 1.2 fusion.17
  133.9 6.2 %fusion.103 = bf16[72,16,128]{2,0,1:T(8,128)(2,1)S(1)} fusion(f32[128]{0:T(128)S(1)} %copy-done.19, bf16[16,72,128]{2,1,0:T(8,128)(2,1)S(1)} %get-tuple-element.54, f32[128]{0:T(128)S(1)} %copy-done.21, f32[128]{0:T(128)S(1)} %copy-done.23, f32[128]{0:T(128)S(1)} %copy-done.25, f32[128]{0:T(128)S(1)} %copy-done.27, f32[128]{0:T(128)S(1)} %copy-done.29, ...), kind=kLoop, calls=%fused_computation.219 | loop fusion | flops 12238848 | bytes 1488384 | tf_op jit(solution)/shard_map/transpose | solution.py:380
  140.2 0.8 pad_maximum_fusion.1
  141.0 0.8 pad_maximum_fusion.3
  141.8 7.9 %all-to-all-start.2 = ((bf16[8,162,128]{2,1,0:T(8,128)(2,1)}), bf16[8,162,128]{2,1,0:T(8,128)(2,1)S(1)}, u32[]{:S(2)}, u32[]{:S(2)}) async-start(bf16[8,162,128]{2,1,0:T(8,128)(2,1)} %pad_maximum_fusion.3), calls=%async_computation.2 | async-start | bytes 688128 | tf_op jit(solution)/shard_map/all_to_all | solution.py:282
  149.6 0.6 pad_maximum_fusion.8.y_ref
  150.3 41.8 %shard_map.94 = (bf16[4,8,17,256]{3,2,1,0:T(8,128)(2,1)}, bf16[16,4,8,2,256]{4,3,2,1,0:T(2,128)(2,1)}) custom-call(bf16[4,8,17,256]{3,2,1,0:T(8,128)(2,1)} %bitcast.301, bf16[4,8,2,256]{3,2,1,0:T(2,128)(2,1)} %pad_maximum_fusion.8.y_ref), custom_call_target="tpu_custom_call" | custom-call | bytes 100000000 | tf_op jit(solution)/shard_map/pallas_call | solution.py:186
  192.0 0.9 fusion.106
  193.5 1.6 convert_multiply_fusion.33
  195.2 1.2 mul.709
  196.4 0.9 copy.52
  197.3 1.8 mul.711
  199.2 0.9 convert_multiply_fusion.58
  200.0 0.9 copy.51
  (141 shorter events, 6.1 us)
Async XLA Ops:
  0.6 92.1 %copy-start = (bf16[4,256,256]{2,1,0:T(8,128)(2,1)S(1)}, bf16[4,256,256]{2,1,0:T(8,128)(2,1)}, u32[]{:S(2)}) copy-start(bf16[4,256,256]{2,1,0:T(8,128)(2,1)} %param.8) | copy-start | bytes 1572868
  0.6 10.3 %copy-start.7 = (bf16[3,3,3,128]{3,2,1,0:T(4,128)(2,1)S(1)}, bf16[3,3,3,128]{3,2,1,0:T(4,128)(2,1)}, u32[]{:S(2)}) copy-start(bf16[3,3,3,128]{3,2,1,0:T(4,128)(2,1)} %param.6) | copy-start | bytes 20740
  3.3 47.8 %all-to-all-start = ((bf16[8,162,128]{2,1,0:T(8,128)(2,1)}), bf16[8,162,128]{2,1,0:T(8,128)(2,1)S(1)}, u32[]{:S(2)}, u32[]{:S(2)}) async-start(bf16[8,162,128]{2,1,0:T(8,128)(2,1)} %pad_maximum_fusion.2), calls=%async_computation | async-start | bytes 688128 | tf_op jit(solution)/shard_map/all_to_all | solution.py:282
  54.3 35.3 %all-to-all-start.1 = ((bf16[16,4,72,128]{3,2,1,0:T(8,128)(2,1)}), bf16[16,4,72,128]{3,2,1,0:T(8,128)(2,1)S(1)}, u32[]{:S(2)}, u32[]{:S(2)}) async-start(bf16[16,4,72,128]{3,2,1,0:T(8,128)(2,1)} %copy.43), calls=%async_computation.1 | async-start | bytes 2359296 | tf_op jit(solution)/shard_map/all_to_all | solution.py:282
  61.1 31.8 %copy-start.6 = (bf16[72,256,1]{1,0,2:T(8,128)(2,1)S(1)}, bf16[72,256,1]{1,0,2:T(8,128)(2,1)}, u32[]{:S(2)}) copy-start(bf16[72,256,1]{1,0,2:T(8,128)(2,1)} %reshape.142) | copy-start | bytes 110596
  126.3 2.5 %copy-start.3 = (bf16[4,128,256]{2,1,0:T(8,128)(2,1)S(1)}, bf16[4,128,256]{2,1,0:T(8,128)(2,1)}, u32[]{:S(2)}) copy-start(bf16[4,128,256]{2,1,0:T(8,128)(2,1)} %param.7) | copy-start | bytes 786436
  126.3 2.5 %copy-start.54 = (bf16[16,288,256]{2,1,0:T(8,128)(2,1)S(1)}, bf16[16,288,256]{2,1,0:T(8,128)(2,1)}, u32[]{:S(2)}) copy-start(bf16[16,288,256]{2,1,0:T(8,128)(2,1)} %get-tuple-element.16) | copy-start | bytes 7077892
  131.5 2.2 %copy-start.9 = (f32[128]{0:T(128)S(1)}, f32[128]{0:T(128)}, u32[]{:S(2)}) copy-start(f32[128]{0:T(128)} %copy-done.8) | copy-start | bytes 1540
  131.5 2.2 %copy-start.11 = (f32[128]{0:T(128)S(1)}, f32[128]{0:T(128)}, u32[]{:S(2)}) copy-start(f32[128]{0:T(128)} %copy-done.10) | copy-start | bytes 1540
  131.5 2.2 %copy-start.13 = (f32[128]{0:T(128)S(1)}, f32[128]{0:T(128)}, u32[]{:S(2)}) copy-start(f32[128]{0:T(128)} %copy-done.12) | copy-start | bytes 1540
  131.5 2.2 %copy-start.15 = (f32[128]{0:T(128)S(1)}, f32[128]{0:T(128)}, u32[]{:S(2)}) copy-start(f32[128]{0:T(128)} %copy-done.14) | copy-start | bytes 1540
  131.5 2.2 %copy-start.17 = (f32[128]{0:T(128)S(1)}, f32[128]{0:T(128)}, u32[]{:S(2)}) copy-start(f32[128]{0:T(128)} %copy-done.16) | copy-start | bytes 1540
  131.5 2.2 %copy-start.19 = (f32[128]{0:T(128)S(1)}, f32[128]{0:T(128)}, u32[]{:S(2)}) copy-start(f32[128]{0:T(128)} %copy-done.18) | copy-start | bytes 1540
  131.5 2.2 %copy-start.21 = (f32[128]{0:T(128)S(1)}, f32[128]{0:T(128)}, u32[]{:S(2)}) copy-start(f32[128]{0:T(128)} %copy-done.20) | copy-start | bytes 1540
  131.5 2.2 %copy-start.23 = (f32[128]{0:T(128)S(1)}, f32[128]{0:T(128)}, u32[]{:S(2)}) copy-start(f32[128]{0:T(128)} %copy-done.22) | copy-start | bytes 1540
  131.5 2.2 %copy-start.25 = (f32[128]{0:T(128)S(1)}, f32[128]{0:T(128)}, u32[]{:S(2)}) copy-start(f32[128]{0:T(128)} %copy-done.24) | copy-start | bytes 1540
  131.6 2.2 %copy-start.27 = (f32[128]{0:T(128)S(1)}, f32[128]{0:T(128)}, u32[]{:S(2)}) copy-start(f32[128]{0:T(128)} %copy-done.26) | copy-start | bytes 1540
  131.6 2.2 %copy-start.29 = (f32[128]{0:T(128)S(1)}, f32[128]{0:T(128)}, u32[]{:S(2)}) copy-start(f32[128]{0:T(128)} %copy-done.28) | copy-start | bytes 1540
  131.6 2.2 %copy-start.31 = (f32[128]{0:T(128)S(1)}, f32[128]{0:T(128)}, u32[]{:S(2)}) copy-start(f32[128]{0:T(128)} %copy-done.30) | copy-start | bytes 1540
  131.6 2.2 %copy-start.33 = (f32[128]{0:T(128)S(1)}, f32[128]{0:T(128)}, u32[]{:S(2)}) copy-start(f32[128]{0:T(128)} %copy-done.32) | copy-start | bytes 1540
  131.6 2.2 %copy-start.35 = (f32[128]{0:T(128)S(1)}, f32[128]{0:T(128)}, u32[]{:S(2)}) copy-start(f32[128]{0:T(128)} %copy-done.34) | copy-start | bytes 1540
  131.6 2.2 %copy-start.37 = (f32[128]{0:T(128)S(1)}, f32[128]{0:T(128)}, u32[]{:S(2)}) copy-start(f32[128]{0:T(128)} %copy-done.36) | copy-start | bytes 1540
  131.6 2.2 %copy-start.39 = (f32[128]{0:T(128)S(1)}, f32[128]{0:T(128)}, u32[]{:S(2)}) copy-start(f32[128]{0:T(128)} %copy-done.38) | copy-start | bytes 1540
  131.6 2.2 %copy-start.41 = (f32[128]{0:T(128)S(1)}, f32[128]{0:T(128)}, u32[]{:S(2)}) copy-start(f32[128]{0:T(128)} %copy-done.40) | copy-start | bytes 1540
  131.6 2.2 %copy-start.43 = (f32[128]{0:T(128)S(1)}, f32[128]{0:T(128)}, u32[]{:S(2)}) copy-start(f32[128]{0:T(128)} %copy-done.42) | copy-start | bytes 1540
  131.6 2.2 %copy-start.45 = (f32[128]{0:T(128)S(1)}, f32[128]{0:T(128)}, u32[]{:S(2)}) copy-start(f32[128]{0:T(128)} %copy-done.44) | copy-start | bytes 1540
  131.7 2.2 %copy-start.47 = (f32[128]{0:T(128)S(1)}, f32[128]{0:T(128)}, u32[]{:S(2)}) copy-start(f32[128]{0:T(128)} %copy-done.46) | copy-start | bytes 1540
  131.7 2.2 %copy-start.49 = (f32[128]{0:T(128)S(1)}, f32[128]{0:T(128)}, u32[]{:S(2)}) copy-start(f32[128]{0:T(128)} %copy-done.48) | copy-start | bytes 1540
  131.7 2.2 %copy-start.51 = (f32[128]{0:T(128)S(1)}, f32[128]{0:T(128)}, u32[]{:S(2)}) copy-start(f32[128]{0:T(128)} %copy-done.50) | copy-start | bytes 1540
  131.7 2.2 %copy-start.53 = (f32[128]{0:T(128)S(1)}, f32[128]{0:T(128)}, u32[]{:S(2)}) copy-start(f32[128]{0:T(128)} %copy-done.52) | copy-start | bytes 1540
  141.8 58.3 %all-to-all-start.2 = ((bf16[8,162,128]{2,1,0:T(8,128)(2,1)}), bf16[8,162,128]{2,1,0:T(8,128)(2,1)S(1)}, u32[]{:S(2)}, u32[]{:S(2)}) async-start(bf16[8,162,128]{2,1,0:T(8,128)(2,1)} %pad_maximum_fusion.3), calls=%async_computation.2 | async-start | bytes 688128 | tf_op jit(solution)/shard_map/all_to_all | solution.py:282
  197.3 1.8 copy-start.4
  (26 other events, 35.8 us)

commit v5 on v4

--- a/solution.py
+++ b/solution.py
@@ -11,6 +11,7 @@
 BASE_DILATION = 12
 ROW_CLASSES = 2
 COL_CLASSES = 4
+CHUNKS = 4
 MESH = pl.DeviceIdType.MESH
 
 
@@ -95,12 +96,13 @@
 
 
 class Ring:
-    def __init__(self, chips, cut, x_ref, held, ring_send, ring_recv, pair_send, pair_recv):
+    def __init__(self, chips, chunk, x_ref, held, ring_send, ring_recv, pair_send, pair_recv):
         self.chips, self.hops, self.x_ref, self.held = chips, chips // 2, x_ref, held
         self.sems = ring_send, ring_recv, pair_send, pair_recv
         self.me = lax.axis_index("chan")
         self.chip, self.core = lax.div(self.me, 2), lax.rem(self.me, 2)
-        self.spans = (pl.ds(0, cut), pl.ds(cut, x_ref.shape[0] - cut))
+        size = x_ref.shape[0]
+        self.spans = [pl.ds(at, min(chunk, size - at)) for at in range(0, size, chunk)]
         self.ways = ({"chan": self.block(1)}, {"chan": self.block(-1)})
         self.twin = {"chan": self.chip * 2 + 1 - self.core}
         self.pairs = []
@@ -108,44 +110,50 @@
     def block(self, away):
         return lax.rem(self.chip + away + self.chips, self.chips) * 2 + self.core
 
-    def refs(self, own, away, way, hop):
-        source, landing = (self.x_ref if own else self.held.at[away]), self.held.at[away]
-        if hop == self.hops:
-            source, landing = source.at[self.spans[way]], landing.at[self.spans[way]]
-        return source, landing
-
-    def ring(self, way, hop):
-        away = self.block(1 - hop if way == 0 else hop - 1)
-        source, landing = self.refs(hop == 1, away, way, hop)
+    def brings(self, way, hop, chunk):
+        return hop < self.hops or (chunk < len(self.spans) // 2) == (way == 0)
+
+    def refs(self, own, away, chunk):
+        landing = self.held.at[away].at[self.spans[chunk]]
+        return (self.x_ref.at[self.spans[chunk]] if own else landing), landing
+
+    def ring(self, way, hop, chunk):
+        source, landing = self.refs(hop == 1, self.block(1 - hop if way == 0 else hop - 1), chunk)
+        at = (way, hop, chunk)
         send, recv, _, _ = self.sems
-        return remote(source, landing, send.at[way, hop], recv.at[way, hop], self.ways[way])
-
-    def pair(self, way, hop):
-        away = self.block(-hop if way == 0 else hop)
-        source, landing = self.refs(hop == 0, away, way, hop)
+        return remote(source, landing, send.at[at], recv.at[at], self.ways[way])
+
+    def pair(self, way, hop, chunk):
+        source, landing = self.refs(hop == 0, self.block(-hop if way == 0 else hop), chunk)
+        at = (way, hop, chunk)
         _, _, send, recv = self.sems
-        return remote(source, landing, send.at[way, hop], recv.at[way, hop], self.twin)
+        return remote(source, landing, send.at[at], recv.at[at], self.twin)
+
+    def both(self, way, hop, chunk):
+        self.pair(way, hop, chunk).start()
+        self.pairs.append((way, hop, chunk))
 
     def start(self):
-        for way in range(2):
-            self.ring(way, 1).start()
-        self.pair(0, 0).start()
-        self.pairs.append((0, 0))
+        for chunk in range(len(self.spans)):
+            for way in range(2):
+                self.ring(way, 1, chunk).start()
+        for chunk in range(len(self.spans)):
+            self.both(0, 0, chunk)
 
     def advance(self, hop):
-        for way in range(2):
-            self.ring(way, hop).wait_recv()
-            if hop < self.hops:
-                self.ring(way, hop + 1).start()
-            self.pair(way, hop).start()
-            self.pairs.append((way, hop))
+        for chunk in range(len(self.spans)):
+            for way in range(2):
+                if self.brings(way, hop, chunk):
+                    self.ring(way, hop, chunk).wait_recv()
+                    if hop < self.hops and self.brings(way, hop + 1, chunk):
+                        self.ring(way, hop + 1, chunk).start()
+                    self.both(way, hop, chunk)
 
     def finish(self):
-        for hop in range(1, self.hops + 1):
-            for way in range(2):
-                self.ring(way, hop).wait_send()
-        for way, hop in self.pairs:
-            self.pair(way, hop).wait()
+        for way, hop, chunk in self.pairs:
+            if hop:
+                self.ring(way, hop, chunk).wait_send()
+            self.pair(way, hop, chunk).wait()
 
 
 def sum_kernel(rows, dps, chips, x_ref, y_ref, out_ref, all_ref, *scratch):
@@ -156,13 +164,17 @@
     greet(main.places() + [*ring.ways, ring.twin])
     side.start(0)
     main.start(0)
-    for level in range(3):
-        side.arrive(level)
-        main.arrive(level)
+    side.arrive(0)
+    side.arrive(1)
+    main.arrive(0)
+    side.arrive(2)
     side.arrive(3)
     ring.start()
-    for hop in range(1, ring.hops + 1):
+    main.arrive(1)
+    for hop in range(1, ring.hops):
         ring.advance(hop)
+    main.arrive(2)
+    ring.advance(ring.hops)
     main.arrive(3)
     out_ref[...] = main.held[...]
     main.finish()
@@ -193,16 +205,16 @@
         scratch_shapes=buffers
         + [pltpu.SemaphoreType.DMA((4, max(rows, dps)))] * 4
         + [pltpu.VMEM(gathered, dtype)]
-        + [pltpu.SemaphoreType.DMA((2, chips // 2 + 1))] * 4,
+        + [pltpu.SemaphoreType.DMA((2, chips // 2 + 1, 2))] * 4,
         compiler_params=pltpu.CompilerParams(collective_id=collective_id, has_side_effects=True),
         cost_estimate=pl.CostEstimate(flops=0, bytes_accessed=100_000_000, transcendentals=0),
     )(value, slices)
 
 
-def ring_kernel(chips, cut, deal, *refs):
+def ring_kernel(chips, chunk, deal, *refs):
     if not deal:
         x_ref, out_ref, held = refs[:3]
-        ring = Ring(chips, cut, x_ref, held, *refs[3:])
+        ring = Ring(chips, chunk, x_ref, held, *refs[3:])
         greet([*ring.ways, ring.twin])
         ring.start()
         for hop in range(1, ring.hops + 1):
@@ -213,7 +225,7 @@
         return
     x_ref, y_ref, first_ref, last_ref, dealt_ref, held, dealt = refs[:7]
     deal_send, deal_recv, twin_send, twin_recv = refs[7:11]
-    ring = Ring(chips, cut, x_ref, held, *refs[11:])
+    ring = Ring(chips, chunk, x_ref, held, *refs[11:])
     greet([ring.twin] + [{"chan": ring.block(step)} for step in range(1, chips)])
 
     def direct(step):
@@ -253,7 +265,7 @@
     dealt_ref[ring.me] = y_ref[ring.chip]
 
 
-def ring_gather(value, cut, collective_id, dealt=None, split=0):
+def ring_gather(value, chunk, collective_id, dealt=None, split=0):
     shares = lax.axis_size("chan")
     chips = shares // 2
     held = (shares,) + value.shape
@@ -266,13 +278,13 @@
         sems = [pltpu.SemaphoreType.DMA((chips,))] * 4
     vmem = pl.BlockSpec(memory_space=pltpu.VMEM)
     return pl.pallas_call(
-        functools.partial(ring_kernel, chips, cut, split),
+        functools.partial(ring_kernel, chips, chunk, split),
         out_shape=[jax.ShapeDtypeStruct(shape, value.dtype) for shape in outs],
         in_specs=[vmem] * len(operands),
         out_specs=[vmem] * len(outs),
         scratch_shapes=[pltpu.VMEM(shape, value.dtype) for shape in buffers]
         + sems
-        + [pltpu.SemaphoreType.DMA((2, chips // 2 + 1))] * 4,
+        + [pltpu.SemaphoreType.DMA((2, chips // 2 + 1, -(-value.shape[0] // chunk)))] * 4,
         compiler_params=pltpu.CompilerParams(collective_id=collective_id, has_side_effects=True),
         cost_estimate=pl.CostEstimate(flops=0, bytes_accessed=80_000_000, transcendentals=0),
     )(*operands)
@@ -308,7 +320,7 @@
     cot = jnp.concatenate([landed[:, area : area + half], landed[:, area + half :]], axis=2)
     cot = cot.reshape(rows, width)
     full_point = ring_gather(
-        point_weights.reshape(branches * channels, width), branches * channels // 2, 2
+        point_weights.reshape(branches * channels, width), branches * channels // CHUNKS, 2
     )[0].reshape((shares,) + point_weights.shape)
 
     pads = ((3 * col_step, 3 * col_step), (3 * row_step, 3 * row_step), (0, 0))
@@ -349,7 +361,7 @@
     pieces = activation.reshape(branches, rows, per, part).transpose(0, 2, 1, 3)
     sent = jnp.concatenate([pre_grad.reshape(branches * rows, width), cot], axis=0)
     incoming, full_cot, slices = ring_gather(
-        sent, sent.shape[0] // 32 * 16, 0, pieces.reshape(chips, rows, part), branches * rows
+        sent, -(-sent.shape[0] // CHUNKS // 16) * 16, 0, pieces.reshape(chips, rows, part), branches * rows
     )
     incoming = incoming.reshape(shares, branches, rows, width)
     core = lax.rem(lax.axis_index("chan"), 2)

time: 202 us -> 198 us (0.980)
  Pallas kernels: 113 us -> 109 us
    pallas_call x2, Pallas kernels: 71.3 us -> 68.5 us  [ring_gather(): pl.pallas_call(functools.partial(ring_kernel, chips, chunk, split), out_s...]
    all_to_all x3, starting transfers between devices: 20.1 us -> 18.1 us  [exchange(): return lax.all_to_all(value, axis, split_axis=0, concat_axis=0, tiled=True)]
  transfers between devices with their start and end apart: 3 -> 3, of which waited for: 1 -> 1; matrix products, arithmetic and copies ran while one was open for 5% -> 6% of each run, Pallas kernels for 40% -> 41%
where the time goes in v5:
time: 198 us; the launch traced here: 196 us
  Pallas kernels  109 us (55%)
  waiting for transfers between devices  28.4 us (14%)
  starting transfers between devices  18.1 us (9%)
  other arithmetic  17.6 us (9%)
  local copies, waits for them, and re-layouts  12.6 us (6%)
  matrix products  8.06 us (4%)
    pallas_call x2, Pallas kernels, ring_gather(): pl.pallas_call(functools.partial(ring_kernel, chips, chunk, split), out_s...  68.5 us
    pallas_call x1, Pallas kernels, group_sum(): pl.pallas_call(functools.partial(sum_kernel, rows, dps, chips), out_shape...  40.7 us
    all_to_all x3, waiting for transfers between devices, exchange(): return lax.all_to_all(value, axis, split_axis=0, concat_axis=0, tiled=True)  28.4 us
    all_to_all x3, starting transfers between devices, exchange(): return lax.all_to_all(value, axis, split_axis=0, concat_axis=0, tiled=True)  18.1 us
    transpose x1, other arithmetic, on_device(): grad_in.astype(jnp.bfloat16).transpose(1, 0, 2)  6.24 us
  transfers between devices with their start and end apart: 3, of which 1 were waited for; matrix products, arithmetic and copies ran while one was open for 6% of the time, Pallas kernels for 41%

profile of v5, /device:TPU:1, one launch (start us, length us, event | category | flops | bytes accessed | tf_op | source)
XLA Modules:
  0.0 195.6 jit_solution(16866306124276695976)
XLA Ops:
  0.7 0.8 copy.41
  1.5 1.0 copy.40
  2.5 0.8 pad_maximum_fusion.2
  3.3 7.6 %all-to-all-start = ((bf16[8,162,128]{2,1,0:T(8,128)(2,1)}), bf16[8,162,128]{2,1,0:T(8,128)(2,1)S(1)}, u32[]{:S(2)}, u32[]{:S(2)}) async-start(bf16[8,162,128]{2,1,0:T(8,128)(2,1)} %pad_maximum_fusion.2), calls=%async_computation | async-start | bytes 688128 | tf_op jit(solution)/shard_map/all_to_all | solution.py:294
  11.0 38.7 %shard_map.92 = bf16[16,512,256]{2,1,0:T(8,128)(2,1)} custom-call(bf16[512,256]{1,0:T(8,128)(2,1)} %bitcast.309), custom_call_target="tpu_custom_call" | custom-call | bytes 80000000 | tf_op jit(solution)/shard_map/pallas_call | solution.py:280
  52.1 1.1 copy.43
  53.2 3.8 %all-to-all-start.1 = ((bf16[16,4,72,128]{3,2,1,0:T(8,128)(2,1)}), bf16[16,4,72,128]{3,2,1,0:T(8,128)(2,1)S(1)}, u32[]{:S(2)}, u32[]{:S(2)}) async-start(bf16[16,4,72,128]{3,2,1,0:T(8,128)(2,1)} %copy.43), calls=%async_computation.1 | async-start | bytes 2359296 | tf_op jit(solution)/shard_map/all_to_all | solution.py:294
  56.9 0.9 fusion.109
  57.8 0.6 reshape.142
  58.5 0.6 reshape.125
  59.1 28.4 %all-to-all-done.1 = bf16[16,4,72,128]{3,2,1,0:T(8,128)(2,1)S(1)} async-done(((bf16[16,4,72,128]{3,2,1,0:T(8,128)(2,1)}), bf16[16,4,72,128]{3,2,1,0:T(8,128)(2,1)S(1)}, u32[]{:S(2)}, u32[]{:S(2)}) %all-to-all-start.1) | async-done | bytes 1179680 | tf_op jit(solution)/shard_map/all_to_all | solution.py:294
  87.5 3.1 %multiply_convert_fusion = (bf16[4,72,256]{2,1,0:T(8,128)(2,1)S(1)}, f32[4,72,256]{2,1,0:T(8,128)S(1)}) fusion(bf16[16,4,72,128]{3,2,1,0:T(8,128)(2,1)S(1)} %all-to-all-done.1, bf16[16,4,128,256]{3,2,1,0:T(8,128)(2,1)} %bitcast.297), kind=kOutput, calls=%fused_computation.214 | convolution fusion | flops 302358528 | bytes 5816320 | tf_op jit(solution)/shard_map/gbnk,gbkf->bnf/dot_general | solution.py:344
  91.4 0.7 pad_maximum_fusion.4.refs_0_
  92.1 0.7 pad_maximum_fusion.5
  92.7 29.9 %shard_map.93 = (bf16[16,288,256]{2,1,0:T(8,128)(2,1)}, bf16[16,72,256]{2,1,0:T(8,128)(2,1)}, bf16[16,72,128]{2,1,0:T(8,128)(2,1)}) custom-call(bf16[360,256]{1,0:T(8,128)(2,1)} %pad_maximum_fusion.4.refs_0_, bf16[8,72,128]{2,1,0:T(8,128)(2,1)} %bitcast.305), custom_call_target="tpu_custom_call" | custom-call | bytes 80000000 | tf_op jit(solution)/shard_map/pallas_call | solution.py:280
  122.6 2.4 %fusion.10 = bf16[4,128,256]{2,1,0:T(8,128)(2,1)S(1)} fusion(bf16[16,4,72,128]{3,2,0,1:T(8,128)(2,1)S(1)} %pad_maximum_fusion, bf16[16,4,72,256]{3,2,1,0:T(8,128)(2,1)} %bitcast.347), kind=kOutput, calls=%fused_computation.87 | convolution fusion | flops 302120960 | bytes 3801088 | tf_op jit(solution)/shard_map/xbnk,xbnf->bkf/dot_general | solution.py:374
  125.1 0.8 fusion.4
  127.1 0.7 fusion.94
  128.7 1.2 fusion.17
  130.2 6.2 %fusion.103 = bf16[72,16,128]{2,0,1:T(8,128)(2,1)S(1)} fusion(f32[128]{0:T(128)S(1)} %copy-done.19, bf16[16,72,128]{2,1,0:T(8,128)(2,1)S(1)} %get-tuple-element.54, f32[128]{0:T(128)S(1)} %copy-done.21, f32[128]{0:T(128)S(1)} %copy-done.23, f32[128]{0:T(128)S(1)} %copy-done.25, f32[128]{0:T(128)S(1)} %copy-done.27, f32[128]{0:T(128)S(1)} %copy-done.29, ...), kind=kLoop, calls=%fused_computation.219 | loop fusion | flops 12238848 | bytes 1488384 | tf_op jit(solution)/shard_map/transpose | solution.py:392
  136.5 0.8 pad_maximum_fusion.1
  137.3 0.8 pad_maximum_fusion.3
  138.1 6.6 %all-to-all-start.2 = ((bf16[8,162,128]{2,1,0:T(8,128)(2,1)}), bf16[8,162,128]{2,1,0:T(8,128)(2,1)S(1)}, u32[]{:S(2)}, u32[]{:S(2)}) async-start(bf16[8,162,128]{2,1,0:T(8,128)(2,1)} %pad_maximum_fusion.3), calls=%async_computation.2 | async-start | bytes 688128 | tf_op jit(solution)/shard_map/all_to_all | solution.py:294
  144.7 0.6 pad_maximum_fusion.8.y_ref
  145.4 40.7 %shard_map.94 = (bf16[4,8,17,256]{3,2,1,0:T(8,128)(2,1)}, bf16[16,4,8,2,256]{4,3,2,1,0:T(2,128)(2,1)}) custom-call(bf16[4,8,17,256]{3,2,1,0:T(8,128)(2,1)} %bitcast.301, bf16[4,8,2,256]{3,2,1,0:T(2,128)(2,1)} %pad_maximum_fusion.8.y_ref), custom_call_target="tpu_custom_call" | custom-call | bytes 100000000 | tf_op jit(solution)/shard_map/pallas_call | solution.py:198
  186.1 0.9 fusion.106
  187.5 1.6 convert_multiply_fusion.33
  189.2 1.2 mul.709
  190.4 0.9 copy.52
  191.4 1.8 mul.711
  193.2 0.9 convert_multiply_fusion.58
  194.1 0.9 copy.51
  (141 shorter events, 6.1 us)
Async XLA Ops:
  0.6 90.0 %copy-start = (bf16[4,256,256]{2,1,0:T(8,128)(2,1)S(1)}, bf16[4,256,256]{2,1,0:T(8,128)(2,1)}, u32[]{:S(2)}) copy-start(bf16[4,256,256]{2,1,0:T(8,128)(2,1)} %param.8) | copy-start | bytes 1572868
  0.6 10.3 %copy-start.7 = (bf16[3,3,3,128]{3,2,1,0:T(4,128)(2,1)S(1)}, bf16[3,3,3,128]{3,2,1,0:T(4,128)(2,1)}, u32[]{:S(2)}) copy-start(bf16[3,3,3,128]{3,2,1,0:T(4,128)(2,1)} %param.6) | copy-start | bytes 20740
  3.3 46.6 %all-to-all-start = ((bf16[8,162,128]{2,1,0:T(8,128)(2,1)}), bf16[8,162,128]{2,1,0:T(8,128)(2,1)S(1)}, u32[]{:S(2)}, u32[]{:S(2)}) async-start(bf16[8,162,128]{2,1,0:T(8,128)(2,1)} %pad_maximum_fusion.2), calls=%async_computation | async-start | bytes 688128 | tf_op jit(solution)/shard_map/all_to_all | solution.py:294
  53.2 34.3 %all-to-all-start.1 = ((bf16[16,4,72,128]{3,2,1,0:T(8,128)(2,1)}), bf16[16,4,72,128]{3,2,1,0:T(8,128)(2,1)S(1)}, u32[]{:S(2)}, u32[]{:S(2)}) async-start(bf16[16,4,72,128]{3,2,1,0:T(8,128)(2,1)} %copy.43), calls=%async_computation.1 | async-start | bytes 2359296 | tf_op jit(solution)/shard_map/all_to_all | solution.py:294
  59.1 31.7 %copy-start.6 = (bf16[72,256,1]{1,0,2:T(8,128)(2,1)S(1)}, bf16[72,256,1]{1,0,2:T(8,128)(2,1)}, u32[]{:S(2)}) copy-start(bf16[72,256,1]{1,0,2:T(8,128)(2,1)} %reshape.142) | copy-start | bytes 110596
  122.6 2.5 %copy-start.3 = (bf16[4,128,256]{2,1,0:T(8,128)(2,1)S(1)}, bf16[4,128,256]{2,1,0:T(8,128)(2,1)}, u32[]{:S(2)}) copy-start(bf16[4,128,256]{2,1,0:T(8,128)(2,1)} %param.7) | copy-start | bytes 786436
  122.6 2.5 %copy-start.54 = (bf16[16,288,256]{2,1,0:T(8,128)(2,1)S(1)}, bf16[16,288,256]{2,1,0:T(8,128)(2,1)}, u32[]{:S(2)}) copy-start(bf16[16,288,256]{2,1,0:T(8,128)(2,1)} %get-tuple-element.16) | copy-start | bytes 7077892
  127.8 2.2 %copy-start.9 = (f32[128]{0:T(128)S(1)}, f32[128]{0:T(128)}, u32[]{:S(2)}) copy-start(f32[128]{0:T(128)} %copy-done.8) | copy-start | bytes 1540
  127.8 2.2 %copy-start.11 = (f32[128]{0:T(128)S(1)}, f32[128]{0:T(128)}, u32[]{:S(2)}) copy-start(f32[128]{0:T(128)} %copy-done.10) | copy-start | bytes 1540
  127.8 2.2 %copy-start.13 = (f32[128]{0:T(128)S(1)}, f32[128]{0:T(128)}, u32[]{:S(2)}) copy-start(f32[128]{0:T(128)} %copy-done.12) | copy-start | bytes 1540
  127.8 2.2 %copy-start.15 = (f32[128]{0:T(128)S(1)}, f32[128]{0:T(128)}, u32[]{:S(2)}) copy-start(f32[128]{0:T(128)} %copy-done.14) | copy-start | bytes 1540
  127.8 2.2 %copy-start.17 = (f32[128]{0:T(128)S(1)}, f32[128]{0:T(128)}, u32[]{:S(2)}) copy-start(f32[128]{0:T(128)} %copy-done.16) | copy-start | bytes 1540
  127.8 2.2 %copy-start.19 = (f32[128]{0:T(128)S(1)}, f32[128]{0:T(128)}, u32[]{:S(2)}) copy-start(f32[128]{0:T(128)} %copy-done.18) | copy-start | bytes 1540
  127.8 2.2 %copy-start.21 = (f32[128]{0:T(128)S(1)}, f32[128]{0:T(128)}, u32[]{:S(2)}) copy-start(f32[128]{0:T(128)} %copy-done.20) | copy-start | bytes 1540
  127.8 2.2 %copy-start.23 = (f32[128]{0:T(128)S(1)}, f32[128]{0:T(128)}, u32[]{:S(2)}) copy-start(f32[128]{0:T(128)} %copy-done.22) | copy-start | bytes 1540
  127.8 2.2 %copy-start.25 = (f32[128]{0:T(128)S(1)}, f32[128]{0:T(128)}, u32[]{:S(2)}) copy-start(f32[128]{0:T(128)} %copy-done.24) | copy-start | bytes 1540
  127.9 2.2 %copy-start.27 = (f32[128]{0:T(128)S(1)}, f32[128]{0:T(128)}, u32[]{:S(2)}) copy-start(f32[128]{0:T(128)} %copy-done.26) | copy-start | bytes 1540
  127.9 2.2 %copy-start.29 = (f32[128]{0:T(128)S(1)}, f32[128]{0:T(128)}, u32[]{:S(2)}) copy-start(f32[128]{0:T(128)} %copy-done.28) | copy-start | bytes 1540
  127.9 2.2 %copy-start.31 = (f32[128]{0:T(128)S(1)}, f32[128]{0:T(128)}, u32[]{:S(2)}) copy-start(f32[128]{0:T(128)} %copy-done.30) | copy-start | bytes 1540
  127.9 2.2 %copy-start.33 = (f32[128]{0:T(128)S(1)}, f32[128]{0:T(128)}, u32[]{:S(2)}) copy-start(f32[128]{0:T(128)} %copy-done.32) | copy-start | bytes 1540
  127.9 2.2 %copy-start.35 = (f32[128]{0:T(128)S(1)}, f32[128]{0:T(128)}, u32[]{:S(2)}) copy-start(f32[128]{0:T(128)} %copy-done.34) | copy-start | bytes 1540
  127.9 2.2 %copy-start.37 = (f32[128]{0:T(128)S(1)}, f32[128]{0:T(128)}, u32[]{:S(2)}) copy-start(f32[128]{0:T(128)} %copy-done.36) | copy-start | bytes 1540
  127.9 2.2 %copy-start.39 = (f32[128]{0:T(128)S(1)}, f32[128]{0:T(128)}, u32[]{:S(2)}) copy-start(f32[128]{0:T(128)} %copy-done.38) | copy-start | bytes 1540
  127.9 2.2 %copy-start.41 = (f32[128]{0:T(128)S(1)}, f32[128]{0:T(128)}, u32[]{:S(2)}) copy-start(f32[128]{0:T(128)} %copy-done.40) | copy-start | bytes 1540
  127.9 2.2 %copy-start.43 = (f32[128]{0:T(128)S(1)}, f32[128]{0:T(128)}, u32[]{:S(2)}) copy-start(f32[128]{0:T(128)} %copy-done.42) | copy-start | bytes 1540
  127.9 2.2 %copy-start.45 = (f32[128]{0:T(128)S(1)}, f32[128]{0:T(128)}, u32[]{:S(2)}) copy-start(f32[128]{0:T(128)} %copy-done.44) | copy-start | bytes 1540
  128.0 2.2 %copy-start.47 = (f32[128]{0:T(128)S(1)}, f32[128]{0:T(128)}, u32[]{:S(2)}) copy-start(f32[128]{0:T(128)} %copy-done.46) | copy-start | bytes 1540
  128.0 2.2 %copy-start.49 = (f32[128]{0:T(128)S(1)}, f32[128]{0:T(128)}, u32[]{:S(2)}) copy-start(f32[128]{0:T(128)} %copy-done.48) | copy-start | bytes 1540
  128.0 2.2 %copy-start.51 = (f32[128]{0:T(128)S(1)}, f32[128]{0:T(128)}, u32[]{:S(2)}) copy-start(f32[128]{0:T(128)} %copy-done.50) | copy-start | bytes 1540
  128.0 2.2 %copy-start.53 = (f32[128]{0:T(128)S(1)}, f32[128]{0:T(128)}, u32[]{:S(2)}) copy-start(f32[128]{0:T(128)} %copy-done.52) | copy-start | bytes 1540
  138.1 56.0 %all-to-all-start.2 = ((bf16[8,162,128]{2,1,0:T(8,128)(2,1)}), bf16[8,162,128]{2,1,0:T(8,128)(2,1)S(1)}, u32[]{:S(2)}, u32[]{:S(2)}) async-start(bf16[8,162,128]{2,1,0:T(8,128)(2,1)} %pad_maximum_fusion.3), calls=%async_computation.2 | async-start | bytes 688128 | tf_op jit(solution)/shard_map/all_to_all | solution.py:294
  191.4 1.8 copy-start.4
  (26 other events, 35.8 us)

commit v6 on v5

--- a/solution.py
+++ b/solution.py
@@ -156,11 +156,11 @@
             self.pair(way, hop, chunk).wait()
 
 
-def sum_kernel(rows, dps, chips, x_ref, y_ref, out_ref, all_ref, *scratch):
+def sum_kernel(rows, dps, chips, take, x_ref, y_ref, out_ref, side_ref, all_ref, *scratch):
     main = Levels(rows, dps, x_ref, *scratch[:5], *scratch[10:12])
     side = Levels(rows, dps, y_ref, *scratch[5:10], *scratch[12:14])
-    gathered = scratch[14]
-    ring = Ring(chips, dps // 2, side.held, gathered, *scratch[15:])
+    gathered, packed = scratch[14:16]
+    ring = Ring(chips, packed.shape[0] // 2, packed, gathered, *scratch[16:])
     greet(main.places() + [*ring.ways, ring.twin])
     side.start(0)
     main.start(0)
@@ -169,6 +169,10 @@
     main.arrive(0)
     side.arrive(2)
     side.arrive(3)
+    for dp in range(dps):
+        for row in range(rows):
+            at = (dp * rows + row) * take
+            packed[at : at + take] = side.held[dp, row, :take]
     ring.start()
     main.arrive(1)
     for hop in range(1, ring.hops):
@@ -180,11 +184,12 @@
     main.finish()
     side.finish()
     ring.finish()
+    side_ref[...] = side.held[...]
     all_ref[...] = gathered[...]
-    all_ref[ring.me] = side.held[...]
-
-
-def group_sum(value, slices, collective_id):
+    all_ref[ring.me] = packed[...]
+
+
+def group_sum(value, slices, take, collective_id):
     dps, rows = value.shape[:2]
     shares = lax.axis_size("chan")
     chips = shares // 2
@@ -193,18 +198,19 @@
     for shape in (value.shape, slices.shape):
         kinds = (shape, shape[1:], shape[1:], shape[2:], shape)
         buffers += [pltpu.VMEM(kind, dtype) for kind in kinds]
-    gathered = (shares,) + slices.shape
+    packed = (dps * rows * take, slices.shape[3])
+    gathered = (shares,) + packed
     vmem = pl.BlockSpec(memory_space=pltpu.VMEM)
     return pl.pallas_call(
-        functools.partial(sum_kernel, rows, dps, chips),
+        functools.partial(sum_kernel, rows, dps, chips, take),
         out_shape=[
-            jax.ShapeDtypeStruct(value.shape, dtype), jax.ShapeDtypeStruct(gathered, dtype)
+            jax.ShapeDtypeStruct(shape, dtype) for shape in (value.shape, slices.shape, gathered)
         ],
         in_specs=[vmem] * 2,
-        out_specs=[vmem] * 2,
+        out_specs=[vmem] * 3,
         scratch_shapes=buffers
         + [pltpu.SemaphoreType.DMA((4, max(rows, dps)))] * 4
-        + [pltpu.VMEM(gathered, dtype)]
+        + [pltpu.VMEM(gathered, dtype), pltpu.VMEM(packed, dtype)]
         + [pltpu.SemaphoreType.DMA((2, chips // 2 + 1, 2))] * 4,
         compiler_params=pltpu.CompilerParams(collective_id=collective_id, has_side_effects=True),
         cost_estimate=pl.CostEstimate(flops=0, bytes_accessed=100_000_000, transcendentals=0),
@@ -397,10 +403,13 @@
     taps = len(depth_sums)
     depth_part = jnp.pad(jnp.stack(depth_sums), ((0, group - taps), (0, width - channels)))
     height = branches * channels // group
-    terms = jnp.concatenate(
-        [point_sum.reshape(group, height, width), depth_part[:, None]], axis=1
+    take = part // 2 // group
+    terms = point_sum.astype(jnp.bfloat16).reshape(dps, bands, height, width)
+    extra = jnp.concatenate(
+        [proj_part.reshape(group, take, width), jnp.pad(depth_part[:, None], ((0, 0), (0, 1), (0, 0)))],
+        axis=1,
     ).astype(jnp.bfloat16)
-    leaving, terms = lax.optimization_barrier((leaving, terms))
+    leaving, terms, extra = lax.optimization_barrier((leaving, terms, extra))
     returned = exchange(leaving, "row")
     output = jnp.concatenate(
         [returned[:, area : area + half], returned[:, area + half :]], axis=2
@@ -410,15 +419,12 @@
     grad_input = returned[:, :area].reshape(ROW_CLASSES, COL_CLASSES, half, cols, channels)
     grad_input = grad_input.transpose(2, 0, 3, 1, 4).reshape(features_in.shape)
 
-    summed, grad_proj = group_sum(
-        terms.reshape(dps, bands, height + 1, width),
-        proj_part.astype(jnp.bfloat16).reshape(dps, bands, -1, width),
-        1,
-    )
-    summed = summed.reshape(group, height + 1, width)
-    grad_point = summed[:, :height].reshape(point_weights.shape).astype(jnp.float32) * weight_scale
-    grad_depth = summed[:taps, height, :channels].reshape(depth_weights.shape)
-    grad_depth = grad_depth.astype(jnp.float32) * weight_scale
+    summed, sides, grad_proj = group_sum(
+        terms, extra.reshape(dps, bands, take + 2, width), take, 1
+    )
+    grad_point = summed.reshape(point_weights.shape).astype(jnp.float32) * weight_scale
+    grad_depth = sides.reshape(group, take + 2, width)[:taps, take, :channels]
+    grad_depth = grad_depth.reshape(depth_weights.shape).astype(jnp.float32) * weight_scale
     grad_proj = grad_proj.reshape(branches, per, 2, part // 2, 2, side).transpose(0, 1, 4, 3, 2, 5)
     grad_proj = grad_proj.reshape(branches, width, width).astype(jnp.float32) * weight_scale
     return (output, grad_input, grad_depth, grad_point, grad_proj)

time: 198 us -> 197 us (level)
  other arithmetic: 17.6 us -> 15.6 us
  transfers between devices with their start and end apart: 3 -> 3, of which waited for: 1 -> 1; matrix products, arithmetic and copies ran while one was open for 6% -> 5% of each run, Pallas kernels for 41% -> 41%
where the time goes in v6:
time: 197 us; the launch traced here: 195 us
  Pallas kernels  110 us (56%)
  waiting for transfers between devices  28.4 us (14%)
  starting transfers between devices  18.1 us (9%)
  other arithmetic  15.6 us (8%)
  local copies, waits for them, and re-layouts  12.6 us (6%)
  matrix products  8.77 us (4%)
    pallas_call x2, Pallas kernels, ring_gather(): pl.pallas_call(functools.partial(ring_kernel, chips, chunk, split), out_s...  68.5 us
    pallas_call x1, Pallas kernels, group_sum(): pl.pallas_call(functools.partial(sum_kernel, rows, dps, chips, take), out...  41.3 us
    all_to_all x3, waiting for transfers between devices, exchange(): return lax.all_to_all(value, axis, split_axis=0, concat_axis=0, tiled=True)  28.4 us
    all_to_all x3, starting transfers between devices, exchange(): return lax.all_to_all(value, axis, split_axis=0, concat_axis=0, tiled=True)  18.1 us
    transpose x1, other arithmetic, on_device(): grad_in.astype(jnp.bfloat16).transpose(1, 0, 2)  6.24 us
  transfers between devices with their start and end apart: 3, of which 1 were waited for; matrix products, arithmetic and copies ran while one was open for 5% of the time, Pallas kernels for 41%

profile of v6, /device:TPU:1, one launch (start us, length us, event | category | flops | bytes accessed | tf_op | source)
XLA Modules:
  0.0 195.0 jit_solution(13634890801497786136)
XLA Ops:
  0.7 0.8 copy.44
  1.5 1.0 copy.43
  2.5 0.8 pad_maximum_fusion.1
  3.3 7.6 %all-to-all-start = ((bf16[8,162,128]{2,1,0:T(8,128)(2,1)}), bf16[8,162,128]{2,1,0:T(8,128)(2,1)S(1)}, u32[]{:S(2)}, u32[]{:S(2)}) async-start(bf16[8,162,128]{2,1,0:T(8,128)(2,1)} %pad_maximum_fusion.1), calls=%async_computation | async-start | bytes 688128 | tf_op jit(solution)/shard_map/all_to_all | solution.py:300
  11.0 38.7 %shard_map.92 = bf16[16,512,256]{2,1,0:T(8,128)(2,1)} custom-call(bf16[512,256]{1,0:T(8,128)(2,1)} %bitcast.306), custom_call_target="tpu_custom_call" | custom-call | bytes 80000000 | tf_op jit(solution)/shard_map/pallas_call | solution.py:286
  52.1 1.1 copy.46
  53.2 3.8 %all-to-all-start.1 = ((bf16[16,4,72,128]{3,2,1,0:T(8,128)(2,1)}), bf16[16,4,72,128]{3,2,1,0:T(8,128)(2,1)S(1)}, u32[]{:S(2)}, u32[]{:S(2)}) async-start(bf16[16,4,72,128]{3,2,1,0:T(8,128)(2,1)} %copy.46), calls=%async_computation.1 | async-start | bytes 2359296 | tf_op jit(solution)/shard_map/all_to_all | solution.py:300
  56.9 0.9 fusion.111
  57.8 0.6 reshape.141
  58.5 0.6 reshape.123
  59.1 28.4 %all-to-all-done.1 = bf16[16,4,72,128]{3,2,1,0:T(8,128)(2,1)S(1)} async-done(((bf16[16,4,72,128]{3,2,1,0:T(8,128)(2,1)}), bf16[16,4,72,128]{3,2,1,0:T(8,128)(2,1)S(1)}, u32[]{:S(2)}, u32[]{:S(2)}) %all-to-all-start.1) | async-done | bytes 1179680 | tf_op jit(solution)/shard_map/all_to_all | solution.py:300
  87.5 3.1 %multiply_convert_fusion = (bf16[4,72,256]{2,1,0:T(8,128)(2,1)S(1)}, f32[4,72,256]{2,1,0:T(8,128)S(1)}) fusion(bf16[16,4,72,128]{3,2,1,0:T(8,128)(2,1)S(1)} %all-to-all-done.1, bf16[16,4,128,256]{3,2,1,0:T(8,128)(2,1)} %bitcast.295), kind=kOutput, calls=%fused_computation.213 | convolution fusion | flops 302358528 | bytes 5816320 | tf_op jit(solution)/shard_map/gbnk,gbkf->bnf/dot_general | solution.py:350
  91.4 0.7 pad_maximum_fusion.3.refs_0_
  92.1 0.7 pad_maximum_fusion.4
  92.7 29.9 %shard_map.93 = (bf16[16,288,256]{2,1,0:T(8,128)(2,1)}, bf16[16,72,256]{2,1,0:T(8,128)(2,1)}, bf16[16,72,128]{2,1,0:T(8,128)(2,1)}) custom-call(bf16[360,256]{1,0:T(8,128)(2,1)} %pad_maximum_fusion.3.refs_0_, bf16[8,72,128]{2,1,0:T(8,128)(2,1)} %bitcast.302), custom_call_target="tpu_custom_call" | custom-call | bytes 80000000 | tf_op jit(solution)/shard_map/pallas_call | solution.py:286
  122.6 3.1 %fusion.10 = bf16[4,128,256]{2,1,0:T(8,128)(2,1)} fusion(bf16[16,4,72,128]{3,2,0,1:T(8,128)(2,1)S(1)} %pad_maximum_fusion, bf16[16,4,72,256]{3,2,1,0:T(8,128)(2,1)} %bitcast.342), kind=kOutput, calls=%fused_computation.87 | convolution fusion | flops 302120960 | bytes 3801088 | tf_op jit(solution)/shard_map/xbnk,xbnf->bkf/dot_general | solution.py:380
  125.8 0.8 fusion.4
  127.2 0.6 fusion.93
  127.8 0.7 fusion.94
  129.4 1.2 fusion.17
  131.0 6.2 %fusion.103 = bf16[72,16,128]{2,0,1:T(8,128)(2,1)S(1)} fusion(f32[128]{0:T(128)S(1)} %copy-done.19, bf16[16,72,128]{2,1,0:T(8,128)(2,1)S(1)} %get-tuple-element.58, f32[128]{0:T(128)S(1)} %copy-done.21, f32[128]{0:T(128)S(1)} %copy-done.23, f32[128]{0:T(128)S(1)} %copy-done.25, f32[128]{0:T(128)S(1)} %copy-done.27, f32[128]{0:T(128)S(1)} %copy-done.29, ...), kind=kLoop, calls=%fused_computation.218 | loop fusion | flops 12238848 | bytes 1488384 | tf_op jit(solution)/shard_map/transpose | solution.py:398
  137.3 0.8 pad_maximum_fusion.2
  138.0 6.6 %all-to-all-start.2 = ((bf16[8,162,128]{2,1,0:T(8,128)(2,1)}), bf16[8,162,128]{2,1,0:T(8,128)(2,1)S(1)}, u32[]{:S(2)}, u32[]{:S(2)}) async-start(bf16[8,162,128]{2,1,0:T(8,128)(2,1)} %pad_maximum_fusion.2), calls=%async_computation.2 | async-start | bytes 688128 | tf_op jit(solution)/shard_map/all_to_all | solution.py:300
  144.7 0.7 copy.55
  145.4 41.3 %shard_map.94 = (bf16[4,8,16,256]{3,2,1,0:T(8,128)(2,1)}, bf16[4,8,4,256]{3,2,1,0:T(4,128)(2,1)}, bf16[16,64,256]{2,1,0:T(8,128)(2,1)}) custom-call(bf16[4,8,16,256]{3,2,1,0:T(8,128)(2,1)} %bitcast.307, bf16[4,8,4,256]{3,2,1,0:T(4,128)(2,1)} %bitcast.308), custom_call_target="tpu_custom_call" | custom-call | bytes 100000000 | tf_op jit(solution)/shard_map/pallas_call | solution.py:204
  186.7 0.8 fusion.108
  188.1 1.2 convert_multiply_fusion.33
  189.8 0.9 copy.56
  190.7 1.8 mul.711
  192.6 0.9 convert_multiply_fusion.58
  193.4 0.9 copy.54
  194.3 0.6 copy.53
  (143 shorter events, 5.5 us)
Async XLA Ops:
  0.6 90.0 %copy-start = (bf16[4,256,256]{2,1,0:T(8,128)(2,1)S(1)}, bf16[4,256,256]{2,1,0:T(8,128)(2,1)}, u32[]{:S(2)}) copy-start(bf16[4,256,256]{2,1,0:T(8,128)(2,1)} %param.8) | copy-start | bytes 1572868
  0.6 10.3 %copy-start.7 = (bf16[3,3,3,128]{3,2,1,0:T(4,128)(2,1)S(1)}, bf16[3,3,3,128]{3,2,1,0:T(4,128)(2,1)}, u32[]{:S(2)}) copy-start(bf16[3,3,3,128]{3,2,1,0:T(4,128)(2,1)} %param.6) | copy-start | bytes 20740
  3.3 46.6 %all-to-all-start = ((bf16[8,162,128]{2,1,0:T(8,128)(2,1)}), bf16[8,162,128]{2,1,0:T(8,128)(2,1)S(1)}, u32[]{:S(2)}, u32[]{:S(2)}) async-start(bf16[8,162,128]{2,1,0:T(8,128)(2,1)} %pad_maximum_fusion.1), calls=%async_computation | async-start | bytes 688128 | tf_op jit(solution)/shard_map/all_to_all | solution.py:300
  53.2 34.3 %all-to-all-start.1 = ((bf16[16,4,72,128]{3,2,1,0:T(8,128)(2,1)}), bf16[16,4,72,128]{3,2,1,0:T(8,128)(2,1)S(1)}, u32[]{:S(2)}, u32[]{:S(2)}) async-start(bf16[16,4,72,128]{3,2,1,0:T(8,128)(2,1)} %copy.46), calls=%async_computation.1 | async-start | bytes 2359296 | tf_op jit(solution)/shard_map/all_to_all | solution.py:300
  59.1 31.7 %copy-start.6 = (bf16[72,256,1]{1,0,2:T(8,128)(2,1)S(1)}, bf16[72,256,1]{1,0,2:T(8,128)(2,1)}, u32[]{:S(2)}) copy-start(bf16[72,256,1]{1,0,2:T(8,128)(2,1)} %reshape.141) | copy-start | bytes 110596
  122.6 3.2 %copy-start.3 = (bf16[4,128,256]{2,1,0:T(8,128)(2,1)S(1)}, bf16[4,128,256]{2,1,0:T(8,128)(2,1)}, u32[]{:S(2)}) copy-start(bf16[4,128,256]{2,1,0:T(8,128)(2,1)} %param.7) | copy-start | bytes 786436
  122.6 3.2 %copy-start.54 = (bf16[16,288,256]{2,1,0:T(8,128)(2,1)S(1)}, bf16[16,288,256]{2,1,0:T(8,128)(2,1)}, u32[]{:S(2)}) copy-start(bf16[16,288,256]{2,1,0:T(8,128)(2,1)} %get-tuple-element.18) | copy-start | bytes 7077892
  128.5 2.3 %copy-start.9 = (f32[128]{0:T(128)S(1)}, f32[128]{0:T(128)}, u32[]{:S(2)}) copy-start(f32[128]{0:T(128)} %copy-done.8) | copy-start | bytes 1540
  128.5 2.3 %copy-start.11 = (f32[128]{0:T(128)S(1)}, f32[128]{0:T(128)}, u32[]{:S(2)}) copy-start(f32[128]{0:T(128)} %copy-done.10) | copy-start | bytes 1540
  128.5 2.3 %copy-start.13 = (f32[128]{0:T(128)S(1)}, f32[128]{0:T(128)}, u32[]{:S(2)}) copy-start(f32[128]{0:T(128)} %copy-done.12) | copy-start | bytes 1540
  128.5 2.3 %copy-start.15 = (f32[128]{0:T(128)S(1)}, f32[128]{0:T(128)}, u32[]{:S(2)}) copy-start(f32[128]{0:T(128)} %copy-done.14) | copy-start | bytes 1540
  128.5 2.3 %copy-start.17 = (f32[128]{0:T(128)S(1)}, f32[128]{0:T(128)}, u32[]{:S(2)}) copy-start(f32[128]{0:T(128)} %copy-done.16) | copy-start | bytes 1540
  128.5 2.3 %copy-start.19 = (f32[128]{0:T(128)S(1)}, f32[128]{0:T(128)}, u32[]{:S(2)}) copy-start(f32[128]{0:T(128)} %copy-done.18) | copy-start | bytes 1540
  128.5 2.3 %copy-start.21 = (f32[128]{0:T(128)S(1)}, f32[128]{0:T(128)}, u32[]{:S(2)}) copy-start(f32[128]{0:T(128)} %copy-done.20) | copy-start | bytes 1540
  128.5 2.3 %copy-start.23 = (f32[128]{0:T(128)S(1)}, f32[128]{0:T(128)}, u32[]{:S(2)}) copy-start(f32[128]{0:T(128)} %copy-done.22) | copy-start | bytes 1540
  128.5 2.3 %copy-start.25 = (f32[128]{0:T(128)S(1)}, f32[128]{0:T(128)}, u32[]{:S(2)}) copy-start(f32[128]{0:T(128)} %copy-done.24) | copy-start | bytes 1540
  128.5 2.3 %copy-start.27 = (f32[128]{0:T(128)S(1)}, f32[128]{0:T(128)}, u32[]{:S(2)}) copy-start(f32[128]{0:T(128)} %copy-done.26) | copy-start | bytes 1540
  128.6 2.3 %copy-start.29 = (f32[128]{0:T(128)S(1)}, f32[128]{0:T(128)}, u32[]{:S(2)}) copy-start(f32[128]{0:T(128)} %copy-done.28) | copy-start | bytes 1540
  128.6 2.3 %copy-start.31 = (f32[128]{0:T(128)S(1)}, f32[128]{0:T(128)}, u32[]{:S(2)}) copy-start(f32[128]{0:T(128)} %copy-done.30) | copy-start | bytes 1540
  128.6 2.3 %copy-start.33 = (f32[128]{0:T(128)S(1)}, f32[128]{0:T(128)}, u32[]{:S(2)}) copy-start(f32[128]{0:T(128)} %copy-done.32) | copy-start | bytes 1540
  128.6 2.3 %copy-start.35 = (f32[128]{0:T(128)S(1)}, f32[128]{0:T(128)}, u32[]{:S(2)}) copy-start(f32[128]{0:T(128)} %copy-done.34) | copy-start | bytes 1540
  128.6 2.3 %copy-start.37 = (f32[128]{0:T(128)S(1)}, f32[128]{0:T(128)}, u32[]{:S(2)}) copy-start(f32[128]{0:T(128)} %copy-done.36) | copy-start | bytes 1540
  128.6 2.3 %copy-start.39 = (f32[128]{0:T(128)S(1)}, f32[128]{0:T(128)}, u32[]{:S(2)}) copy-start(f32[128]{0:T(128)} %copy-done.38) | copy-start | bytes 1540
  128.6 2.3 %copy-start.41 = (f32[128]{0:T(128)S(1)}, f32[128]{0:T(128)}, u32[]{:S(2)}) copy-start(f32[128]{0:T(128)} %copy-done.40) | copy-start | bytes 1540
  128.6 2.3 %copy-start.43 = (f32[128]{0:T(128)S(1)}, f32[128]{0:T(128)}, u32[]{:S(2)}) copy-start(f32[128]{0:T(128)} %copy-done.42) | copy-start | bytes 1540
  128.6 2.3 %copy-start.45 = (f32[128]{0:T(128)S(1)}, f32[128]{0:T(128)}, u32[]{:S(2)}) copy-start(f32[128]{0:T(128)} %copy-done.44) | copy-start | bytes 1540
  128.6 2.3 %copy-start.47 = (f32[128]{0:T(128)S(1)}, f32[128]{0:T(128)}, u32[]{:S(2)}) copy-start(f32[128]{0:T(128)} %copy-done.46) | copy-start | bytes 1540
  128.7 2.3 %copy-start.49 = (f32[128]{0:T(128)S(1)}, f32[128]{0:T(128)}, u32[]{:S(2)}) copy-start(f32[128]{0:T(128)} %copy-done.48) | copy-start | bytes 1540
  128.7 2.3 %copy-start.51 = (f32[128]{0:T(128)S(1)}, f32[128]{0:T(128)}, u32[]{:S(2)}) copy-start(f32[128]{0:T(128)} %copy-done.50) | copy-start | bytes 1540
  128.7 2.3 %copy-start.53 = (f32[128]{0:T(128)S(1)}, f32[128]{0:T(128)}, u32[]{:S(2)}) copy-start(f32[128]{0:T(128)} %copy-done.52) | copy-start | bytes 1540
  138.0 55.4 %all-to-all-start.2 = ((bf16[8,162,128]{2,1,0:T(8,128)(2,1)}), bf16[8,162,128]{2,1,0:T(8,128)(2,1)S(1)}, u32[]{:S(2)}, u32[]{:S(2)}) async-start(bf16[8,162,128]{2,1,0:T(8,128)(2,1)} %pad_maximum_fusion.2), calls=%async_computation.2 | async-start | bytes 688128 | tf_op jit(solution)/shard_map/all_to_all | solution.py:300
  190.7 1.8 copy-start.4
  (26 other events, 35.9 us)
